TPU v7x, 512 devices: a whole 4x4x16 slice. The times are simulated.
512 devices in a mesh: dp: 32 (over y, x, core), seq: 16 (over z).
Axes of the slice: x: 4, y: 4, z: 16, core: 2. Of those that a mesh axis runs over, the one named last changes fastest.
Arguments:
- tokens: bfloat16 [64, 4096, 768], P('dp', 'seq'), may hold values from -6 to 6
- norm_gain: float32 [768], replicated, may hold values from 0.1 to 1.9
- dilated_weight: bfloat16 [3, 768, 384], P(None, None, 'seq'), may hold values from -0.125 to 0.125
- output_weight: bfloat16 [384, 768], P(None, 'seq'), may hold values from -0.3125 to 0.3125
- cotangent: bfloat16 [64, 4096, 768], P('dp', 'seq'), may hold values from -6 to 6
Outputs:
- block_output: bfloat16 [64, 4096, 768], P('dp', 'seq')
- token_input_gradient: bfloat16 [64, 4096, 768], P('dp', 'seq')
- dilated_gradient: float32 [3, 768, 384], P(None, None, 'seq')
- output_gradient: float32 [384, 768], P(None, 'seq')
- gain_gradient: float32 [768], P('seq')
All inputs are finite; a program needn't handle non-finite values.
Results may differ from a plain program's by a relative error of at most 0.017.
Values may be sent and summed in bfloat16 or wider, within the bound.
No kernel may reach another device: no remote copies, remote signals or barrier semaphores. Data moves between devices by JAX's collectives and lax.ppermute only.
A program may use at most 64 MiB of HBM per device.

v0:
```python
import jax
import jax.numpy as jnp
from jax import lax
from jax.sharding import PartitionSpec as P

DILATION_STEP = 64


gelu_scale = 0.7978845608
cubic_term = 0.044715
epsilon = 1e-06


def extended(value, sides, width):
    for axis, dim in sides:
        size, length = (lax.axis_size(axis), value.shape[dim])
        up = [(i, (i + 1) % size) for i in range(size - 1)]
        down = [(j, i) for i, j in up]
        last = lax.slice_in_dim(value, length - width, length, axis=dim)
        first = lax.slice_in_dim(value, 0, width, axis=dim)
        before = lax.ppermute(last, axis, up)
        after = lax.ppermute(first, axis, down)
        value = jnp.concatenate([before, value, after], axis=dim)
    return value


def activate(value):
    inner = jnp.tanh(gelu_scale * (value + cubic_term * value * value * value))
    return 0.5 * value * (1.0 + inner)


def derivative(value):
    inner = jnp.tanh(gelu_scale * (value + cubic_term * value * value * value))
    return 0.5 * (1.0 + inner) + 0.5 * value * (1.0 - inner * inner) * gelu_scale * (
        1.0 + 3.0 * cubic_term * value * value
    )


def combine_block_parts(received, sequence_number):
    return jnp.sum(
        received.reshape(sequence_number, received.shape[0] // sequence_number, received.shape[1]),
        axis=0,
    )


def on_device(tokens, norm_gain, dilated_weight, output_weight, cotangent):
    seqs_here, local_bins, channel_count = tokens.shape
    sequence_number = lax.axis_size("seq")
    collected_dilated, collected_output = (
        lax.all_gather(
            dilated_weight.reshape(3 * channel_count, dilated_weight.shape[2]),
            "seq",
            axis=1,
            tiled=True,
        ),
        lax.all_gather(output_weight, "seq", axis=1, tiled=True),
    )
    hidden_width = collected_dilated.shape[1]
    kernel_taps = collected_dilated.reshape(3, channel_count, hidden_width)
    as_float = tokens.astype(jnp.float32)
    inverse_rms = lax.rsqrt(jnp.mean(as_float * as_float, axis=-1, keepdims=True) + epsilon)
    normed = as_float * inverse_rms * norm_gain
    gelu_activated = activate(normed).astype(jnp.bfloat16)
    padded_input = extended(gelu_activated, (("seq", 1),), DILATION_STEP)
    dilated_sum = jnp.zeros((seqs_here * local_bins, hidden_width), jnp.float32)
    for tap_index in range(3):
        dilated_sum = dilated_sum + jnp.dot(
            padded_input[
                :, tap_index * DILATION_STEP : tap_index * DILATION_STEP + local_bins
            ].reshape(-1, channel_count),
            kernel_taps[tap_index],
            preferred_element_type=jnp.float32,
        )
    dilated_sum = dilated_sum.reshape(seqs_here, local_bins, hidden_width)
    hidden = activate(dilated_sum).astype(jnp.bfloat16)
    hidden_rows = hidden.reshape(-1, hidden_width)
    projected = jnp.dot(hidden_rows, collected_output, preferred_element_type=jnp.float32)
    residual_output = (as_float + projected.reshape(seqs_here, local_bins, channel_count)).astype(
        jnp.bfloat16
    )
    cot_rows = cotangent.reshape(-1, channel_count)
    hidden_cot = jnp.einsum(
        "nc,hc->nh", cot_rows, collected_output, preferred_element_type=jnp.float32
    ).astype(jnp.bfloat16)
    output_piece = jnp.einsum(
        "nh,nc->hc", hidden_rows, cot_rows, preferred_element_type=jnp.float32
    )
    cotangent_sum = (
        hidden_cot.reshape(seqs_here, local_bins, hidden_width).astype(jnp.float32)
        * derivative(dilated_sum)
    ).astype(jnp.bfloat16)
    padded_cotangent = extended(cotangent_sum, (("seq", 1),), DILATION_STEP)
    act_cot = jnp.zeros((seqs_here * local_bins, channel_count), jnp.float32)
    dilated_pieces = []
    for tap_index in range(3):
        start_offset = (2 - tap_index) * DILATION_STEP
        piece = padded_cotangent[:, start_offset : start_offset + local_bins].reshape(
            -1, hidden_width
        )
        act_cot = act_cot + jnp.einsum(
            "nh,ch->nc", piece, kernel_taps[tap_index], preferred_element_type=jnp.float32
        )
        dilated_pieces.append(
            jnp.einsum(
                "blc,blh->ch",
                padded_input[:, tap_index * DILATION_STEP : tap_index * DILATION_STEP + local_bins],
                cotangent_sum,
                preferred_element_type=jnp.float32,
            )
        )
    act_cot = act_cot.astype(jnp.bfloat16).reshape(seqs_here, local_bins, channel_count)
    normed_cot = act_cot.astype(jnp.float32) * derivative(normed)
    scaled_cot = norm_gain * normed_cot
    token_cotangent = (
        cotangent.astype(jnp.float32)
        + inverse_rms * scaled_cot
        - as_float * inverse_rms**3 * jnp.mean(scaled_cot * as_float, axis=-1, keepdims=True)
    )
    token_cotangent = token_cotangent.astype(jnp.bfloat16)
    gain_piece = jnp.sum(normed_cot * as_float * inverse_rms, axis=(0, 1))
    dilated_piece = jnp.stack(dilated_pieces).reshape(3 * channel_count, hidden_width)
    incoming_dilated, incoming_output, incoming_gain = (
        lax.all_to_all(dilated_piece, "seq", split_axis=1, concat_axis=0, tiled=True),
        lax.all_to_all(output_piece, "seq", split_axis=1, concat_axis=0, tiled=True),
        lax.all_to_all(
            gain_piece.reshape(1, channel_count), "seq", split_axis=1, concat_axis=0, tiled=True
        ),
    )
    dilated_weight_portion = combine_block_parts(incoming_dilated, sequence_number)
    output_weight_portion = combine_block_parts(incoming_output, sequence_number)
    gain_share = combine_block_parts(incoming_gain, sequence_number)
    dilated_total, output_total, gain_total = lax.psum(
        (dilated_weight_portion, output_weight_portion, gain_share), "dp"
    )
    scale_factor = 1.0 / (seqs_here * lax.axis_size("dp"))
    return (
        residual_output,
        token_cotangent,
        (dilated_total * scale_factor).reshape(3, channel_count, -1),
        output_total * scale_factor,
        (gain_total * scale_factor).reshape(-1),
    )


def solution(mesh):
    in_specs = (
        P("dp", "seq", None),
        P(),
        P(None, None, "seq"),
        P(None, "seq"),
        P("dp", "seq", None),
    )
    out_specs = (
        P("dp", "seq", None),
        P("dp", "seq", None),
        P(None, None, "seq"),
        P(None, "seq"),
        P("seq"),
    )
    return jax.shard_map(
        on_device, mesh=mesh, in_specs=in_specs, out_specs=out_specs, check_vma=False
    )
```

profile of v0, /device:TPU:1, one launch (start us, length us, event | category | flops | bytes accessed | tf_op | source)
XLA Modules:
  0.0 478.6 jit_solution(10501041938618014832)
XLA Ops:
  7.2 1.6 copy.32
  8.9 1.4 fusion.6
  10.3 0.6 multiply_multiply_fusion.3
  10.9 1.4 fusion.11
  12.3 4.4 collective-permute-start
  16.7 1.3 collective-permute-start.1
  18.0 1.2 copy.26
  19.2 35.4 %all_gather.7 = bf16[384,768]{0,1:T(8,128)(2,1)S(1)} all-gather(bf16[384,48]{0,1:T(8,128)(2,1)S(1)} %copy-done.11), channel_id=1, replica_groups=mesh['dp'=32,'seq'=16] {'seq'}, dimensions={1}, use_global_device_ids=true | all-gather | bytes 626688 | tf_op jit(solution)/shard_map/all_gather | solution.py:56
  54.6 1.5 fusion.21
  56.1 1.0 pad_maximum_fusion.2
  57.1 22.8 %all-gather.2.cloned.1.call-done = bf16[2304,384]{0,1:T(8,128)(2,1)} async-done(((bf16[2304,24]{0,1:T(8,128)(2,1)}), bf16[2304,384]{0,1:T(8,128)(2,1)}) %all-gather.2.cloned.1.call-update) | async-done | bytes 1769488 | tf_op jit(solution)/shard_map/all_gather | solution.py:50
  79.9 1.8 fusion.39
  81.7 0.6 fusion.45
  82.3 0.5 copy-done.7
  82.8 1.5 multiply_convert_fusion
  84.3 0.5 fusion.30
  84.9 3.3 collective-permute-start.3
  88.2 1.3 collective-permute-start.2
  89.5 0.9 fusion.43
  90.5 3.1 collective-permute-done.2
  93.6 0.6 fusion.47
  94.2 0.6 add_convert_fusion
  94.9 2.4 fusion.19
  97.3 0.7 all_to_all.31
  98.0 7.4 %all-to-all-start.2 = ((f32[1,16,48]{2,0,1:T(1,128)}), f32[1,16,48]{2,0,1:T(1,128)S(1)}, u32[]{:S(2)}, u32[]{:S(2)}) async-start(f32[1,16,48]{2,0,1:T(1,128)} %all_to_all.31), calls=%async_computation.2 | async-start | bytes 16384 | tf_op jit(solution)/shard_map/all_to_all | solution.py:125
  105.4 2.9 fusion.51
  108.3 8.4 %all-to-all-done.2 = f32[1,16,48]{2,0,1:T(1,128)S(1)} async-done(((f32[1,16,48]{2,0,1:T(1,128)}), f32[1,16,48]{2,0,1:T(1,128)S(1)}, u32[]{:S(2)}, u32[]{:S(2)}) %all-to-all-start.2) | async-done | bytes 3104 | tf_op jit(solution)/shard_map/all_to_all | solution.py:125
  116.6 4.4 all-to-all-start.1
  121.0 1.7 convolution_bitcast_fusion
  122.8 0.6 convolution_bitcast_fusion.1
  123.4 0.5 copy-done.8
  123.9 0.6 convolution_bitcast_fusion.2
  124.5 2.0 pad_maximum_fusion
  126.5 6.4 %copy.25 = f32[3,768,384]{1,0,2:T(4,128)} copy(f32[3,768,384]{2,1,0:T(8,128)} %pad_maximum_fusion) | data formatting | bytes 7077888 | tf_op jit(solution)/shard_map/stack | solution.py:121
  133.0 6.6 %all_to_all.13 = f32[2304,16,24]{0,2,1:T(8,128)} reshape(f32[3,768,384]{1,0,2:T(4,128)} %copy.25) | data formatting | bytes 7077888 | tf_op jit(solution)/shard_map/all_to_all | solution.py:123
  139.6 22.8 %all-to-all-done.1 = f32[384,16,48]{0,2,1:T(8,128)} async-done(((f32[384,16,48]{0,2,1:T(8,128)}), f32[384,16,48]{0,2,1:T(8,128)}, u32[]{:S(2)}, u32[]{:S(2)}) %all-to-all-start.1) | async-done | bytes 1179680 | tf_op jit(solution)/shard_map/all_to_all | solution.py:124
  162.4 17.7 %all-to-all-start = ((f32[2304,16,24]{0,2,1:T(8,128)}), f32[2304,16,24]{0,2,1:T(8,128)}, u32[]{:S(2)}, u32[]{:S(2)}) async-start(f32[2304,16,24]{0,2,1:T(8,128)} %all_to_all.13), calls=%async_computation | async-start | bytes 7077888 | tf_op jit(solution)/shard_map/all_to_all | solution.py:123
  180.2 1.5 fusion.13
  181.6 2.5 fusion.16
  184.2 70.6 %psum.23 = f32[1,48]{1,0:T(1,128)S(1)} all-reduce(f32[1,48]{1,0:T(1,128)S(1)} %bitcast.73), channel_id=1, replica_groups=mesh['dp'=32,'seq'=16] {'dp'}, use_global_device_ids=true, to_apply=%region_8.0 | all-reduce | flops 48 | bytes 384 | tf_op jit(solution)/shard_map/psum | solution.py:132
  254.7 2.0 reduce_sum.59
  256.7 77.1 %all-to-all-done = f32[2304,16,24]{0,2,1:T(8,128)} async-done(((f32[2304,16,24]{0,2,1:T(8,128)}), f32[2304,16,24]{0,2,1:T(8,128)}, u32[]{:S(2)}, u32[]{:S(2)}) %all-to-all-start) | async-done | bytes 3538976 | tf_op jit(solution)/shard_map/all_to_all | solution.py:123
  333.8 2.9 reduce_sum.58
  336.7 0.5 multiply_bitcast_fusion
  337.2 131.4 %all-reduce.3.cloned.1.call-done = (f32[2304,24]{0,1:T(8,128)}, f32[384,48]{0,1:T(8,128)}) async-done(((f32[2304,24]{0,1:T(8,128)}, f32[384,48]{0,1:T(8,128)}), (f32[2304,24]{0,1:T(8,128)}, f32[384,48]{0,1:T(8,128)})) %all-reduce.3.cloned.1.call-update) | async-done | bytes 294928 | tf_op jit(solution)/shard_map/psum | solution.py:132
  468.6 1.0 broadcast_multiply_fusion
  469.5 0.7 copy.34
  470.2 1.5 broadcast_multiply_fusion.1
  (38 shorter events, 0.4 us)
Async XLA Ops:
  7.2 3.7 copy-start
  7.2 72.7 %all-gather.2.cloned.1.call-start = ((), (), s32[]{:S(2)}) async-start(), calls=%async_computation.3 | async-start | bytes 1880064 | tf_op jit(solution)/shard_map/all_gather | solution.py:50
  8.9 9.1 %copy-start.1 = (bf16[2,256,768]{2,1,0:T(8,128)(2,1)S(1)}, bf16[2,256,768]{2,1,0:T(8,128)(2,1)}, u32[]{:S(2)}) copy-start(bf16[2,256,768]{2,1,0:T(8,128)(2,1)} %param.9) | copy-start | bytes 2359300
  12.3 6.9 %copy-start.11 = (bf16[384,48]{0,1:T(8,128)(2,1)S(1)}, bf16[384,48]{0,1:T(8,128)(2,1)}, u32[]{:S(2)}) copy-start(bf16[384,48]{0,1:T(8,128)(2,1)} %param.8) | copy-start | bytes 110596
  12.3 43.8 %collective-permute-start = (bf16[2,64,768]{2,1,0:T(8,128)(2,1)S(1)}, bf16[2,64,768]{2,1,0:T(8,128)(2,1)S(1)}, u32[]{:S(2)}, u32[]{:S(2)}) collective-permute-start(bf16[2,64,768]{2,1,0:T(8,128)(2,1)S(1)} %get-tuple-element.21), channel_id=1, source_target_pairs={{0,1},{1,2},{2,3},{3,4},{4,5},{5,6},{6,7},{7,8},{8,9},{9,10},{10,1... | collective-permute-start | bytes 589832 | tf_op jit(solution)/shard_map/ppermute | solution.py:21
  16.7 39.4 %collective-permute-start.1 = (bf16[2,64,768]{2,1,0:T(8,128)(2,1)S(1)}, bf16[2,64,768]{2,1,0:T(8,128)(2,1)S(1)}, u32[]{:S(2)}, u32[]{:S(2)}) collective-permute-start(bf16[2,64,768]{2,1,0:T(8,128)(2,1)S(1)} %get-tuple-element.22), channel_id=1, source_target_pairs={{1,0},{2,1},{3,2},{4,3},{5,4},{6,5},{7,6},{8,7},{9,8},{10,9},{11,1... | collective-permute-start | bytes 589832 | tf_op jit(solution)/shard_map/ppermute | solution.py:22
  54.6 1.5 copy-start.3
  57.1 25.2 %copy-start.2 = (bf16[2,256,768]{2,1,0:T(8,128)(2,1)}, bf16[2,256,768]{2,1,0:T(8,128)(2,1)S(1)}, u32[]{:S(2)}) copy-start(bf16[2,256,768]{2,1,0:T(8,128)(2,1)S(1)} %get-tuple-element.20) | copy-start | bytes 2359300
  79.9 1.8 copy-start.5
  81.7 1.1 copy-start.7
  82.8 1.5 copy-start.6
  84.9 5.6 %collective-permute-start.3 = (bf16[2,64,384]{2,1,0:T(8,128)(2,1)S(1)}, bf16[2,64,384]{2,1,0:T(8,128)(2,1)S(1)}, u32[]{:S(2)}, u32[]{:S(2)}) collective-permute-start(bf16[2,64,384]{2,1,0:T(8,128)(2,1)S(1)} %get-tuple-element.25), channel_id=1, source_target_pairs={{0,1},{1,2},{2,3},{3,4},{4,5},{5,6},{6,7},{7,8},{8,9},{9,10},{10,1... | collective-permute-start | bytes 294920 | tf_op jit(solution)/shard_map/ppermute | solution.py:21
  88.2 5.4 %collective-permute-start.2 = (bf16[2,64,384]{2,1,0:T(8,128)(2,1)S(1)}, bf16[2,64,384]{2,1,0:T(8,128)(2,1)S(1)}, u32[]{:S(2)}, u32[]{:S(2)}) collective-permute-start(bf16[2,64,384]{2,1,0:T(8,128)(2,1)S(1)} %get-tuple-element.26), channel_id=1, source_target_pairs={{1,0},{2,1},{3,2},{4,3},{5,4},{6,5},{7,6},{8,7},{9,8},{10,9},{11,1... | collective-permute-start | bytes 294920 | tf_op jit(solution)/shard_map/ppermute | solution.py:22
  94.2 0.7 copy-start.10
  98.0 18.7 %all-to-all-start.2 = ((f32[1,16,48]{2,0,1:T(1,128)}), f32[1,16,48]{2,0,1:T(1,128)S(1)}, u32[]{:S(2)}, u32[]{:S(2)}) async-start(f32[1,16,48]{2,0,1:T(1,128)} %all_to_all.31), calls=%async_computation.2 | async-start | bytes 16384 | tf_op jit(solution)/shard_map/all_to_all | solution.py:125
  116.6 45.7 %all-to-all-start.1 = ((f32[384,16,48]{0,2,1:T(8,128)}), f32[384,16,48]{0,2,1:T(8,128)}, u32[]{:S(2)}, u32[]{:S(2)}) async-start(f32[384,16,48]{0,2,1:T(8,128)} %fusion.51), calls=%async_computation.1 | async-start | bytes 2359296 | tf_op jit(solution)/shard_map/all_to_all | solution.py:124
  122.8 1.1 copy-start.8
  139.6 40.5 %copy-start.4 = (bf16[384,768]{0,1:T(8,128)(2,1)S(1)}, bf16[384,768]{0,1:T(8,128)(2,1)}, u32[]{:S(2)}) copy-start(bf16[384,768]{0,1:T(8,128)(2,1)} %copy-done.3) | copy-start | bytes 1769476
  139.6 40.5 %copy-start.9 = (bf16[512,384]{1,0:T(8,128)(2,1)S(1)}, bf16[512,384]{1,0:T(8,128)(2,1)}, u32[]{:S(2)}) copy-start(bf16[512,384]{1,0:T(8,128)(2,1)} %get-tuple-element.29) | copy-start | bytes 1179652
  162.4 171.4 %all-to-all-start = ((f32[2304,16,24]{0,2,1:T(8,128)}), f32[2304,16,24]{0,2,1:T(8,128)}, u32[]{:S(2)}, u32[]{:S(2)}) async-start(f32[2304,16,24]{0,2,1:T(8,128)} %all_to_all.13), calls=%async_computation | async-start | bytes 7077888 | tf_op jit(solution)/shard_map/all_to_all | solution.py:123
  180.1 1.6 copy-start.12
  180.1 1.6 copy-start.13
  180.1 288.5 %all-reduce.3.cloned.1.call-start = ((), (), s32[]{:S(2)}) async-start(), calls=%async_computation.4 | async-start | bytes 589824 | tf_op jit(solution)/shard_map/psum | solution.py:132
Sparse Core Ops, SparseCore 0:
  10.7 69.1 all-gather.1
  336.8 131.7 all-reduce.2
where the time goes:
time: 480 us; the launch traced here: 479 us
  waiting for transfers between devices  266 us (55%)
  blocking collectives  106 us (22%)
  starting transfers between devices  39.9 us (8%)
  other arithmetic  19.7 us (4%)
  local copies, waits for them, and re-layouts  18.5 us (4%)
  matrix products  14.7 us (3%)
  between operations  14.3 us (3%)
    psum x1, waiting for transfers between devices, on_device(): lax.psum((dilated_weight_portion, output_weight_portion, gain_share), 'dp')  131 us
    all_to_all x1, waiting for transfers between devices, on_device(): lax.all_to_all(dilated_piece, 'seq', split_axis=1, concat_axis=0, tiled=T...  77.1 us
    psum x1, blocking collectives, on_device(): lax.psum((dilated_weight_portion, output_weight_portion, gain_share), 'dp')  70.6 us
    all_gather x1, blocking collectives, on_device(): lax.all_gather(output_weight, 'seq', axis=1, tiled=True)  35.4 us
    all_gather x1, waiting for transfers between devices, on_device(): lax.all_gather(dilated_weight.reshape(3 * channel_count, dilated_weight.s...  22.8 us
    all_to_all x1, waiting for transfers between devices, on_device(): lax.all_to_all(output_piece, 'seq', split_axis=1, concat_axis=0, tiled=True)  22.8 us
    all_to_all x1, starting transfers between devices, on_device(): lax.all_to_all(dilated_piece, 'seq', split_axis=1, concat_axis=0, tiled=T...  17.7 us
  transfers between devices with their start and end apart: 9, of which 6 were waited for; matrix products, arithmetic and copies ran while one was open for 6% of the time, Pallas kernels for 0%

commit v1 on v0

v1 whole, which is shorter than its diff:
```python
import jax
import jax.numpy as jnp
import numpy as np
from jax import lax
from jax.sharding import Mesh, PartitionSpec as P

DILATION_STEP = 64
gelu_scale = 0.7978845608
cubic_term = 0.044715
epsilon = 1e-06
bf16 = jnp.bfloat16
f32 = jnp.float32


def activate(value):
    inner = jnp.tanh(gelu_scale * (value + cubic_term * value * value * value))
    return 0.5 * value * (1.0 + inner)


def derivative(value):
    inner = jnp.tanh(gelu_scale * (value + cubic_term * value * value * value))
    return 0.5 * (1.0 + inner) + 0.5 * value * (1.0 - inner * inner) * gelu_scale * (
        1.0 + 3.0 * cubic_term * value * value
    )


def permutation(groups_outer, groups_inner, width):
    size = groups_outer * groups_inner * width
    order = np.arange(size).reshape(groups_inner, groups_outer, width).transpose(1, 0, 2).reshape(-1)
    matrix = np.zeros((size, size), np.float32)
    matrix[order, np.arange(size)] = 1.0
    return matrix


def on_device(tokens, norm_gain, dilated_weight, output_weight, cotangent):
    seqs, bins, channels = tokens.shape
    hidden_width = output_weight.shape[0]
    D = DILATION_STEP
    yx = ("y", "x")
    core = lax.axis_index("c")
    part = core * 16 + lax.axis_index(yx)
    lane_perm = jnp.asarray(permutation(4, 16, 6), bf16)
    row_perm = jnp.asarray(permutation(8, 16, 6), bf16)

    slice_d = (
        dilated_weight.transpose(0, 2, 1)
        .reshape(3, 4, 6, 2, 384)
        .transpose(1, 0, 3, 2, 4)
        .reshape(24, 6, 384)
    )
    slice_o = jnp.dot(output_weight.T, lane_perm, preferred_element_type=f32).astype(bf16)
    pieces = jnp.concatenate([slice_d, slice_o.reshape(8, 6, 384)])
    piece = lax.dynamic_index_in_dim(pieces, part, 0, keepdims=True)
    from_z = lax.all_to_all(jnp.broadcast_to(piece, (16, 6, 384)), "z", 0, 0)
    stacked = from_z.reshape(1, 96, 384)
    half = lax.all_to_all(jnp.broadcast_to(stacked, (16, 96, 384)), yx, 0, 0)
    other = lax.ppermute(half, "c", [(0, 1), (1, 0)])
    lower = jnp.where(core == 0, half, other)
    upper = jnp.where(core == 0, other, half)
    gathered = jnp.concatenate([lower, upper])
    taps = (
        gathered[:24].reshape(4, 3, 2, 96, 384).transpose(1, 0, 3, 2, 4).reshape(3, hidden_width, channels)
    )
    out_t = gathered[24:].reshape(channels, hidden_width)

    as_float = tokens.astype(f32)
    inverse_rms = lax.rsqrt(jnp.mean(as_float * as_float, axis=-1, keepdims=True) + epsilon)
    normed = as_float * inverse_rms * norm_gain
    activated = activate(normed).astype(bf16)
    cot_perm = jnp.einsum("snc,cd->snd", cotangent, row_perm, preferred_element_type=f32).astype(bf16)
    up = [(i, i + 1) for i in range(15)]
    down = [(i + 1, i) for i in range(15)]
    before = lax.ppermute(jnp.concatenate([activated[:, -2 * D :], cot_perm[:, -D:]], 1), "z", up)
    after = lax.ppermute(jnp.concatenate([activated[:, : 2 * D], cot_perm[:, :D]], 1), "z", down)
    act_ext = jnp.concatenate([before[:, : 2 * D], activated, after[:, : 2 * D]], 1)
    cot_ext = jnp.concatenate([before[:, 2 * D :], cot_perm, after[:, 2 * D :]], 1)

    ext = bins + 2 * D
    dilated_sum = sum(
        jnp.einsum("snc,hc->snh", act_ext[:, k * D : k * D + ext], taps[k], preferred_element_type=f32)
        for k in range(3)
    )
    hidden_cot = jnp.einsum("snc,ch->snh", cot_ext, out_t, preferred_element_type=f32).astype(bf16)
    sum_cot = (hidden_cot.astype(f32) * derivative(dilated_sum)).astype(bf16)
    hidden = activate(dilated_sum[:, D : D + bins]).astype(bf16)
    mine = sum_cot[:, D : D + bins]
    grad_d = jnp.stack(
        [
            jnp.einsum(
                "snh,snc->hc", mine, act_ext[:, (k + 1) * D : (k + 1) * D + bins], preferred_element_type=f32
            )
            for k in range(3)
        ]
    ).astype(bf16)
    grad_o = jnp.einsum("snc,snh->ch", cot_perm, hidden, preferred_element_type=f32).astype(bf16)
    grad = jnp.concatenate(
        [
            grad_d.reshape(3, 4, 96, 2, 384).transpose(1, 0, 3, 2, 4).reshape(24, 96, 384),
            grad_o.reshape(8, 96, 384),
        ]
    ).reshape(2, 16, 96, 384)
    keep = lax.dynamic_index_in_dim(grad, core, 0, keepdims=False)
    send = lax.dynamic_index_in_dim(grad, 1 - core, 0, keepdims=False)
    received = lax.ppermute(send, "c", [(0, 1), (1, 0)])
    chip = (keep.astype(f32) + received.astype(f32)).astype(bf16)
    plane = jnp.sum(lax.all_to_all(chip, yx, 0, 0).astype(f32), 0).astype(bf16).reshape(16, 6, 384)

    act_cot = sum(
        jnp.einsum("snh,hc->snc", sum_cot[:, (2 - k) * D : (2 - k) * D + bins], taps[k], preferred_element_type=f32)
        for k in range(3)
    )
    normed_cot = act_cot.astype(bf16).astype(f32) * derivative(normed)
    scaled_cot = norm_gain * normed_cot
    token_cotangent = (
        cotangent.astype(f32)
        + inverse_rms * scaled_cot
        - as_float * inverse_rms**3 * jnp.mean(scaled_cot * as_float, axis=-1, keepdims=True)
    ).astype(bf16)
    gain = jnp.sum(normed_cot * as_float * inverse_rms, axis=(0, 1)).reshape(16, 1, 48)
    out_nat = jnp.dot(row_perm, out_t, preferred_element_type=f32).astype(bf16)
    projected = jnp.einsum("snh,ch->snc", hidden, out_nat, preferred_element_type=f32)
    residual_output = (as_float + projected).astype(bf16)

    def with_gain(block, value):
        high = value.astype(bf16)
        low = (value - high.astype(f32)).astype(bf16)
        extra = jnp.concatenate([high, low], -2)
        extra = jnp.pad(extra, ((0, 0),) * (extra.ndim - 1) + ((0, 384 - 48),))
        return jnp.concatenate([block, extra], -2)

    over_z = lax.all_to_all(with_gain(plane, gain), "z", 0, 0).astype(f32)
    summed = jnp.sum(over_z, 0)
    gain_z = (summed[6:7] + summed[7:8])[:, :48]
    final = with_gain(summed[:6].astype(bf16), gain_z)
    spread = lax.all_to_all(jnp.broadcast_to(final[None], (32, 8, 384)), ("c", "y", "x"), 0, 0)
    scale = 1.0 / 64
    full = spread[:, :6]
    d_t = full[:24].reshape(4, 3, 2, 6, 384).transpose(1, 0, 3, 2, 4).reshape(3, 24, 768)
    o_t = jnp.einsum("ch,gh->cg", full[24:].reshape(48, 384), lane_perm, preferred_element_type=f32)
    gain_total = jnp.sum(spread[:, 6:, :48].astype(f32), axis=(0, 1))
    return (
        residual_output,
        token_cotangent,
        d_t.transpose(0, 2, 1).astype(f32) * scale,
        o_t.T * scale,
        gain_total * scale,
    )


def solution(mesh):
    fine = Mesh(mesh.devices.reshape(4, 4, 2, 16), ("y", "x", "c", "z"))
    dp = ("y", "x", "c")
    in_specs = (
        P(dp, "z", None),
        P(),
        P(None, None, "z"),
        P(None, "z"),
        P(dp, "z", None),
    )
    out_specs = (
        P(dp, "z", None),
        P(dp, "z", None),
        P(None, None, "z"),
        P(None, "z"),
        P("z"),
    )
    return jax.shard_map(on_device, mesh=fine, in_specs=in_specs, out_specs=out_specs, check_vma=False)
```

time: 480 us -> 177 us (0.37)
  waiting for transfers between devices: 266 us -> 53.4 us
  blocking collectives: 106 us -> 27.4 us
  between operations: 14.3 us -> 1.31 us
  matrix products: 14.7 us -> 22.7 us
  other arithmetic: 19.7 us -> 11.9 us
    psum x1 -> x0, waiting for transfers between devices: 131 us -> none  [on_device(): lax.psum((dilated_weight_portion, output_weight_portion, gain_share), 'dp')]
    psum x1 -> x0, blocking collectives: 70.6 us -> none  [on_device(): lax.psum((dilated_weight_portion, output_weight_portion, gain_share), 'dp')]
    all_to_all x3 -> x4, waiting for transfers between devices: 108 us -> 41.7 us  [the longest x1 15.3 us: on_device(): lax.all_to_all(chip, yx, 0, 0).astype(f32)]
    all_gather x1 -> x0, blocking collectives: 35.4 us -> none  [on_device(): lax.all_gather(output_weight, 'seq', axis=1, tiled=True)]
    all_to_all x0 -> x1, blocking collectives: none -> 27.4 us  [on_device(): from_z = lax.all_to_all(jnp.broadcast_to(piece, (16, 6, 384)), 'z', 0, 0)]
    all_gather x1 -> x0, waiting for transfers between devices: 22.8 us -> none  [on_device(): lax.all_gather(dilated_weight.reshape(3 * channel_count, dilated_weight.s...]
    ppermute x4, waiting for transfers between devices: 3.12 us -> 11.7 us  [the longest x1 10.7 us: on_device(): lax.ppermute(jnp.concatenate([activated[:, :2 * D], cot_perm[:, :D]], 1),...]
    dot_general x12 -> x15, matrix products: 14.7 us -> 22.7 us  [the longest x3 6.46 us: on_device(): jnp.einsum('snh,hc->snc', sum_cot[:, (2 - k) * D:(2 - k) * D + bins], tap...]
  transfers between devices with their start and end apart: 9 -> 8, of which waited for: 6 -> 6; matrix products, arithmetic and copies ran while one was open for 6% -> 11% of each run, Pallas kernels for 0% -> 0%
where the time goes in v1:
time: 177 us; the launch traced here: 176 us
  waiting for transfers between devices  53.4 us (30%)
  starting transfers between devices  40.5 us (23%)
  blocking collectives  27.4 us (15%)
  matrix products  22.7 us (13%)
  local copies, waits for them, and re-layouts  18.6 us (11%)
  other arithmetic  11.9 us (7%)
    all_to_all x1, blocking collectives, on_device(): from_z = lax.all_to_all(jnp.broadcast_to(piece, (16, 6, 384)), 'z', 0, 0)  27.4 us
    all_to_all x1, waiting for transfers between devices, on_device(): lax.all_to_all(chip, yx, 0, 0).astype(f32)  15.3 us
    all_to_all x1, waiting for transfers between devices, on_device(): half = lax.all_to_all(jnp.broadcast_to(stacked, (16, 96, 384)), yx, 0, 0)  12.8 us
    ppermute x1, waiting for transfers between devices, on_device(): lax.ppermute(jnp.concatenate([activated[:, :2 * D], cot_perm[:, :D]], 1),...  10.7 us
    all_to_all x1, starting transfers between devices, on_device(): over_z = lax.all_to_all(with_gain(plane, gain), 'z', 0, 0).astype(f32)  8.71 us
    all_to_all x1, waiting for transfers between devices, on_device(): over_z = lax.all_to_all(with_gain(plane, gain), 'z', 0, 0).astype(f32)  8.15 us
    all_to_all x1, starting transfers between devices, on_device(): half = lax.all_to_all(jnp.broadcast_to(stacked, (16, 96, 384)), yx, 0, 0)  6.89 us
    dot_general x3, matrix products, on_device(): jnp.einsum('snh,hc->snc', sum_cot[:, (2 - k) * D:(2 - k) * D + bins], tap...  6.46 us
  transfers between devices with their start and end apart: 8, of which 6 were waited for; matrix products, arithmetic and copies ran while one was open for 11% of the time, Pallas kernels for 0%

profile of v1, /device:TPU:1, one launch (start us, length us, event | category | flops | bytes accessed | tf_op | source)
XLA Modules:
  0.0 175.8 jit_solution(8457120202614248761)
XLA Ops:
  0.7 0.7 copy-done
  1.4 1.1 fusion.51
  2.6 0.9 reshape.127
  3.7 27.4 %all_to_all.25 = bf16[16,6,384]{2,1,0:T(8,128)(2,1)S(1)} all-to-all(bf16[16,6,384]{2,1,0:T(8,128)(2,1)S(1)} %broadcast_in_dim.11), channel_id=1, replica_groups=mesh['y'=4,'x'=4,'c'=2,'z'=16] {'z'}, dimensions={0} | all-to-all | bytes 147456 | tf_op jit(solution)/shard_map/all_to_all | solution.py:54
  31.2 1.1 broadcast_in_dim.13
  32.3 6.9 %all-to-all-start.1 = ((bf16[16,96,384]{2,1,0:T(8,128)(2,1)}), bf16[16,96,384]{2,1,0:T(8,128)(2,1)S(1)}, u32[]{:S(2)}, u32[]{:S(2)}) async-start(bf16[16,96,384]{2,1,0:T(8,128)(2,1)} %broadcast_in_dim.13), calls=%async_computation.1 | async-start | bytes 2359296 | tf_op jit(solution)/shard_map/all_to_all | solution.py:56
  39.5 0.7 fusion.12
  40.7 1.7 fusion.29
  42.4 12.8 %all-to-all-done.1 = bf16[16,96,384]{2,1,0:T(8,128)(2,1)S(1)} async-done(((bf16[16,96,384]{2,1,0:T(8,128)(2,1)}), bf16[16,96,384]{2,1,0:T(8,128)(2,1)S(1)}, u32[]{:S(2)}, u32[]{:S(2)}) %all-to-all-start.1) | async-done | bytes 1179680 | tf_op jit(solution)/shard_map/all_to_all | solution.py:56
  55.2 6.0 %collective-permute-start.1 = (bf16[16,96,384]{2,1,0:T(8,128)(2,1)S(1)}, bf16[16,96,384]{2,1,0:T(8,128)(2,1)}, u32[]{:S(2)}, u32[]{:S(2)}) collective-permute-start(bf16[16,96,384]{2,1,0:T(8,128)(2,1)S(1)} %all-to-all-done.1), channel_id=1, source_target_pairs={{0,16},{16,0},{1,17},{17,1},{2,18},{18,2},{3,19},{19,3},{4,20},{20... | collective-permute-start | bytes 3538952 | tf_op jit(solution)/shard_map/ppermute | solution.py:57
  61.2 1.1 fusion.89
  62.3 0.9 pad_maximum_fusion.8
  63.2 1.3 collective-permute-start.2
  64.5 0.9 pad_maximum_fusion.7
  65.4 4.2 %collective-permute-start = (bf16[2,192,768]{2,1,0:T(8,128)(2,1)}, bf16[2,192,768]{2,1,0:T(8,128)(2,1)S(1)}, u32[]{:S(2)}, u32[]{:S(2)}) collective-permute-start(bf16[2,192,768]{2,1,0:T(8,128)(2,1)} %pad_maximum_fusion.7), channel_id=1, source_target_pairs={{0,1},{1,2},{2,3},{3,4},{4,5},{5,6},{6,7},{7,8},{8,9},{9,10},{10,1... | collective-permute-start | bytes 1769480 | tf_op jit(solution)/shard_map/ppermute | solution.py:73
  69.6 10.7 %collective-permute-done.2 = bf16[2,192,768]{2,1,0:T(8,128)(2,1)S(1)} collective-permute-done((bf16[2,192,768]{2,1,0:T(8,128)(2,1)}, bf16[2,192,768]{2,1,0:T(8,128)(2,1)S(1)}, u32[]{:S(2)}, u32[]{:S(2)}) %collective-permute-start.2) | collective-permute-done | bytes 589856 | tf_op jit(solution)/shard_map/ppermute | solution.py:74
  80.2 0.8 slice.131
  81.1 1.0 collective-permute-done
  82.1 0.8 slice.127
  82.9 1.6 broadcast_select_fusion.1
  84.5 0.9 slice.135
  87.1 1.2 reshape.145
  89.2 2.2 %fusion.41 = f32[2,384,384]{2,1,0:T(8,128)S(1)} fusion(bf16[384,768,1]{1,0,2:T(8,128)(2,1)} %reshape.145, bf16[2,128,768]{2,1,0:T(8,128)(2,1)} %slice.131, bf16[2,256,768]{2,1,0:T(8,128)(2,1)S(1)} %copy-done.3), kind=kOutput, calls=%fused_computation.67 | convolution fusion | flops 455344128 | bytes 2949120 | tf_op jit(solution)/shard_map/snc,hc->snh/dot_general | solution.py:80
  91.5 0.8 fusion.36
  92.3 0.8 fusion.21
  93.4 1.5 fusion.25
  95.3 1.2 fusion.28
  97.6 1.4 fusion.23
  99.1 1.8 %stack.13 = bf16[1,4,96,2,384]{4,3,2,1,0:T(2,128)(2,1)S(1)} reshape(bf16[384,768]{1,0:T(8,128)(2,1)} %fusion.23) | data formatting | bytes 1179648 | tf_op jit(solution)/shard_map/stack | solution.py:87
  101.5 0.8 copy-done.15
  102.6 1.2 dynamic-slice_bitcast_fusion
  103.8 3.0 %collective-permute-start.3 = (bf16[16,96,384]{2,1,0:T(8,128)(2,1)}, bf16[16,96,384]{2,1,0:T(8,128)(2,1)}, u32[]{:S(2)}, u32[]{:S(2)}) collective-permute-start(bf16[16,96,384]{2,1,0:T(8,128)(2,1)} %dynamic-slice_bitcast_fusion), channel_id=1, source_target_pairs={{0,16},{16,0},{1,17},{17,1},{2,18},{18,2},{3,19},{19,3},{4,20},{20... | collective-permute-start | bytes 3538952 | tf_op jit(solution)/shard_map/ppermute | solution.py:104
  106.8 3.0 %fusion.69 = f32[2,256,768]{2,1,0:T(8,128)} fusion(bf16[384,768,1]{1,0,2:T(8,128)(2,1)} %copy-done.6, bf16[2,384,384]{2,1,0:T(8,128)(2,1)} %copy-done.12), kind=kOutput, calls=%fused_computation.102 | convolution fusion | flops 301989888 | bytes 2555904 | tf_op jit(solution)/shard_map/snh,hc->snc/dot_general | solution.py:109
  109.8 2.7 %fusion = bf16[16,96,384]{2,1,0:T(8,128)(2,1)} fusion(bf16[16,96,384]{2,1,0:T(8,128)(2,1)} %collective-permute-done.3, bf16[2,16,96,384]{3,2,1,0:T(8,128)(2,1)S(1)} %bitcast.74, s32[]{:T(128)S(6)} %select_n.27), kind=kLoop, calls=%fused_computation.10 | loop fusion | flops 2359296 | bytes 3538948 | tf_op jit(solution)/shard_map/convert_element_type | solution.py:105
  112.5 4.1 %all-to-all-start.2 = ((bf16[16,96,384]{2,1,0:T(8,128)(2,1)}), bf16[16,96,384]{2,1,0:T(8,128)(2,1)S(1)}, u32[]{:S(2)}, u32[]{:S(2)}) async-start(bf16[16,96,384]{2,1,0:T(8,128)(2,1)} %fusion), calls=%async_computation.2 | async-start | bytes 2359296 | tf_op jit(solution)/shard_map/all_to_all | solution.py:106
  117.1 0.8 copy-done.8
  118.1 2.9 %fusion.20 = (f32[768]{0:T(1024)S(1)}, f32[2,256]{1,0:T(2,128)S(1)}, f32[2,256,768]{2,1,0:T(8,128)}) fusion(bf16[2,256,768]{2,1,0:T(8,128)(2,1)S(1)} %copy-done.1, f32[2,256]{1,0:T(2,128)S(1)} %get-tuple-element.23, f32[768]{0:T(1024)S(1)} %copy-done.23, bf16[384,768,1]{1,0,2:T(8,128)(2,1)S(1)} %copy-done.20, bf16[2,384,384]{2,1,0:T(8,128)(2,1)S(1)} %copy-done.13, ...), kind=kOutput, calls=%fused_computation.34 | convolution fusion | flops 314178304 | bytes 6499328 | tf_op jit(solution)/shard_map/snh,hc->snc/dot_general | solution.py:109
  121.2 15.3 %all-to-all-done.2 = bf16[16,96,384]{2,1,0:T(8,128)(2,1)S(1)} async-done(((bf16[16,96,384]{2,1,0:T(8,128)(2,1)}), bf16[16,96,384]{2,1,0:T(8,128)(2,1)S(1)}, u32[]{:S(2)}, u32[]{:S(2)}) %all-to-all-start.2) | async-done | bytes 1179680 | tf_op jit(solution)/shard_map/all_to_all | solution.py:106
  136.7 0.7 pad_maximum_fusion.9
  137.4 8.7 %all-to-all-start.3 = ((bf16[16,8,384]{2,1,0:T(8,128)(2,1)}), bf16[16,8,384]{2,1,0:T(8,128)(2,1)S(1)}, u32[]{:S(2)}, u32[]{:S(2)}) async-start(bf16[16,8,384]{2,1,0:T(8,128)(2,1)} %pad_maximum_fusion.9), calls=%async_computation.3 | async-start | bytes 196608 | tf_op jit(solution)/shard_map/all_to_all | solution.py:131
  146.1 3.7 %fusion.14 = bf16[2,256,768]{2,1,0:T(8,128)(2,1)} fusion(bf16[2,256,768]{2,1,0:T(8,128)(2,1)S(1)} %copy-done.1, bf16[768,384]{1,0:T(8,128)(2,1)S(1)} %bitcast.80, bf16[768,768]{1,0:T(8,128)(2,1)} %constant.77.clone, f32[2,384,384]{2,1,0:T(8,128)} %copy-done.11), kind=kOutput, calls=%fused_computation.28 | convolution fusion | flops 758218752 | bytes 4128768 | tf_op jit(solution)/shard_map/snh,ch->snc/dot_general | solution.py:121
  149.8 8.1 %all-to-all-done.3 = bf16[16,8,384]{2,1,0:T(8,128)(2,1)S(1)} async-done(((bf16[16,8,384]{2,1,0:T(8,128)(2,1)}), bf16[16,8,384]{2,1,0:T(8,128)(2,1)S(1)}, u32[]{:S(2)}, u32[]{:S(2)}) %all-to-all-start.3) | async-done | bytes 98336 | tf_op jit(solution)/shard_map/all_to_all | solution.py:131
  158.0 0.7 broadcast_in_dim.28
  158.7 6.3 %all-to-all-start.4 = ((bf16[32,8,384]{2,1,0:T(8,128)(2,1)}), bf16[32,8,384]{2,1,0:T(8,128)(2,1)S(1)}, u32[]{:S(2)}, u32[]{:S(2)}) async-start(bf16[32,8,384]{2,1,0:T(8,128)(2,1)} %broadcast_in_dim.28), calls=%async_computation.4 | async-start | bytes 393216 | tf_op jit(solution)/shard_map/all_to_all | solution.py:135
  165.1 2.6 %fusion.17 = bf16[2,256,768]{2,1,0:T(8,128)(2,1)} fusion(bf16[2,256,768]{2,1,0:T(8,128)(2,1)S(1)} %copy-done.1, bf16[2,256,768]{2,1,0:T(8,128)(2,1)} %param.11, f32[2,256,768]{2,1,0:T(8,128)S(1)} %copy-done.7, f32[2,256]{1,0:T(2,128)S(1)} %broadcast_multiply_fusion, f32[2,256]{1,0:T(2,128)S(1)} %get-tuple-element.22, f32[768]{0:T(1024)S(1)} %copy-done.23, ...), kind=kLoop, calls=%fused_computation.31 | loop fusion | flops 3538944 | bytes 3941376 | tf_op jit(solution)/shard_map/convert_element_type | solution.py:118
  167.7 5.5 %all-to-all-done.4 = bf16[32,8,384]{2,1,0:T(8,128)(2,1)S(1)} async-done(((bf16[32,8,384]{2,1,0:T(8,128)(2,1)}), bf16[32,8,384]{2,1,0:T(8,128)(2,1)S(1)}, u32[]{:S(2)}, u32[]{:S(2)}) %all-to-all-start.4) | async-done | bytes 196640 | tf_op jit(solution)/shard_map/all_to_all | solution.py:135
  173.8 0.9 fusion.50
  174.9 0.9 mul.275
  (101 shorter events, 8.2 us)
Async XLA Ops:
  0.6 0.8 copy-start
  31.2 8.0 %copy-start.1 = (bf16[2,256,768]{2,1,0:T(8,128)(2,1)S(1)}, bf16[2,256,768]{2,1,0:T(8,128)(2,1)}, u32[]{:S(2)}) copy-start(bf16[2,256,768]{2,1,0:T(8,128)(2,1)} %param.7) | copy-start | bytes 2359300
  32.3 7.2 %copy-start.23 = (f32[768]{0:T(1024)S(1)}, f32[768]{0:T(1024)}, u32[]{:S(2)}) copy-start(f32[768]{0:T(1024)} %param.8) | copy-start | bytes 9220
  32.3 22.9 %all-to-all-start.1 = ((bf16[16,96,384]{2,1,0:T(8,128)(2,1)}), bf16[16,96,384]{2,1,0:T(8,128)(2,1)S(1)}, u32[]{:S(2)}, u32[]{:S(2)}) async-start(bf16[16,96,384]{2,1,0:T(8,128)(2,1)} %broadcast_in_dim.13), calls=%async_computation.1 | async-start | bytes 2359296 | tf_op jit(solution)/shard_map/all_to_all | solution.py:56
  39.2 1.1 copy-start.14
  39.2 1.5 copy-start.24
  40.7 21.5 %copy-start.2 = (bf16[2,256,768]{2,1,0:T(8,128)(2,1)}, bf16[2,256,768]{2,1,0:T(8,128)(2,1)S(1)}, u32[]{:S(2)}) copy-start(bf16[2,256,768]{2,1,0:T(8,128)(2,1)S(1)} %fusion.12) | copy-start | bytes 2359300
  55.2 27.7 %collective-permute-start.1 = (bf16[16,96,384]{2,1,0:T(8,128)(2,1)S(1)}, bf16[16,96,384]{2,1,0:T(8,128)(2,1)}, u32[]{:S(2)}, u32[]{:S(2)}) collective-permute-start(bf16[16,96,384]{2,1,0:T(8,128)(2,1)S(1)} %all-to-all-done.1), channel_id=1, source_target_pairs={{0,16},{16,0},{1,17},{17,1},{2,18},{18,2},{3,19},{19,3},{4,20},{20... | collective-permute-start | bytes 3538952 | tf_op jit(solution)/shard_map/ppermute | solution.py:57
  63.2 17.0 %collective-permute-start.2 = (bf16[2,192,768]{2,1,0:T(8,128)(2,1)}, bf16[2,192,768]{2,1,0:T(8,128)(2,1)S(1)}, u32[]{:S(2)}, u32[]{:S(2)}) collective-permute-start(bf16[2,192,768]{2,1,0:T(8,128)(2,1)} %pad_maximum_fusion.8), channel_id=1, source_target_pairs={{1,0},{2,1},{3,2},{4,3},{5,4},{6,5},{7,6},{8,7},{9,8},{10,9},{11,1... | collective-permute-start | bytes 1769480 | tf_op jit(solution)/shard_map/ppermute | solution.py:74
  65.4 16.7 %collective-permute-start = (bf16[2,192,768]{2,1,0:T(8,128)(2,1)}, bf16[2,192,768]{2,1,0:T(8,128)(2,1)S(1)}, u32[]{:S(2)}, u32[]{:S(2)}) collective-permute-start(bf16[2,192,768]{2,1,0:T(8,128)(2,1)} %pad_maximum_fusion.7), channel_id=1, source_target_pairs={{0,1},{1,2},{2,3},{3,4},{4,5},{5,6},{6,7},{7,8},{8,9},{9,10},{10,1... | collective-permute-start | bytes 1769480 | tf_op jit(solution)/shard_map/ppermute | solution.py:73
  80.2 4.2 %copy-start.16 = (bf16[2,192,768]{2,1,0:T(8,128)(2,1)}, bf16[2,192,768]{2,1,0:T(8,128)(2,1)S(1)}, u32[]{:S(2)}) copy-start(bf16[2,192,768]{2,1,0:T(8,128)(2,1)S(1)} %collective-permute-done.2) | copy-start | bytes 1769476
  82.1 2.4 %copy-start.17 = (bf16[2,192,768]{2,1,0:T(8,128)(2,1)}, bf16[2,192,768]{2,1,0:T(8,128)(2,1)S(1)}, u32[]{:S(2)}) copy-start(bf16[2,192,768]{2,1,0:T(8,128)(2,1)S(1)} %collective-permute-done) | copy-start | bytes 1769476
  86.6 5.6 %copy-start.4 = (bf16[384,768,1]{1,0,2:T(8,128)(2,1)}, bf16[384,768,1]{1,0,2:T(8,128)(2,1)S(1)}, u32[]{:S(2)}) copy-start(bf16[384,768,1]{1,0,2:T(8,128)(2,1)S(1)} %reshape.143) | copy-start | bytes 1769476
  87.1 2.1 %copy-start.3 = (bf16[2,256,768]{2,1,0:T(8,128)(2,1)S(1)}, bf16[2,256,768]{2,1,0:T(8,128)(2,1)}, u32[]{:S(2)}) copy-start(bf16[2,256,768]{2,1,0:T(8,128)(2,1)} %copy-done.2) | copy-start | bytes 2359300
  89.2 2.2 %copy-start.6 = (bf16[384,768,1]{1,0,2:T(8,128)(2,1)}, bf16[384,768,1]{1,0,2:T(8,128)(2,1)S(1)}, u32[]{:S(2)}) copy-start(bf16[384,768,1]{1,0,2:T(8,128)(2,1)S(1)} %reshape.144) | copy-start | bytes 1769476
  89.2 2.2 %copy-start.9 = (bf16[2,128,768]{2,1,0:T(8,128)(2,1)S(1)}, bf16[2,128,768]{2,1,0:T(8,128)(2,1)}, u32[]{:S(2)}) copy-start(bf16[2,128,768]{2,1,0:T(8,128)(2,1)} %slice.127) | copy-start | bytes 1179652
  89.2 2.2 %copy-start.21 = (bf16[2,128,768]{2,1,0:T(8,128)(2,1)S(1)}, bf16[2,128,768]{2,1,0:T(8,128)(2,1)}, u32[]{:S(2)}) copy-start(bf16[2,128,768]{2,1,0:T(8,128)(2,1)} %slice.131) | copy-start | bytes 1179652
  92.3 1.1 copy-start.22
  93.4 1.5 copy-start.11
  93.4 1.5 slice-start
  93.4 1.5 slice-start.1
  93.4 1.9 %copy-start.18 = (bf16[8,96,384]{2,1,0:T(8,128)(2,1)S(1)}, bf16[8,96,384]{2,1,0:T(8,128)(2,1)}, u32[]{:S(2)}) copy-start(bf16[8,96,384]{2,1,0:T(8,128)(2,1)} %slice.135) | copy-start | bytes 1769476
  96.5 1.0 copy-start.12
  101.3 1.1 copy-start.15
  103.8 6.0 %collective-permute-start.3 = (bf16[16,96,384]{2,1,0:T(8,128)(2,1)}, bf16[16,96,384]{2,1,0:T(8,128)(2,1)}, u32[]{:S(2)}, u32[]{:S(2)}) collective-permute-start(bf16[16,96,384]{2,1,0:T(8,128)(2,1)} %dynamic-slice_bitcast_fusion), channel_id=1, source_target_pairs={{0,16},{16,0},{1,17},{17,1},{2,18},{18,2},{3,19},{19,3},{4,20},{20... | collective-permute-start | bytes 3538952 | tf_op jit(solution)/shard_map/ppermute | solution.py:104
  112.5 4.1 %copy-start.5 = (bf16[384,768,1]{1,0,2:T(8,128)(2,1)S(1)}, bf16[384,768,1]{1,0,2:T(8,128)(2,1)}, u32[]{:S(2)}) copy-start(bf16[384,768,1]{1,0,2:T(8,128)(2,1)} %copy-done.4) | copy-start | bytes 1769476
  112.5 4.1 %copy-start.13 = (bf16[2,384,384]{2,1,0:T(8,128)(2,1)S(1)}, bf16[2,384,384]{2,1,0:T(8,128)(2,1)}, u32[]{:S(2)}) copy-start(bf16[2,384,384]{2,1,0:T(8,128)(2,1)} %copy-done.12) | copy-start | bytes 1769476
  112.5 24.0 %all-to-all-start.2 = ((bf16[16,96,384]{2,1,0:T(8,128)(2,1)}), bf16[16,96,384]{2,1,0:T(8,128)(2,1)S(1)}, u32[]{:S(2)}, u32[]{:S(2)}) async-start(bf16[16,96,384]{2,1,0:T(8,128)(2,1)} %fusion), calls=%async_computation.2 | async-start | bytes 2359296 | tf_op jit(solution)/shard_map/all_to_all | solution.py:106
  116.6 1.4 copy-start.8
  116.6 1.5 copy-start.20
  121.0 25.1 %copy-start.19 = (bf16[8,96,384]{2,1,0:T(8,128)(2,1)S(1)}, bf16[8,96,384]{2,1,0:T(8,128)(2,1)}, u32[]{:S(2)}) copy-start(bf16[8,96,384]{2,1,0:T(8,128)(2,1)} %slice.135) | copy-start | bytes 1769476
  137.4 20.6 %all-to-all-start.3 = ((bf16[16,8,384]{2,1,0:T(8,128)(2,1)}), bf16[16,8,384]{2,1,0:T(8,128)(2,1)S(1)}, u32[]{:S(2)}, u32[]{:S(2)}) async-start(bf16[16,8,384]{2,1,0:T(8,128)(2,1)} %pad_maximum_fusion.9), calls=%async_computation.3 | async-start | bytes 196608 | tf_op jit(solution)/shard_map/all_to_all | solution.py:131
  146.1 19.0 %copy-start.7 = (f32[2,256,768]{2,1,0:T(8,128)S(1)}, f32[2,256,768]{2,1,0:T(8,128)}, u32[]{:S(2)}) copy-start(f32[2,256,768]{2,1,0:T(8,128)} %get-tuple-element.24) | copy-start | bytes 4718596
  158.7 14.4 %all-to-all-start.4 = ((bf16[32,8,384]{2,1,0:T(8,128)(2,1)}), bf16[32,8,384]{2,1,0:T(8,128)(2,1)S(1)}, u32[]{:S(2)}, u32[]{:S(2)}) async-start(bf16[32,8,384]{2,1,0:T(8,128)(2,1)} %broadcast_in_dim.28), calls=%async_computation.4 | async-start | bytes 393216 | tf_op jit(solution)/shard_map/all_to_all | solution.py:135
  165.1 8.7 %copy-start.10 = (bf16[384,384]{1,0:T(8,128)(2,1)S(1)}, bf16[384,384]{1,0:T(8,128)(2,1)}, u32[]{:S(2)}) copy-start(bf16[384,384]{1,0:T(8,128)(2,1)} %constant.76.clone) | copy-start | bytes 884740

commit v2 on v1

--- a/solution.py
+++ b/solution.py
@@ -42,6 +42,16 @@
     lane_perm = jnp.asarray(permutation(4, 16, 6), bf16)
     row_perm = jnp.asarray(permutation(8, 16, 6), bf16)
 
+    as_float = tokens.astype(f32)
+    inverse_rms = lax.rsqrt(jnp.mean(as_float * as_float, axis=-1, keepdims=True) + epsilon)
+    normed = as_float * inverse_rms * norm_gain
+    activated = activate(normed).astype(bf16)
+    cot_perm = jnp.einsum("snc,cd->snd", cotangent, row_perm, preferred_element_type=f32).astype(bf16)
+    up = [(i, i + 1) for i in range(15)]
+    down = [(i + 1, i) for i in range(15)]
+    before = lax.ppermute(jnp.concatenate([activated[:, -2 * D :], cot_perm[:, -D:]], 1), "z", up)
+    after = lax.ppermute(jnp.concatenate([activated[:, : 2 * D], cot_perm[:, :D]], 1), "z", down)
+
     slice_d = (
         dilated_weight.transpose(0, 2, 1)
         .reshape(3, 4, 6, 2, 384)
@@ -52,6 +62,7 @@
     pieces = jnp.concatenate([slice_d, slice_o.reshape(8, 6, 384)])
     piece = lax.dynamic_index_in_dim(pieces, part, 0, keepdims=True)
     from_z = lax.all_to_all(jnp.broadcast_to(piece, (16, 6, 384)), "z", 0, 0)
+    from_z, before, after = lax.optimization_barrier((from_z, before, after))
     stacked = from_z.reshape(1, 96, 384)
     half = lax.all_to_all(jnp.broadcast_to(stacked, (16, 96, 384)), yx, 0, 0)
     other = lax.ppermute(half, "c", [(0, 1), (1, 0)])
@@ -63,15 +74,6 @@
     )
     out_t = gathered[24:].reshape(channels, hidden_width)
 
-    as_float = tokens.astype(f32)
-    inverse_rms = lax.rsqrt(jnp.mean(as_float * as_float, axis=-1, keepdims=True) + epsilon)
-    normed = as_float * inverse_rms * norm_gain
-    activated = activate(normed).astype(bf16)
-    cot_perm = jnp.einsum("snc,cd->snd", cotangent, row_perm, preferred_element_type=f32).astype(bf16)
-    up = [(i, i + 1) for i in range(15)]
-    down = [(i + 1, i) for i in range(15)]
-    before = lax.ppermute(jnp.concatenate([activated[:, -2 * D :], cot_perm[:, -D:]], 1), "z", up)
-    after = lax.ppermute(jnp.concatenate([activated[:, : 2 * D], cot_perm[:, :D]], 1), "z", down)
     act_ext = jnp.concatenate([before[:, : 2 * D], activated, after[:, : 2 * D]], 1)
     cot_ext = jnp.concatenate([before[:, 2 * D :], cot_perm, after[:, 2 * D :]], 1)
 
@@ -121,6 +123,10 @@
     projected = jnp.einsum("snh,ch->snc", hidden, out_nat, preferred_element_type=f32)
     residual_output = (as_float + projected).astype(bf16)
 
+    plane, gain, residual_output, token_cotangent = lax.optimization_barrier(
+        (plane, gain, residual_output, token_cotangent)
+    )
+
     def with_gain(block, value):
         high = value.astype(bf16)
         low = (value - high.astype(f32)).astype(bf16)

time: 177 us -> 161 us (0.910)
  blocking collectives: 27.4 us -> 81.2 us
  waiting for transfers between devices: 53.4 us -> 7.08 us
  starting transfers between devices: 40.5 us -> 17.8 us
  matrix products: 22.7 us -> 25.1 us
  other arithmetic: 11.9 us -> 9.85 us
    all_to_all x0 -> x3, blocking collectives: none -> 53 us  [the longest x1 22.2 us: on_device(): half = lax.all_to_all(jnp.broadcast_to(stacked, (16, 96, 384)), yx, 0, 0)]
    all_to_all x3 -> x0, waiting for transfers between devices: 26.4 us -> none  [the longest x1 12.8 us: on_device(): half = lax.all_to_all(jnp.broadcast_to(stacked, (16, 96, 384)), yx, 0, 0)]
    all_to_all x3 -> x0, starting transfers between devices: 21.9 us -> none  [the longest x1 8.71 us: on_device(): over_z = lax.all_to_all(with_gain(plane, gain), 'z', 0, 0).astype(f32)]
    ppermute x1, waiting for transfers between devices: 10.7 us -> 0.01 us  [on_device(): lax.ppermute(jnp.concatenate([activated[:, :2 * D], cot_perm[:, :D]], 1),...]
    all_to_all x1, waiting for transfers between devices: 15.3 us -> 7.07 us  [on_device(): lax.all_to_all(chip, yx, 0, 0).astype(f32)]
    dot_general x3, matrix products: 6.46 us -> 9.54 us  [on_device(): jnp.einsum('snh,hc->snc', sum_cot[:, (2 - k) * D:(2 - k) * D + bins], tap...]
    unnamed x51 -> x53, local copies, waits for them, and re-layouts: 3.8 us -> 3.68 us
  transfers between devices with their start and end apart: 8 -> 5, of which waited for: 6 -> 1; matrix products, arithmetic and copies ran while one was open for 11% -> 13% of each run, Pallas kernels for 0% -> 0%
where the time goes in v2:
time: 161 us
  blocking collectives  81.2 us (50%)
  matrix products  25.1 us (16%)
  local copies, waits for them, and re-layouts  18.2 us (11%)
  starting transfers between devices  17.8 us (11%)
  other arithmetic  9.85 us (6%)
  waiting for transfers between devices  7.08 us (4%)
    all_to_all x1, blocking collectives, on_device(): from_z = lax.all_to_all(jnp.broadcast_to(piece, (16, 6, 384)), 'z', 0, 0)  28.2 us
    all_to_all x1, blocking collectives, on_device(): half = lax.all_to_all(jnp.broadcast_to(stacked, (16, 96, 384)), yx, 0, 0)  22.2 us
    all_to_all x1, blocking collectives, on_device(): over_z = lax.all_to_all(with_gain(plane, gain), 'z', 0, 0).astype(f32)  15.5 us
    all_to_all x1, blocking collectives, on_device(): lax.all_to_all(jnp.broadcast_to(final[None], (32, 8, 384)), ('c', 'y', 'x...  15.2 us
    dot_general x3, matrix products, on_device(): jnp.einsum('snh,hc->snc', sum_cot[:, (2 - k) * D:(2 - k) * D + bins], tap...  9.54 us
    all_to_all x1, waiting for transfers between devices, on_device(): lax.all_to_all(chip, yx, 0, 0).astype(f32)  7.07 us
    ppermute x1, starting transfers between devices, on_device(): other = lax.ppermute(half, 'c', [(0, 1), (1, 0)])  6 us
    ppermute x1, starting transfers between devices, on_device(): lax.ppermute(jnp.concatenate([activated[:, -2 * D:], cot_perm[:, -D:]], 1...  4.54 us
  transfers between devices with their start and end apart: 5, of which 1 were waited for; matrix products, arithmetic and copies ran while one was open for 13% of the time, Pallas kernels for 0%

profile of v2, /device:TPU:1, one launch (start us, length us, event | category | flops | bytes accessed | tf_op | source)
XLA Modules:
  0.0 160.6 jit_solution(4991748633210273957)
XLA Ops:
  0.6 1.4 fusion.7
  2.1 2.3 %fusion.28 = bf16[2,256,768]{2,1,0:T(8,128)(2,1)S(1)} fusion(bf16[768,768,1]{1,0,2:T(8,128)(2,1)} %constant.85, bf16[2,256,768]{2,1,0:T(8,128)(2,1)} %param.11), kind=kOutput, calls=%fused_computation.53 | convolution fusion | flops 604372992 | bytes 2752512 | tf_op jit(solution)/shard_map/snc,cd->snd/dot_general | solution.py:49
  4.5 0.8 copy-done.23
  5.3 0.7 fusion.12
  6.1 4.5 %collective-permute-start = (bf16[2,192,768]{2,1,0:T(8,128)(2,1)S(1)}, bf16[2,192,768]{2,1,0:T(8,128)(2,1)S(1)}, u32[]{:S(2)}, u32[]{:S(2)}) collective-permute-start(bf16[2,192,768]{2,1,0:T(8,128)(2,1)S(1)} %pad_maximum_fusion.7), channel_id=1, source_target_pairs={{0,1},{1,2},{2,3},{3,4},{4,5},{5,6},{6,7},{7,8},{8,9},{9,10},{10,1... | collective-permute-start | bytes 1769480 | tf_op jit(solution)/shard_map/ppermute | solution.py:52
  10.7 1.3 collective-permute-start.1
  12.3 0.9 reshape.91
  13.4 28.2 %all_to_all.25 = bf16[16,6,384]{2,1,0:T(8,128)(2,1)S(1)} all-to-all(bf16[16,6,384]{2,1,0:T(8,128)(2,1)S(1)} %broadcast_in_dim.11), channel_id=1, replica_groups=mesh['y'=4,'x'=4,'c'=2,'z'=16] {'z'}, dimensions={0} | all-to-all | bytes 147456 | tf_op jit(solution)/shard_map/all_to_all | solution.py:64
  41.7 0.8 copy-done.18
  42.8 22.2 %all_to_all.26 = bf16[16,96,384]{2,1,0:T(8,128)(2,1)S(1)} all-to-all(bf16[16,96,384]{2,1,0:T(8,128)(2,1)S(1)} %broadcast_in_dim.13), channel_id=1, replica_groups=mesh['y'=4,'x'=4,'c'=2,'z'=16] {'y','x'}, dimensions={0} | all-to-all | bytes 2359296 | tf_op jit(solution)/shard_map/all_to_all | solution.py:67
  65.1 6.0 %collective-permute-start.2 = (bf16[16,96,384]{2,1,0:T(8,128)(2,1)S(1)}, bf16[16,96,384]{2,1,0:T(8,128)(2,1)S(1)}, u32[]{:S(2)}, u32[]{:S(2)}) collective-permute-start(bf16[16,96,384]{2,1,0:T(8,128)(2,1)S(1)} %all_to_all.26), channel_id=1, source_target_pairs={{0,16},{16,0},{1,17},{17,1},{2,18},{18,2},{3,19},{19,3},{4,20},{20... | collective-permute-start | bytes 3538952 | tf_op jit(solution)/shard_map/ppermute | solution.py:68
  71.1 1.8 %slice.105 = bf16[2,128,768]{2,1,0:T(8,128)(2,1)} slice(bf16[2,192,768]{2,1,0:T(8,128)(2,1)} %copy-done.18), slice={[0:2], [0:128], [0:768]} | slice | bytes 786432 | tf_op jit(solution)/shard_map/slice | solution.py:77
  72.9 0.8 slice.108
  73.9 0.9 slice.129
  75.0 1.6 copy.74
  76.6 1.5 fusion.85
  78.1 1.2 reshape.110
  79.3 0.4 reshape.109
  79.7 0.4 reshape.108
  80.1 2.0 %fusion.41 = f32[2,384,384]{2,1,0:T(8,128)S(1)} fusion(bf16[384,768,1]{1,0,2:T(8,128)(2,1)S(1)} %reshape.108, bf16[2,256,768]{2,1,0:T(8,128)(2,1)S(1)} %copy-done.3, bf16[2,128,768]{2,1,0:T(8,128)(2,1)} %slice.105), kind=kOutput, calls=%fused_computation.69 | convolution fusion | flops 455344128 | bytes 2949120 | tf_op jit(solution)/shard_map/snc,hc->snh/dot_general | solution.py:82
  82.2 0.8 convolution_add_fusion.1
  83.0 0.2 copy-done.7
  83.2 0.8 convolution_add_fusion
  84.0 0.3 copy-done.24
  84.4 1.5 fusion.24
  85.9 0.3 copy-done.21
  86.2 1.2 fusion.27
  87.5 0.5 fusion.23
  88.0 0.5 fusion.21
  88.5 1.4 fusion.22
  90.1 1.8 %stack.13 = bf16[1,4,96,2,384]{4,3,2,1,0:T(2,128)(2,1)S(1)} reshape(bf16[384,768]{1,0:T(8,128)(2,1)} %fusion.22) | data formatting | bytes 1179648 | tf_op jit(solution)/shard_map/stack | solution.py:89
  92.5 0.8 copy-done.17
  93.3 0.3 pad_maximum_fusion
  93.6 1.2 dynamic-slice_bitcast_fusion
  94.7 2.1 %collective-permute-start.3 = (bf16[16,96,384]{2,1,0:T(8,128)(2,1)}, bf16[16,96,384]{2,1,0:T(8,128)(2,1)}, u32[]{:S(2)}, u32[]{:S(2)}) collective-permute-start(bf16[16,96,384]{2,1,0:T(8,128)(2,1)} %dynamic-slice_bitcast_fusion), channel_id=1, source_target_pairs={{0,16},{16,0},{1,17},{17,1},{2,18},{18,2},{3,19},{19,3},{4,20},{20... | collective-permute-start | bytes 3538952 | tf_op jit(solution)/shard_map/ppermute | solution.py:106
  96.9 3.0 %fusion.64 = f32[2,256,768]{2,1,0:T(8,128)} fusion(bf16[384,768,1]{1,0,2:T(8,128)(2,1)} %copy-done.4, bf16[2,384,384]{2,1,0:T(8,128)(2,1)} %copy-done.14), kind=kOutput, calls=%fused_computation.99 | convolution fusion | flops 301989888 | bytes 2555904 | tf_op jit(solution)/shard_map/snh,hc->snc/dot_general | solution.py:111
  100.0 1.7 %fusion.62 = f32[2,256,768]{2,1,0:T(8,128)} fusion(bf16[384,768,1]{1,0,2:T(8,128)(2,1)S(1)} %copy-done.6, bf16[2,384,384]{2,1,0:T(8,128)(2,1)S(1)} %copy-done.15), kind=kOutput, calls=%fused_computation.97 | convolution fusion | flops 301989888 | bytes 2555904 | tf_op jit(solution)/shard_map/snh,hc->snc/dot_general | solution.py:111
  101.7 2.7 %fusion = bf16[16,96,384]{2,1,0:T(8,128)(2,1)} fusion(bf16[16,96,384]{2,1,0:T(8,128)(2,1)} %collective-permute-done.3, bf16[2,16,96,384]{3,2,1,0:T(8,128)(2,1)S(1)} %bitcast.75, s32[]{:T(128)S(6)} %select_n.27), kind=kLoop, calls=%fused_computation.10 | loop fusion | flops 2359296 | bytes 3538948 | tf_op jit(solution)/shard_map/convert_element_type | solution.py:107
  104.4 3.8 %all-to-all-start.2 = ((bf16[16,96,384]{2,1,0:T(8,128)(2,1)}), bf16[16,96,384]{2,1,0:T(8,128)(2,1)S(1)}, u32[]{:S(2)}, u32[]{:S(2)}) async-start(bf16[16,96,384]{2,1,0:T(8,128)(2,1)} %fusion), calls=%async_computation.2 | async-start | bytes 2359296 | tf_op jit(solution)/shard_map/all_to_all | solution.py:108
  108.2 4.8 %fusion.20 = (f32[2,256]{1,0:T(2,128)S(1)}, f32[768]{0:T(1024)S(1)}, f32[2,256,768]{2,1,0:T(8,128)}) fusion(bf16[2,256,768]{2,1,0:T(8,128)(2,1)S(1)} %copy-done.1, f32[768]{0:T(1024)S(1)} %copy-done.25, f32[2,256]{1,0:T(2,128)S(1)} %get-tuple-element.37, bf16[384,768,1]{1,0,2:T(8,128)(2,1)S(1)} %copy-done.8, bf16[2,384,384]{2,1,0:T(8,128)(2,1)S(1)} %copy-done.16, ...), kind=kOutput, calls=%fused_computation.35 | convolution fusion | flops 314178304 | bytes 6499328 | tf_op jit(solution)/shard_map/snh,hc->snc/dot_general | solution.py:111
  113.1 3.1 %fusion.19 = bf16[2,256,768]{2,1,0:T(8,128)(2,1)} fusion(bf16[2,256,768]{2,1,0:T(8,128)(2,1)S(1)} %copy-done.1, bf16[2,256,768]{2,1,0:T(8,128)(2,1)} %param.11, f32[2,256,768]{2,1,0:T(8,128)} %get-tuple-element.38, f32[2,256]{1,0:T(2,128)S(1)} %broadcast_multiply_fusion, f32[2,256]{1,0:T(2,128)S(1)} %get-tuple-element.36, f32[768]{0:T(1024)S(1)} %copy-done.25, ...), kind=kLoop, calls=%fused_computation.34 | loop fusion | flops 3538944 | bytes 3941376 | tf_op jit(solution)/shard_map/convert_element_type | solution.py:120
  116.3 3.5 %fusion.16 = bf16[2,256,768]{2,1,0:T(8,128)(2,1)} fusion(bf16[2,256,768]{2,1,0:T(8,128)(2,1)S(1)} %copy-done.1, bf16[768,384]{1,0:T(8,128)(2,1)} %bitcast.81, bf16[768,768]{1,0:T(8,128)(2,1)} %constant.77.clone, f32[2,384,384]{2,1,0:T(8,128)S(1)} %copy-done.13), kind=kOutput, calls=%fused_computation.31 | convolution fusion | flops 758218752 | bytes 4128768 | tf_op jit(solution)/shard_map/snh,ch->snc/dot_general | solution.py:123
  119.7 7.1 %all-to-all-done.2 = bf16[16,96,384]{2,1,0:T(8,128)(2,1)S(1)} async-done(((bf16[16,96,384]{2,1,0:T(8,128)(2,1)}), bf16[16,96,384]{2,1,0:T(8,128)(2,1)S(1)}, u32[]{:S(2)}, u32[]{:S(2)}) %all-to-all-start.2) | async-done | bytes 1179680 | tf_op jit(solution)/shard_map/all_to_all | solution.py:108
  127.1 15.5 %all_to_all.27 = bf16[16,8,384]{2,1,0:T(8,128)(2,1)S(1)} all-to-all(bf16[16,8,384]{2,1,0:T(8,128)(2,1)S(1)} %pad_maximum_fusion.9), channel_id=1, replica_groups=mesh['y'=4,'x'=4,'c'=2,'z'=16] {'z'}, dimensions={0} | all-to-all | bytes 196608 | tf_op jit(solution)/shard_map/all_to_all | solution.py:137
  142.8 15.2 %all_to_all.28 = bf16[32,8,384]{2,1,0:T(8,128)(2,1)S(1)} all-to-all(bf16[32,8,384]{2,1,0:T(8,128)(2,1)S(1)} %broadcast_in_dim.28), channel_id=1, replica_groups=mesh['y'=4,'x'=4,'c'=2,'z'=16] {'c','y','x'}, dimensions={0} | all-to-all | bytes 393216 | tf_op jit(solution)/shard_map/all_to_all | solution.py:141
  158.1 0.5 broadcast_multiply_fusion.1
  158.6 0.9 fusion.48
  159.7 0.9 mul.275
  (98 shorter events, 2.9 us)
Async XLA Ops:
  0.6 11.4 %copy-start = (bf16[384,48]{0,1:T(8,128)(2,1)S(1)}, bf16[384,48]{0,1:T(8,128)(2,1)}, u32[]{:S(2)}) copy-start(bf16[384,48]{0,1:T(8,128)(2,1)} %param.10) | copy-start | bytes 110596
  2.0 3.3 %copy-start.1 = (bf16[2,256,768]{2,1,0:T(8,128)(2,1)S(1)}, bf16[2,256,768]{2,1,0:T(8,128)(2,1)}, u32[]{:S(2)}) copy-start(bf16[2,256,768]{2,1,0:T(8,128)(2,1)} %param.7) | copy-start | bytes 2359300
  2.0 3.3 %copy-start.25 = (f32[768]{0:T(1024)S(1)}, f32[768]{0:T(1024)}, u32[]{:S(2)}) copy-start(f32[768]{0:T(1024)} %param.8) | copy-start | bytes 9220
  4.4 0.9 copy-start.23
  6.0 4.7 %copy-start.2 = (bf16[2,256,768]{2,1,0:T(8,128)(2,1)}, bf16[2,256,768]{2,1,0:T(8,128)(2,1)S(1)}, u32[]{:S(2)}) copy-start(bf16[2,256,768]{2,1,0:T(8,128)(2,1)S(1)} %fusion.12) | copy-start | bytes 2359300
  6.1 6.0 %copy-start.10 = (bf16[384,384]{1,0:T(8,128)(2,1)S(1)}, bf16[384,384]{1,0:T(8,128)(2,1)}, u32[]{:S(2)}) copy-start(bf16[384,384]{1,0:T(8,128)(2,1)} %constant.76.clone) | copy-start | bytes 884740
  6.1 35.5 %collective-permute-start = (bf16[2,192,768]{2,1,0:T(8,128)(2,1)S(1)}, bf16[2,192,768]{2,1,0:T(8,128)(2,1)S(1)}, u32[]{:S(2)}, u32[]{:S(2)}) collective-permute-start(bf16[2,192,768]{2,1,0:T(8,128)(2,1)S(1)} %pad_maximum_fusion.7), channel_id=1, source_target_pairs={{0,1},{1,2},{2,3},{3,4},{4,5},{5,6},{6,7},{7,8},{8,9},{9,10},{10,1... | collective-permute-start | bytes 1769480 | tf_op jit(solution)/shard_map/ppermute | solution.py:52
  10.7 30.9 %collective-permute-start.1 = (bf16[2,192,768]{2,1,0:T(8,128)(2,1)S(1)}, bf16[2,192,768]{2,1,0:T(8,128)(2,1)S(1)}, u32[]{:S(2)}, u32[]{:S(2)}) collective-permute-start(bf16[2,192,768]{2,1,0:T(8,128)(2,1)S(1)} %pad_maximum_fusion.8), channel_id=1, source_target_pairs={{1,0},{2,1},{3,2},{4,3},{5,4},{6,5},{7,6},{8,7},{9,8},{10,9},{11,1... | collective-permute-start | bytes 1769480 | tf_op jit(solution)/shard_map/ppermute | solution.py:53
  41.7 0.8 copy-start.18
  41.7 1.0 copy-start.19
  65.1 8.6 %collective-permute-start.2 = (bf16[16,96,384]{2,1,0:T(8,128)(2,1)S(1)}, bf16[16,96,384]{2,1,0:T(8,128)(2,1)S(1)}, u32[]{:S(2)}, u32[]{:S(2)}) collective-permute-start(bf16[16,96,384]{2,1,0:T(8,128)(2,1)S(1)} %all_to_all.26), channel_id=1, source_target_pairs={{0,16},{16,0},{1,17},{17,1},{2,18},{18,2},{3,19},{19,3},{4,20},{20... | collective-permute-start | bytes 3538952 | tf_op jit(solution)/shard_map/ppermute | solution.py:68
  71.1 1.8 %copy-start.20 = (bf16[2,192,768]{2,1,0:T(8,128)(2,1)S(1)}, bf16[2,192,768]{2,1,0:T(8,128)(2,1)}, u32[]{:S(2)}) copy-start(bf16[2,192,768]{2,1,0:T(8,128)(2,1)} %copy-done.19) | copy-start | bytes 1769476
  78.1 2.0 %copy-start.3 = (bf16[2,256,768]{2,1,0:T(8,128)(2,1)S(1)}, bf16[2,256,768]{2,1,0:T(8,128)(2,1)}, u32[]{:S(2)}) copy-start(bf16[2,256,768]{2,1,0:T(8,128)(2,1)} %copy-done.2) | copy-start | bytes 2359300
  79.7 2.5 %copy-start.4 = (bf16[384,768,1]{1,0,2:T(8,128)(2,1)}, bf16[384,768,1]{1,0,2:T(8,128)(2,1)S(1)}, u32[]{:S(2)}) copy-start(bf16[384,768,1]{1,0,2:T(8,128)(2,1)S(1)} %reshape.109) | copy-start | bytes 1769476
  80.1 2.1 %copy-start.5 = (bf16[384,768,1]{1,0,2:T(8,128)(2,1)}, bf16[384,768,1]{1,0,2:T(8,128)(2,1)S(1)}, u32[]{:S(2)}) copy-start(bf16[384,768,1]{1,0,2:T(8,128)(2,1)S(1)} %reshape.108) | copy-start | bytes 1769476
  80.1 2.1 %copy-start.9 = (bf16[2,128,768]{2,1,0:T(8,128)(2,1)S(1)}, bf16[2,128,768]{2,1,0:T(8,128)(2,1)}, u32[]{:S(2)}) copy-start(bf16[2,128,768]{2,1,0:T(8,128)(2,1)} %slice.108) | copy-start | bytes 1179652
  80.1 2.1 %copy-start.22 = (bf16[2,128,768]{2,1,0:T(8,128)(2,1)S(1)}, bf16[2,128,768]{2,1,0:T(8,128)(2,1)}, u32[]{:S(2)}) copy-start(bf16[2,128,768]{2,1,0:T(8,128)(2,1)} %slice.105) | copy-start | bytes 1179652
  82.2 1.1 copy-start.7
  83.2 1.1 copy-start.24
  84.4 1.5 copy-start.12
  84.4 1.5 slice-start
  84.4 1.5 slice-start.1
  84.4 1.9 %copy-start.21 = (bf16[8,96,384]{2,1,0:T(8,128)(2,1)S(1)}, bf16[8,96,384]{2,1,0:T(8,128)(2,1)}, u32[]{:S(2)}) copy-start(bf16[8,96,384]{2,1,0:T(8,128)(2,1)} %slice.129) | copy-start | bytes 1769476
  87.5 1.0 copy-start.14
  92.2 1.1 copy-start.17
  94.7 6.9 %collective-permute-start.3 = (bf16[16,96,384]{2,1,0:T(8,128)(2,1)}, bf16[16,96,384]{2,1,0:T(8,128)(2,1)}, u32[]{:S(2)}, u32[]{:S(2)}) collective-permute-start(bf16[16,96,384]{2,1,0:T(8,128)(2,1)} %dynamic-slice_bitcast_fusion), channel_id=1, source_target_pairs={{0,16},{16,0},{1,17},{17,1},{2,18},{18,2},{3,19},{19,3},{4,20},{20... | collective-permute-start | bytes 3538952 | tf_op jit(solution)/shard_map/ppermute | solution.py:106
  96.9 3.1 %copy-start.6 = (bf16[384,768,1]{1,0,2:T(8,128)(2,1)S(1)}, bf16[384,768,1]{1,0,2:T(8,128)(2,1)}, u32[]{:S(2)}) copy-start(bf16[384,768,1]{1,0,2:T(8,128)(2,1)} %copy-done.5) | copy-start | bytes 1769476
  96.9 3.0 %copy-start.15 = (bf16[2,384,384]{2,1,0:T(8,128)(2,1)S(1)}, bf16[2,384,384]{2,1,0:T(8,128)(2,1)}, u32[]{:S(2)}) copy-start(bf16[2,384,384]{2,1,0:T(8,128)(2,1)} %copy-done.14) | copy-start | bytes 1769476
  104.4 3.8 %copy-start.8 = (bf16[384,768,1]{1,0,2:T(8,128)(2,1)S(1)}, bf16[384,768,1]{1,0,2:T(8,128)(2,1)}, u32[]{:S(2)}) copy-start(bf16[384,768,1]{1,0,2:T(8,128)(2,1)} %reshape.110) | copy-start | bytes 1769476
  104.4 3.9 %copy-start.16 = (bf16[2,384,384]{2,1,0:T(8,128)(2,1)S(1)}, bf16[2,384,384]{2,1,0:T(8,128)(2,1)}, u32[]{:S(2)}) copy-start(bf16[2,384,384]{2,1,0:T(8,128)(2,1)} %copy-done.14) | copy-start | bytes 1769476
  104.4 22.4 %all-to-all-start.2 = ((bf16[16,96,384]{2,1,0:T(8,128)(2,1)}), bf16[16,96,384]{2,1,0:T(8,128)(2,1)S(1)}, u32[]{:S(2)}, u32[]{:S(2)}) async-start(bf16[16,96,384]{2,1,0:T(8,128)(2,1)} %fusion), calls=%async_computation.2 | async-start | bytes 2359296 | tf_op jit(solution)/shard_map/all_to_all | solution.py:108
  113.1 3.1 %copy-start.13 = (f32[2,384,384]{2,1,0:T(8,128)S(1)}, f32[2,384,384]{2,1,0:T(8,128)}, u32[]{:S(2)}) copy-start(f32[2,384,384]{2,1,0:T(8,128)} %copy-done.12) | copy-start | bytes 3538948
  119.7 38.9 %copy-start.11 = (bf16[384,384]{1,0:T(8,128)(2,1)S(1)}, bf16[384,384]{1,0:T(8,128)(2,1)}, u32[]{:S(2)}) copy-start(bf16[384,384]{1,0:T(8,128)(2,1)} %constant.76.clone) | copy-start | bytes 884740

commit v3 on v1

v3 whole, which is shorter than its diff:
```python
import jax
import jax.numpy as jnp
import numpy as np
from jax import lax
from jax.experimental import pallas as pl
from jax.experimental.pallas import tpu as pltpu
from jax.sharding import Mesh, PartitionSpec as P

STEP = 64
SEQS = 2
BINS = 256
CHANNELS = 768
HIDDEN = 384
EXT = BINS + 2 * STEP
gelu_scale = 0.7978845608
cubic_term = 0.044715
epsilon = 1e-06
bf16 = jnp.bfloat16
f32 = jnp.float32
HBM = pl.BlockSpec(memory_space=pl.ANY)
SMEM = pl.BlockSpec(memory_space=pltpu.SMEM)
VMEM = pl.BlockSpec(memory_space=pltpu.VMEM)
PARAMS = pltpu.CompilerParams(vmem_limit_bytes=48 * 1024 * 1024)


def permutation(outer, inner, width):
    size = outer * inner * width
    order = np.arange(size).reshape(inner, outer, width).transpose(1, 0, 2).reshape(-1)
    matrix = np.zeros((size, size), np.float32)
    matrix[order, np.arange(size)] = 1.0
    return matrix


def dot(a, b, ca, cb):
    return lax.dot_general(a, b, (((ca,), (cb,)), ((), ())), preferred_element_type=f32)


def tanh_of(v):
    return jnp.tanh(gelu_scale * (v + cubic_term * v * v * v))


def activate(v, t):
    return 0.5 * v * (1.0 + t)


def derivative(v, t):
    return 0.5 * (1.0 + t) + 0.5 * v * (1.0 - t * t) * gelu_scale * (1.0 + 3.0 * cubic_term * v * v)


def inverse_rms_of(v):
    return lax.rsqrt(jnp.mean(v * v, axis=-1, keepdims=True) + epsilon)


def piece_kernel(part, taps, proj, perm, out, pieces):
    for k in range(3):
        tap = taps[k].astype(f32)
        for q in range(4):
            for half in range(2):
                pieces[(q * 3 + k) * 2 + half, 0:6] = tap[6 * q : 6 * q + 6, half * 384 : half * 384 + 384]
    rows = dot(proj[...], perm[...], 1, 0)
    for u in range(8):
        pieces[24 + u, 0:6] = rows[6 * u : 6 * u + 6]
    pieces[:, 6:8] = jnp.zeros((32, 2, 384), f32)
    own = pieces[part[0]].astype(bf16)
    for z in range(16):
        out[z] = own


def stack_kernel(given, out, rows, packed, sems):
    for z in range(16):
        rows[6 * z : 6 * z + 6] = given[z].astype(f32)[0:6]
    packed[...] = rows[...].astype(bf16)
    copies = [pltpu.make_async_copy(packed, out.at[i], sems.at[i]) for i in range(16)]
    for c in copies:
        c.start()
    for c in copies:
        c.wait()


def norm_kernel(tokens, gain, cot, perm, activated, cot_perm, up, down):
    v = tokens[0].astype(f32)
    normed = v * inverse_rms_of(v) * gain[...]
    a = activate(normed, tanh_of(normed)).astype(bf16)
    c = dot(cot[0], perm[...], 1, 0).astype(bf16)
    activated[0] = a
    cot_perm[0] = c
    up[0, 0 : 2 * STEP] = a[BINS - 2 * STEP :]
    up[0, 2 * STEP :] = c[BINS - STEP :]
    down[0, 0 : 2 * STEP] = a[: 2 * STEP]
    down[0, 2 * STEP :] = c[:STEP]


def weight_copies(core, mine, other, taps, proj, sems, act):
    for here in range(2):

        @pl.when(core[0] == here)
        def _(here=here):
            for p in range(32):
                source = (mine if p // 16 == here else other).at[p % 16]
                if p < 24:
                    q, k, half = p // 6, p % 6 // 2, p % 2
                    target = taps.at[k, 96 * q : 96 * q + 96, 384 * half : 384 * half + 384]
                else:
                    target = proj.at[96 * (p - 24) : 96 * (p - 24) + 96]
                copy = pltpu.make_async_copy(source, target, sems.at[p])
                copy.start() if act else copy.wait()


def main_kernel(
    core, mine, other, activated, cot_perm, before, after,
    keep, send, sum_cot_out, hidden_out,
    taps, proj, act, cot, sum_cot, hidden, grad, wsems, sems,
):
    weight_copies(core, mine, other, taps, proj, wsems, True)
    halo, own = 2 * STEP, BINS
    loads = [
        (before.at[:, 0:halo], act.at[:, 0:halo]),
        (activated, act.at[:, halo : halo + own]),
        (after.at[:, 0:halo], act.at[:, halo + own :]),
        (before.at[:, halo:], cot.at[:, 0:STEP]),
        (cot_perm, cot.at[:, STEP : STEP + own]),
        (after.at[:, halo:], cot.at[:, STEP + own :]),
    ]
    loads = [pltpu.make_async_copy(a, b, sems.at[i]) for i, (a, b) in enumerate(loads)]
    for c in loads:
        c.start()
    for c in loads:
        c.wait()
    weight_copies(core, mine, other, taps, proj, wsems, False)
    for s in range(SEQS):
        total = dot(act[s, 0:EXT], taps[0], 1, 1)
        total += dot(act[s, STEP : STEP + EXT], taps[1], 1, 1)
        total += dot(act[s, 2 * STEP : 2 * STEP + EXT], taps[2], 1, 1)
        hidden_cot = dot(cot[s], proj[...], 1, 0).astype(bf16).astype(f32)
        t = tanh_of(total)
        hidden[s] = activate(total, t)[STEP : STEP + own].astype(bf16)
        sum_cot[s] = (hidden_cot * derivative(total, t)).astype(bf16)
    saves = [
        pltpu.make_async_copy(sum_cot, sum_cot_out, sems.at[6]),
        pltpu.make_async_copy(hidden, hidden_out, sems.at[7]),
    ]
    for c in saves:
        c.start()
    centre = jnp.concatenate([sum_cot[s, STEP : STEP + own] for s in range(SEQS)])
    for k in range(3):
        rows = jnp.concatenate([act[s, STEP * (k + 1) : STEP * (k + 1) + own] for s in range(SEQS)])
        g = dot(centre, rows, 0, 0).astype(bf16)
        for q in range(4):
            for half in range(2):
                grad[(q * 3 + k) * 2 + half] = g[96 * q : 96 * q + 96, 384 * half : 384 * half + 384]
    rows = jnp.concatenate([cot[s, STEP : STEP + own] for s in range(SEQS)])
    g = dot(rows, jnp.concatenate([hidden[s] for s in range(SEQS)]), 0, 0).astype(bf16)
    for u in range(8):
        grad[24 + u] = g[96 * u : 96 * u + 96]
    saves += [
        pltpu.make_async_copy(grad.at[pl.ds(16 * core[0], 16)], keep, sems.at[8]),
        pltpu.make_async_copy(grad.at[pl.ds(16 - 16 * core[0], 16)], send, sems.at[9]),
    ]
    for c in saves[2:]:
        c.start()
    for c in saves:
        c.wait()


def pair_kernel(a, b, out):
    out[...] = (a[...].astype(f32) + b[...].astype(f32)).astype(bf16)


def tail_kernel(
    core, mine, other, sum_cot, hidden, tokens, gain, cot, perm,
    block_output, token_gradient, gain_rows,
    taps, proj, wsems,
):
    weight_copies(core, mine, other, taps, proj, wsems, True)
    weight_copies(core, mine, other, taps, proj, wsems, False)
    natural = dot(perm[...], proj[...], 1, 0).astype(bf16)
    gain_row = gain[...]
    gain_sum = jnp.zeros((1, CHANNELS), f32)
    for s in range(SEQS):
        v = tokens[s].astype(f32)
        block_output[s] = (v + dot(hidden[s], natural, 1, 1)).astype(bf16)
        total = dot(sum_cot[s, 2 * STEP : 2 * STEP + BINS], taps[0], 1, 0)
        total += dot(sum_cot[s, STEP : STEP + BINS], taps[1], 1, 0)
        total += dot(sum_cot[s, 0:BINS], taps[2], 1, 0)
        inverse_rms = inverse_rms_of(v)
        normed = v * inverse_rms * gain_row
        normed_cot = total.astype(bf16).astype(f32) * derivative(normed, tanh_of(normed))
        scaled_cot = gain_row * normed_cot
        mean = jnp.mean(scaled_cot * v, axis=-1, keepdims=True)
        token_gradient[s] = (
            cot[s].astype(f32) + inverse_rms * scaled_cot - v * (inverse_rms * inverse_rms * inverse_rms) * mean
        ).astype(bf16)
        gain_sum += jnp.sum(normed_cot * v * inverse_rms, axis=0, keepdims=True)
    gain_rows[...] = jnp.zeros((16, 384), f32)
    for z in range(16):
        gain_rows[z : z + 1, 0:48] = gain_sum[:, 48 * z : 48 * z + 48]


def split_high_low(v):
    high = v.astype(bf16).astype(f32)
    return high, v - high


def plane_kernel(given, gain_rows, out, rows):
    total = given[0].astype(f32)
    for i in range(1, 16):
        total += given[i].astype(f32)
    rows[...] = total
    for z in range(16):
        high, low = split_high_low(gain_rows[z : z + 1])
        out[z] = jnp.concatenate([rows[6 * z : 6 * z + 6], high, low]).astype(bf16)


def column_kernel(given, out):
    total = given[0].astype(f32)
    for z in range(1, 16):
        total += given[z].astype(f32)
    high, low = split_high_low(total[6:7] + total[7:8])
    block = jnp.concatenate([total[0:6], high, low]).astype(bf16)
    for i in range(32):
        out[i] = block


def final_kernel(given, perm, taps, proj, gain, rows):
    scale = 1.0 / 64
    for q in range(4):
        for k in range(3):
            for half in range(2):
                block = given[(q * 3 + k) * 2 + half].astype(f32)
                taps[k, 6 * q : 6 * q + 6, 384 * half : 384 * half + 384] = block[0:6] * scale
    for u in range(8):
        rows[6 * u : 6 * u + 6] = given[24 + u].astype(f32)[0:6]
    proj[...] = dot(rows[...].astype(bf16), perm[...], 1, 1) * scale
    total = given[0].astype(f32)
    for i in range(1, 32):
        total += given[i].astype(f32)
    gain[...] = (total[6:7] + total[7:8])[:, 0:128] * scale


def call(kernel, out, ins, outs, name, scratch=(), **more):
    return pl.pallas_call(
        kernel,
        out_shape=out,
        in_specs=ins,
        out_specs=outs,
        scratch_shapes=scratch,
        compiler_params=PARAMS,
        name=name,
        **more,
    )


def shape(dims, kind):
    return jax.ShapeDtypeStruct(dims, kind)


HALF = shape((16, 96, 384), bf16)
ROWS = shape((SEQS, BINS, CHANNELS), bf16)
WEIGHTS = [pltpu.VMEM((3, HIDDEN, CHANNELS), bf16), pltpu.VMEM((CHANNELS, HIDDEN), bf16)]


def make_piece(part, taps, proj, perm):
    return call(
        piece_kernel, shape((16, 8, 384), bf16), [SMEM] + [VMEM] * 3, VMEM, "piece", [pltpu.VMEM((32, 8, 384), f32)]
    )(part, taps, proj, perm)


def make_stack(given):
    scratch = [pltpu.VMEM((96, 384), f32), pltpu.VMEM((96, 384), bf16), pltpu.SemaphoreType.DMA((16,))]
    return call(stack_kernel, HALF, [VMEM], HBM, "stack", scratch)(given)


def make_norm(tokens, gain, cot, perm):
    block = pl.BlockSpec((1, BINS, CHANNELS), lambda s: (s, 0, 0))
    edge = pl.BlockSpec((1, 3 * STEP, CHANNELS), lambda s: (s, 0, 0))
    edge_shape = shape((SEQS, 3 * STEP, CHANNELS), bf16)
    return call(
        norm_kernel,
        [ROWS, ROWS, edge_shape, edge_shape],
        [
            block,
            pl.BlockSpec((1, CHANNELS), lambda s: (0, 0)),
            block,
            pl.BlockSpec((CHANNELS, CHANNELS), lambda s: (0, 0)),
        ],
        [block, block, edge, edge],
        "norm",
        grid=(SEQS,),
    )(tokens, gain, cot, perm)


def make_main(core, mine, other, activated, cot_perm, before, after):
    sum_cot = (SEQS, EXT, HIDDEN)
    hidden = (SEQS, BINS, HIDDEN)
    return call(
        main_kernel,
        [HALF, HALF, shape(sum_cot, bf16), shape(hidden, bf16)],
        [SMEM] + [HBM] * 6,
        [HBM] * 4,
        "main",
        WEIGHTS
        + [
            pltpu.VMEM((SEQS, BINS + 4 * STEP, CHANNELS), bf16),
            pltpu.VMEM((SEQS, EXT, CHANNELS), bf16),
            pltpu.VMEM(sum_cot, bf16),
            pltpu.VMEM(hidden, bf16),
            pltpu.VMEM((32, 96, 384), bf16),
            pltpu.SemaphoreType.DMA((32,)),
            pltpu.SemaphoreType.DMA((10,)),
        ],
    )(core, mine, other, activated, cot_perm, before, after)


def make_pair(a, b):
    block = pl.BlockSpec((4, 96, 384), lambda i: (i, 0, 0))
    return call(pair_kernel, HALF, [block, block], block, "pair", grid=(4,))(a, b)


def make_tail(core, mine, other, sum_cot, hidden, tokens, gain, cot, perm):
    return call(
        tail_kernel,
        [ROWS, ROWS, shape((16, 384), f32)],
        [SMEM, HBM, HBM] + [VMEM] * 6,
        [VMEM] * 3,
        "tail",
        WEIGHTS + [pltpu.SemaphoreType.DMA((32,))],
    )(core, mine, other, sum_cot, hidden, tokens, gain, cot, perm)


def make_plane(given, gain_rows):
    return call(
        plane_kernel, shape((16, 8, 384), bf16), [VMEM] * 2, VMEM, "plane", [pltpu.VMEM((96, 384), f32)]
    )(given, gain_rows)


def make_column(given):
    return call(column_kernel, shape((32, 8, 384), bf16), [VMEM], VMEM, "column")(given)


def make_final(given, perm):
    return call(
        final_kernel,
        [shape((3, 24, CHANNELS), f32), shape((48, 384), f32), shape((1, 128), f32)],
        [VMEM] * 2,
        [VMEM] * 3,
        "final",
        [pltpu.VMEM((48, 384), f32)],
    )(given, perm)


def on_device(tokens, norm_gain, dilated_weight, output_weight, cotangent):
    yx = ("y", "x")
    swap = [(0, 1), (1, 0)]
    core = lax.axis_index("c").reshape(1)
    part = core * 16 + lax.axis_index(yx)
    lane_perm = jnp.asarray(permutation(4, 16, 6), bf16)
    row_perm = jnp.asarray(permutation(8, 16, 6), bf16)
    gain_row = norm_gain.reshape(1, CHANNELS)

    activated, cot_perm, up, down = make_norm(tokens, gain_row, cotangent, row_perm)
    before = lax.ppermute(up, "z", [(i, i + 1) for i in range(15)])
    after = lax.ppermute(down, "z", [(i + 1, i) for i in range(15)])

    piece = make_piece(part, dilated_weight.transpose(0, 2, 1), output_weight.T, lane_perm)
    from_z = lax.all_to_all(piece, "z", 0, 0)
    from_z, before, after = lax.optimization_barrier((from_z, before, after))
    mine = lax.all_to_all(make_stack(from_z), yx, 0, 0)
    other = lax.ppermute(mine, "c", swap)

    keep, send, sum_cot, hidden = make_main(core, mine, other, activated, cot_perm, before, after)
    received = lax.ppermute(send, "c", swap)
    plane = lax.all_to_all(make_pair(keep, received), yx, 0, 0)
    residual_output, token_cotangent, gain_rows = make_tail(
        core, mine, other, sum_cot, hidden, tokens, gain_row, cotangent, row_perm
    )
    column = lax.all_to_all(make_plane(plane, gain_rows), "z", 0, 0)
    spread = lax.all_to_all(make_column(column), ("c", "y", "x"), 0, 0)
    taps, proj, gain = make_final(spread, lane_perm)
    return residual_output, token_cotangent, taps.transpose(0, 2, 1), proj.T, gain[0, :48]


def solution(mesh):
    fine = Mesh(mesh.devices.reshape(4, 4, 2, 16), ("y", "x", "c", "z"))
    dp = ("y", "x", "c")
    rows = P(dp, "z", None)
    in_specs = (rows, P(), P(None, None, "z"), P(None, "z"), rows)
    out_specs = (rows, rows, P(None, None, "z"), P(None, "z"), P("z"))
    return jax.shard_map(on_device, mesh=fine, in_specs=in_specs, out_specs=out_specs, check_vma=False)
```

time: 177 us -> 154 us (0.87)
  blocking collectives: 27.4 us -> 82.4 us
  waiting for transfers between devices: 53.4 us -> 12.9 us
  matrix products: 22.7 us -> 0 us
  starting transfers between devices: 40.5 us -> 18.3 us
  Pallas kernels: 0 us -> 20.9 us
  other arithmetic: 11.9 us -> 0 us
    all_to_all x1 -> x4, blocking collectives: 27.4 us -> 82.4 us  [the longest x1 28.2 us: on_device(): from_z = lax.all_to_all(piece, 'z', 0, 0)]
    all_to_all x4 -> x1, waiting for transfers between devices: 41.7 us -> 8.01 us  [on_device(): plane = lax.all_to_all(make_pair(keep, received), yx, 0, 0)]
    dot_general x15 -> x0, matrix products: 22.7 us -> none  [the longest x3 6.46 us: on_device(): jnp.einsum('snh,hc->snc', sum_cot[:, (2 - k) * D:(2 - k) * D + bins], tap...]
    all_to_all x4 -> x1, starting transfers between devices: 26 us -> 4.51 us  [on_device(): plane = lax.all_to_all(make_pair(keep, received), yx, 0, 0)]
    pallas_call x0 -> x9, Pallas kernels: none -> 20.9 us  [the longest x1 7.25 us: make_main(): call(main_kernel, [HALF, HALF, shape(sum_cot, bf16), shape(hidden, bf16)]...]
    unnamed x51 -> x56, local copies, waits for them, and re-layouts: 3.8 us -> 16.3 us
    ppermute x4, waiting for transfers between devices: 11.7 us -> 4.91 us  [the longest x1 2.45 us: on_device(): other = lax.ppermute(mine, 'c', swap)]
    convert_element_type x5 -> x0, other arithmetic: 6 us -> none  [the longest x1 2.69 us: on_device(): chip = (keep.astype(f32) + received.astype(f32)).astype(bf16)]
  transfers between devices with their start and end apart: 8 -> 5, of which waited for: 6 -> 3; matrix products, arithmetic and copies ran while one was open for 11% -> 0% of each run, Pallas kernels for 0% -> 4%
where the time goes in v3:
time: 154 us; the launch traced here: 153 us
  blocking collectives  82.4 us (54%)
  Pallas kernels  20.9 us (14%)
  starting transfers between devices  18.3 us (12%)
  local copies, waits for them, and re-layouts  17.5 us (11%)
  waiting for transfers between devices  12.9 us (8%)
    all_to_all x1, blocking collectives, on_device(): from_z = lax.all_to_all(piece, 'z', 0, 0)  28.2 us
    all_to_all x1, blocking collectives, on_device(): mine = lax.all_to_all(make_stack(from_z), yx, 0, 0)  22.4 us
    all_to_all x1, blocking collectives, on_device(): column = lax.all_to_all(make_plane(plane, gain_rows), 'z', 0, 0)  17.1 us
    unnamed x56, local copies, waits for them, and re-layouts  16.3 us
    all_to_all x1, blocking collectives, on_device(): spread = lax.all_to_all(make_column(column), ('c', 'y', 'x'), 0, 0)  14.7 us
    all_to_all x1, waiting for transfers between devices, on_device(): plane = lax.all_to_all(make_pair(keep, received), yx, 0, 0)  8.01 us
    pallas_call x1, Pallas kernels, make_main(): call(main_kernel, [HALF, HALF, shape(sum_cot, bf16), shape(hidden, bf16)]...  7.25 us
    pallas_call x1, Pallas kernels, make_tail(): call(tail_kernel, [ROWS, ROWS, shape((16, 384), f32)], [SMEM, HBM, HBM] +...  6.3 us
  transfers between devices with their start and end apart: 5, of which 3 were waited for; matrix products, arithmetic and copies ran while one was open for 0% of the time, Pallas kernels for 4%

profile of v3, /device:TPU:1, one launch (start us, length us, event | category | flops | bytes accessed | tf_op | source)
XLA Modules:
  0.0 152.8 jit_solution(7272888213856424502)
XLA Ops:
  0.6 0.7 reshape.17.gain
  1.3 1.3 copy-done.2
  2.6 1.1 copy-done.6
  3.7 1.1 copy-done.8
  4.9 1.4 norm.1
  6.3 0.0 copy-start.12
  6.3 0.9 copy-done.12
  7.1 0.9 copy-done.14
  8.0 4.4 %collective-permute-start = (bf16[2,192,768]{2,1,0:T(8,128)(2,1)S(1)}, bf16[2,192,768]{2,1,0:T(8,128)(2,1)S(1)}, u32[]{:S(2)}, u32[]{:S(2)}) collective-permute-start(bf16[2,192,768]{2,1,0:T(8,128)(2,1)S(1)} %get-tuple-element.22), channel_id=1, source_target_pairs={{0,1},{1,2},{2,3},{3,4},{4,5},{5,6},{6,7},{7,8},{8,9},{9,10},{10,1... | collective-permute-start | bytes 1769480 | tf_op jit(solution)/shard_map/ppermute | solution.py:361
  12.4 1.3 collective-permute-start.1
  13.8 0.2 piece.1
  14.0 28.2 %all_to_all.25.given = bf16[16,8,384]{2,1,0:T(8,128)(2,1)S(1)} all-to-all(bf16[16,8,384]{2,1,0:T(8,128)(2,1)S(1)} %piece.1), channel_id=1, replica_groups=mesh['y'=4,'x'=4,'c'=2,'z'=16] {'z'}, dimensions={0} | all-to-all | bytes 196608 | tf_op jit(solution)/shard_map/all_to_all | solution.py:365
  42.2 0.0 collective-permute-done.before
  42.2 0.8 copy-done.18
  43.0 0.0 collective-permute-done.1.after
  43.0 0.8 copy-done.20
  43.9 1.7 %stack.1 = bf16[16,96,384]{2,1,0:T(8,128)(2,1)S(1)} custom-call(bf16[16,8,384]{2,1,0:T(8,128)(2,1)S(1)} %all_to_all.25.given), custom_call_target="tpu_custom_call" | custom-call | tf_op jit(solution)/shard_map/stack/pallas_call | solution.py:270
  45.6 0.0 copy-start.13
  45.6 0.0 copy-start.15
  45.6 22.4 %all_to_all.26.mine = bf16[16,96,384]{2,1,0:T(8,128)(2,1)S(1)} all-to-all(bf16[16,96,384]{2,1,0:T(8,128)(2,1)S(1)} %stack.1), channel_id=1, replica_groups=mesh['y'=4,'x'=4,'c'=2,'z'=16] {'y','x'}, dimensions={0} | all-to-all | bytes 2359296 | tf_op jit(solution)/shard_map/all_to_all | solution.py:367
  68.0 5.8 %collective-permute-start.2 = (bf16[16,96,384]{2,1,0:T(8,128)(2,1)S(1)}, bf16[16,96,384]{2,1,0:T(8,128)(2,1)S(1)}, u32[]{:S(2)}, u32[]{:S(2)}) collective-permute-start(bf16[16,96,384]{2,1,0:T(8,128)(2,1)S(1)} %all_to_all.26.mine), channel_id=1, source_target_pairs={{0,16},{16,0},{1,17},{17,1},{2,18},{18,2},{3,19},{19,3},{4,20},{20... | collective-permute-start | bytes 3538952 | tf_op jit(solution)/shard_map/ppermute | solution.py:368
  73.8 2.5 %collective-permute-done.2.other = bf16[16,96,384]{2,1,0:T(8,128)(2,1)S(1)} collective-permute-done((bf16[16,96,384]{2,1,0:T(8,128)(2,1)S(1)}, bf16[16,96,384]{2,1,0:T(8,128)(2,1)S(1)}, u32[]{:S(2)}, u32[]{:S(2)}) %collective-permute-start.2) | collective-permute-done | bytes 1179680 | tf_op jit(solution)/shard_map/ppermute | solution.py:368
  76.3 1.0 copy-done.4
  77.3 1.1 copy-done.21
  78.3 7.2 %main.1 = (bf16[16,96,384]{2,1,0:T(8,128)(2,1)S(1)}, bf16[16,96,384]{2,1,0:T(8,128)(2,1)S(1)}, bf16[2,384,384]{2,1,0:T(8,128)(2,1)S(1)}, bf16[2,256,384]{2,1,0:T(8,128)(2,1)S(1)}) custom-call(s32[1]{0:T(128)} %bitcast.core, bf16[16,96,384]{2,1,0:T(8,128)(2,1)} %copy-done, bf16[16,96,384]{2,1,0:T(8,128)(2,1)} %copy-done.4, ...), custom_call_target="tpu_custom_call" | custom-call | tf_op jit(solution)/shard_map/main/pallas_call | solution.py:295
  85.6 0.0 copy-start.16
  85.6 0.8 copy-done.16
  86.4 0.7 copy-done.22
  87.2 2.3 %collective-permute-start.3 = (bf16[16,96,384]{2,1,0:T(8,128)(2,1)S(1)}, bf16[16,96,384]{2,1,0:T(8,128)(2,1)S(1)}, u32[]{:S(2)}, u32[]{:S(2)}) collective-permute-start(bf16[16,96,384]{2,1,0:T(8,128)(2,1)S(1)} %get-tuple-element.34), channel_id=1, source_target_pairs={{0,16},{16,0},{1,17},{17,1},{2,18},{18,2},{3,19},{19,3},{4,20},{20... | collective-permute-start | bytes 3538952 | tf_op jit(solution)/shard_map/ppermute | solution.py:371
  89.4 2.5 %collective-permute-done.3.b = bf16[16,96,384]{2,1,0:T(8,128)(2,1)S(1)} collective-permute-done((bf16[16,96,384]{2,1,0:T(8,128)(2,1)S(1)}, bf16[16,96,384]{2,1,0:T(8,128)(2,1)S(1)}, u32[]{:S(2)}, u32[]{:S(2)}) %collective-permute-start.3) | collective-permute-done | bytes 1179680 | tf_op jit(solution)/shard_map/ppermute | solution.py:371
  91.9 1.7 %pair.1 = bf16[16,96,384]{2,1,0:T(8,128)(2,1)} custom-call(bf16[16,96,384]{2,1,0:T(8,128)(2,1)S(1)} %get-tuple-element.33.a, bf16[16,96,384]{2,1,0:T(8,128)(2,1)S(1)} %collective-permute-done.3.b), custom_call_target="tpu_custom_call" | custom-call | tf_op jit(solution)/shard_map/pair/pallas_call | solution.py:316
  93.6 4.5 %all-to-all-start.2 = ((bf16[16,96,384]{2,1,0:T(8,128)(2,1)}), bf16[16,96,384]{2,1,0:T(8,128)(2,1)}, u32[]{:S(2)}, u32[]{:S(2)}) async-start(bf16[16,96,384]{2,1,0:T(8,128)(2,1)} %pair.1), calls=%async_computation.2 | async-start | bytes 2359296 | tf_op jit(solution)/shard_map/all_to_all | solution.py:372
  98.1 0.0 copy-start.7
  98.2 1.1 copy-done.7
  99.3 1.1 copy-done.9
  100.4 1.1 copy-done.17
  101.5 1.0 copy-done.23
  102.5 6.3 %tail.1 = (bf16[2,256,768]{2,1,0:T(8,128)(2,1)}, bf16[2,256,768]{2,1,0:T(8,128)(2,1)}, f32[16,384]{1,0:T(8,128)S(1)}) custom-call(s32[1]{0:T(128)} %bitcast.core, bf16[16,96,384]{2,1,0:T(8,128)(2,1)S(1)} %copy-done.1, bf16[16,96,384]{2,1,0:T(8,128)(2,1)S(1)} %copy-done.5, bf16[2,384,384]{2,1,0:T(8,128)(2,1)S(1)} %copy-done.17, ...), custom_call_target="tpu_custom_call" | custom-call | tf_op jit(solution)/shard_map/tail/pallas_call | solution.py:320
  108.8 0.0 copy-start.26
  108.8 0.6 copy-done.26
  109.4 8.0 %all-to-all-done.2.given = bf16[16,96,384]{2,1,0:T(8,128)(2,1)} async-done(((bf16[16,96,384]{2,1,0:T(8,128)(2,1)}), bf16[16,96,384]{2,1,0:T(8,128)(2,1)}, u32[]{:S(2)}, u32[]{:S(2)}) %all-to-all-start.2) | async-done | bytes 1179680 | tf_op jit(solution)/shard_map/all_to_all | solution.py:372
  117.4 0.7 copy-done.27
  118.1 1.5 plane.1
  119.6 17.1 %all_to_all.27.given = bf16[16,8,384]{2,1,0:T(8,128)(2,1)S(1)} all-to-all(bf16[16,8,384]{2,1,0:T(8,128)(2,1)S(1)} %plane.1), channel_id=1, replica_groups=mesh['y'=4,'x'=4,'c'=2,'z'=16] {'z'}, dimensions={0} | all-to-all | bytes 196608 | tf_op jit(solution)/shard_map/all_to_all | solution.py:376
  136.8 14.7 %all_to_all.28.given = bf16[32,8,384]{2,1,0:T(8,128)(2,1)S(1)} all-to-all(bf16[32,8,384]{2,1,0:T(8,128)(2,1)S(1)} %column.1), channel_id=1, replica_groups=mesh['y'=4,'x'=4,'c'=2,'z'=16] {'c','y','x'}, dimensions={0} | all-to-all | bytes 393216 | tf_op jit(solution)/shard_map/all_to_all | solution.py:377
  151.4 0.0 copy-done.11
  151.4 0.9 final.1
  152.3 0.5 slice_bitcast_fusion
  (33 shorter events, 0.1 us)
Async XLA Ops:
  1.3 1.3 copy-start.2
  2.6 1.1 copy-start.6
  3.7 1.1 copy-start.8
  4.9 8.9 %copy-start.10 = (bf16[384,384]{1,0:T(8,128)(2,1)S(1)}, bf16[384,384]{1,0:T(8,128)(2,1)}, u32[]{:S(2)}) copy-start(bf16[384,384]{1,0:T(8,128)(2,1)} %constant.24.clone.perm) | copy-start | bytes 884740
  4.9 8.9 %copy-start.24 = (bf16[3,768,24]{1,2,0:T(8,128)(2,1)S(1)}, bf16[3,768,24]{1,2,0:T(8,128)(2,1)}, u32[]{:S(2)}) copy-start(bf16[3,768,24]{1,2,0:T(8,128)(2,1)} %param.9) | copy-start | bytes 331780
  4.9 8.9 %copy-start.25 = (bf16[384,48]{0,1:T(8,128)(2,1)S(1)}, bf16[384,48]{0,1:T(8,128)(2,1)}, u32[]{:S(2)}) copy-start(bf16[384,48]{0,1:T(8,128)(2,1)} %param.10) | copy-start | bytes 110596
  6.3 0.9 copy-start.12
  7.1 0.9 copy-start.14
  8.0 34.2 %collective-permute-start = (bf16[2,192,768]{2,1,0:T(8,128)(2,1)S(1)}, bf16[2,192,768]{2,1,0:T(8,128)(2,1)S(1)}, u32[]{:S(2)}, u32[]{:S(2)}) collective-permute-start(bf16[2,192,768]{2,1,0:T(8,128)(2,1)S(1)} %get-tuple-element.22), channel_id=1, source_target_pairs={{0,1},{1,2},{2,3},{3,4},{4,5},{5,6},{6,7},{7,8},{8,9},{9,10},{10,1... | collective-permute-start | bytes 1769480 | tf_op jit(solution)/shard_map/ppermute | solution.py:361
  12.4 30.6 %collective-permute-start.1 = (bf16[2,192,768]{2,1,0:T(8,128)(2,1)S(1)}, bf16[2,192,768]{2,1,0:T(8,128)(2,1)S(1)}, u32[]{:S(2)}, u32[]{:S(2)}) collective-permute-start(bf16[2,192,768]{2,1,0:T(8,128)(2,1)S(1)} %get-tuple-element.23), channel_id=1, source_target_pairs={{1,0},{2,1},{3,2},{4,3},{5,4},{6,5},{7,6},{8,7},{9,8},{10,9},{11,1... | collective-permute-start | bytes 1769480 | tf_op jit(solution)/shard_map/ppermute | solution.py:362
  42.2 0.8 copy-start.18
  43.0 0.8 copy-start.20
  45.6 31.7 %copy-start.13 = (bf16[2,256,768]{2,1,0:T(8,128)(2,1)S(1)}, bf16[2,256,768]{2,1,0:T(8,128)(2,1)}, u32[]{:S(2)}) copy-start(bf16[2,256,768]{2,1,0:T(8,128)(2,1)} %copy-done.12) | copy-start | bytes 2359300
  45.6 31.7 %copy-start.15 = (bf16[2,256,768]{2,1,0:T(8,128)(2,1)S(1)}, bf16[2,256,768]{2,1,0:T(8,128)(2,1)}, u32[]{:S(2)}) copy-start(bf16[2,256,768]{2,1,0:T(8,128)(2,1)} %copy-done.14) | copy-start | bytes 2359300
  45.6 31.7 %copy-start.19 = (bf16[2,192,768]{2,1,0:T(8,128)(2,1)S(1)}, bf16[2,192,768]{2,1,0:T(8,128)(2,1)}, u32[]{:S(2)}) copy-start(bf16[2,192,768]{2,1,0:T(8,128)(2,1)} %copy-done.18) | copy-start | bytes 1769476
  68.0 8.3 %copy-start = (bf16[16,96,384]{2,1,0:T(8,128)(2,1)}, bf16[16,96,384]{2,1,0:T(8,128)(2,1)S(1)}, u32[]{:S(2)}) copy-start(bf16[16,96,384]{2,1,0:T(8,128)(2,1)S(1)} %all_to_all.26.mine) | copy-start | bytes 3538948
  68.0 8.3 %collective-permute-start.2 = (bf16[16,96,384]{2,1,0:T(8,128)(2,1)S(1)}, bf16[16,96,384]{2,1,0:T(8,128)(2,1)S(1)}, u32[]{:S(2)}, u32[]{:S(2)}) collective-permute-start(bf16[16,96,384]{2,1,0:T(8,128)(2,1)S(1)} %all_to_all.26.mine), channel_id=1, source_target_pairs={{0,16},{16,0},{1,17},{17,1},{2,18},{18,2},{3,19},{19,3},{4,20},{20... | collective-permute-start | bytes 3538952 | tf_op jit(solution)/shard_map/ppermute | solution.py:368
  76.3 1.0 copy-start.4
  77.3 1.1 copy-start.21
  85.6 0.8 copy-start.16
  86.4 0.7 copy-start.22
  87.2 4.7 %collective-permute-start.3 = (bf16[16,96,384]{2,1,0:T(8,128)(2,1)S(1)}, bf16[16,96,384]{2,1,0:T(8,128)(2,1)S(1)}, u32[]{:S(2)}, u32[]{:S(2)}) collective-permute-start(bf16[16,96,384]{2,1,0:T(8,128)(2,1)S(1)} %get-tuple-element.34), channel_id=1, source_target_pairs={{0,16},{16,0},{1,17},{17,1},{2,18},{18,2},{3,19},{19,3},{4,20},{20... | collective-permute-start | bytes 3538952 | tf_op jit(solution)/shard_map/ppermute | solution.py:371
  91.9 6.2 %copy-start.5 = (bf16[16,96,384]{2,1,0:T(8,128)(2,1)S(1)}, bf16[16,96,384]{2,1,0:T(8,128)(2,1)}, u32[]{:S(2)}) copy-start(bf16[16,96,384]{2,1,0:T(8,128)(2,1)} %copy-done.4) | copy-start | bytes 3538948
  93.6 4.5 %copy-start.1 = (bf16[16,96,384]{2,1,0:T(8,128)(2,1)S(1)}, bf16[16,96,384]{2,1,0:T(8,128)(2,1)}, u32[]{:S(2)}) copy-start(bf16[16,96,384]{2,1,0:T(8,128)(2,1)} %copy-done) | copy-start | bytes 3538948
  93.6 4.5 %copy-start.3 = (bf16[768,768]{1,0:T(8,128)(2,1)S(1)}, bf16[768,768]{1,0:T(8,128)(2,1)}, u32[]{:S(2)}) copy-start(bf16[768,768]{1,0:T(8,128)(2,1)} %constant.25.clone.perm) | copy-start | bytes 3538948
  93.6 23.8 %all-to-all-start.2 = ((bf16[16,96,384]{2,1,0:T(8,128)(2,1)}), bf16[16,96,384]{2,1,0:T(8,128)(2,1)}, u32[]{:S(2)}, u32[]{:S(2)}) async-start(bf16[16,96,384]{2,1,0:T(8,128)(2,1)} %pair.1), calls=%async_computation.2 | async-start | bytes 2359296 | tf_op jit(solution)/shard_map/all_to_all | solution.py:372
  98.1 1.1 copy-start.7
  99.3 1.1 copy-start.9
  100.4 1.1 copy-start.17
  101.5 1.0 copy-start.23
  108.8 0.6 copy-start.26
  109.4 42.1 %copy-start.11 = (bf16[384,384]{1,0:T(8,128)(2,1)S(1)}, bf16[384,384]{1,0:T(8,128)(2,1)}, u32[]{:S(2)}) copy-start(bf16[384,384]{1,0:T(8,128)(2,1)} %constant.24.clone.perm) | copy-start | bytes 884740
  117.4 0.7 copy-start.27

commit v4 on v3

v4 whole, which is shorter than its diff:
```python
import jax
import jax.numpy as jnp
import numpy as np
from jax import lax
from jax.experimental import pallas as pl
from jax.experimental.pallas import tpu as pltpu
from jax.sharding import Mesh, PartitionSpec as P

STEP = 64
SEQS = 2
BINS = 256
CHANNELS = 768
HIDDEN = 384
EXT = BINS + 2 * STEP
gelu_scale = 0.7978845608
cubic_term = 0.044715
epsilon = 1e-06
bf16 = jnp.bfloat16
f32 = jnp.float32
HBM = pl.BlockSpec(memory_space=pl.ANY)
SMEM = pl.BlockSpec(memory_space=pltpu.SMEM)
VMEM = pl.BlockSpec(memory_space=pltpu.VMEM)
FAR = pl.BlockSpec(memory_space=pltpu.HBM)
MB = 1024 * 1024


def permutation(outer, inner, width):
    size = outer * inner * width
    order = np.arange(size).reshape(inner, outer, width).transpose(1, 0, 2).reshape(-1)
    matrix = np.zeros((size, size), np.float32)
    matrix[order, np.arange(size)] = 1.0
    return matrix


def dot(a, b, ca, cb):
    return lax.dot_general(a, b, (((ca,), (cb,)), ((), ())), preferred_element_type=f32)


def tanh_of(v):
    return jnp.tanh(gelu_scale * (v + cubic_term * v * v * v))


def activate(v, t):
    return 0.5 * v * (1.0 + t)


def derivative(v, t):
    return 0.5 * (1.0 + t) + 0.5 * v * (1.0 - t * t) * gelu_scale * (1.0 + 3.0 * cubic_term * v * v)


def inverse_rms_of(v):
    return lax.rsqrt(jnp.mean(v * v, axis=-1, keepdims=True) + epsilon)


def piece_kernel(part, taps, proj, perm, out, pieces):
    for k in range(3):
        tap = taps[k].astype(f32)
        for q in range(4):
            for half in range(2):
                pieces[(q * 3 + k) * 2 + half, 0:6] = tap[6 * q : 6 * q + 6, half * 384 : half * 384 + 384]
    rows = dot(proj[...], perm[...], 1, 0)
    for u in range(8):
        pieces[24 + u, 0:6] = rows[6 * u : 6 * u + 6]
    pieces[:, 6:8] = jnp.zeros((32, 2, 384), f32)
    own = pieces[part[0]].astype(bf16)
    for z in range(16):
        out[z] = own


def stack_kernel(given, out, rows):
    for z in range(16):
        rows[6 * z : 6 * z + 6] = given[z].astype(f32)[0:6]
    packed = rows[...].astype(bf16)
    for i in range(16):
        out[i] = packed


def run(pairs, sems):
    copies = [pltpu.make_async_copy(a, b, sems.at[i]) for i, (a, b) in enumerate(pairs)]
    for c in copies:
        c.start()
    return copies


def norm_kernel(tokens, gain_in, cot, up, down, rows, gain, sems):
    loads = [(tokens.at[s], rows.at[s]) for s in range(SEQS)]
    loads += [
        (gain_in, gain),
        (cot.at[:, BINS - STEP :], up.at[:, 2 * STEP :]),
        (cot.at[:, 0:STEP], down.at[:, 2 * STEP :]),
    ]
    loads = run(loads, sems)
    loads[SEQS].wait()
    gain_row = gain[...].reshape(1, CHANNELS)
    for s in range(SEQS):
        loads[s].wait()
        v = rows[s].astype(f32)
        normed = v * inverse_rms_of(v) * gain_row
        a = activate(normed, tanh_of(normed)).astype(bf16)
        up[s, 0 : 2 * STEP] = a[BINS - 2 * STEP :]
        down[s, 0 : 2 * STEP] = a[: 2 * STEP]
    for c in loads[SEQS + 1 :]:
        c.wait()


def ready_kernel(
    tokens, gain, cot, perm, up, down, before, after,
    act, cot_perm, slope,
    rows, cots, matrix, sems,
):
    loads = [(cot, cots), (perm, matrix), (tokens, rows)]
    loads = run(loads, sems)
    half = 2 * STEP
    act[:, 0:half] = before[:, 0:half]
    act[:, half : 2 * half] = down[:, 0:half]
    act[:, 2 * half : 3 * half] = up[:, 0:half]
    act[:, 3 * half :] = after[:, 0:half]
    for c in loads:
        c.wait()
    order = matrix[...]
    gain_row = gain[...].reshape(1, CHANNELS)
    for s in range(SEQS):
        cot_perm[s, STEP : STEP + BINS] = dot(cots[s], order, 1, 0).astype(bf16)
        edges = dot(jnp.concatenate([before[s, half:], after[s, half:]]), order, 1, 0).astype(bf16)
        cot_perm[s, 0:STEP] = edges[0:STEP]
        cot_perm[s, STEP + BINS :] = edges[STEP:]
        v = rows[s].astype(f32)
        normed = v * inverse_rms_of(v) * gain_row
        slope[s] = derivative(normed, tanh_of(normed))


def weight_copies(core, mine, other, taps, proj, sems, act):
    for here in range(2):

        @pl.when(core[0] == here)
        def _(here=here):
            for p in range(32):
                source = (mine if p // 16 == here else other).at[p % 16]
                if p < 24:
                    q, k, half = p // 6, p % 6 // 2, p % 2
                    target = taps.at[k, 96 * q : 96 * q + 96, 384 * half : 384 * half + 384]
                else:
                    target = proj.at[96 * (p - 24) : 96 * (p - 24) + 96]
                copy = pltpu.make_async_copy(source, target, sems.at[p])
                copy.start() if act else copy.wait()


def main_kernel(
    core, mine, other, act, cot,
    keep, send, sum_cot, hidden, taps, proj,
    grad, wsems, sems,
):
    own = BINS
    weight_copies(core, mine, other, taps, proj, wsems, True)
    weight_copies(core, mine, other, taps, proj, wsems, False)
    for s in range(SEQS):
        total = dot(act[s, 0:EXT], taps[0], 1, 1)
        total += dot(act[s, STEP : STEP + EXT], taps[1], 1, 1)
        total += dot(act[s, 2 * STEP : 2 * STEP + EXT], taps[2], 1, 1)
        hidden_cot = dot(cot[s], proj[...], 1, 0).astype(bf16).astype(f32)
        t = tanh_of(total)
        hidden[s] = activate(total, t)[STEP : STEP + own].astype(bf16)
        sum_cot[s] = (hidden_cot * derivative(total, t)).astype(bf16)
    centre = jnp.concatenate([sum_cot[s, STEP : STEP + own] for s in range(SEQS)])
    for k in range(3):
        rows = jnp.concatenate([act[s, STEP * (k + 1) : STEP * (k + 1) + own] for s in range(SEQS)])
        g = dot(centre, rows, 0, 0).astype(bf16)
        for q in range(4):
            for half in range(2):
                grad[(q * 3 + k) * 2 + half] = g[96 * q : 96 * q + 96, 384 * half : 384 * half + 384]
    rows = jnp.concatenate([cot[s, STEP : STEP + own] for s in range(SEQS)])
    g = dot(rows, jnp.concatenate([hidden[s] for s in range(SEQS)]), 0, 0).astype(bf16)
    for u in range(8):
        grad[24 + u] = g[96 * u : 96 * u + 96]
    saves = [
        (grad.at[pl.ds(16 * core[0], 16)], keep),
        (grad.at[pl.ds(16 - 16 * core[0], 16)], send),
    ]
    for c in run(saves, sems):
        c.wait()


def pair_kernel(a, b, out):
    out[...] = (a[...].astype(f32) + b[...].astype(f32)).astype(bf16)


def tail_kernel(
    taps, proj, sum_cot, hidden, slope, tokens, gain, cot, perm,
    block_output, token_gradient, gain_rows,
    rows, cots, matrix, result, sems, out_sems,
):
    loads = run([(tokens, rows), (cot, cots), (perm, matrix)], sems)
    for c in loads:
        c.wait()
    natural = dot(matrix[...], proj[...], 1, 0).astype(bf16)
    gain_row = gain[...].reshape(1, CHANNELS)
    gain_sum = jnp.zeros((1, CHANNELS), f32)
    saves = []
    for s in range(SEQS):
        v = rows[s].astype(f32)
        result[0, s] = (v + dot(hidden[s], natural, 1, 1)).astype(bf16)
        total = dot(sum_cot[s, 2 * STEP : 2 * STEP + BINS], taps[0], 1, 0)
        total += dot(sum_cot[s, STEP : STEP + BINS], taps[1], 1, 0)
        total += dot(sum_cot[s, 0:BINS], taps[2], 1, 0)
        inverse_rms = inverse_rms_of(v)
        normed_cot = total.astype(bf16).astype(f32) * slope[s]
        scaled_cot = gain_row * normed_cot
        mean = jnp.mean(scaled_cot * v, axis=-1, keepdims=True)
        result[1, s] = (
            cots[s].astype(f32) + inverse_rms * scaled_cot - v * (inverse_rms * inverse_rms * inverse_rms) * mean
        ).astype(bf16)
        saves += [
            pltpu.make_async_copy(result.at[0, s], block_output.at[s], out_sems.at[2 * s]),
            pltpu.make_async_copy(result.at[1, s], token_gradient.at[s], out_sems.at[2 * s + 1]),
        ]
        saves[-2].start()
        saves[-1].start()
        gain_sum += jnp.sum(normed_cot * v * inverse_rms, axis=0, keepdims=True)
    gain_rows[...] = jnp.zeros((16, 384), f32)
    for z in range(16):
        gain_rows[z : z + 1, 0:48] = gain_sum[:, 48 * z : 48 * z + 48]
    for c in saves:
        c.wait()


def split_high_low(v):
    high = v.astype(bf16).astype(f32)
    return high, v - high


def plane_kernel(given, gain_rows, out, rows):
    total = given[0].astype(f32)
    for i in range(1, 16):
        total += given[i].astype(f32)
    rows[...] = total
    for z in range(16):
        high, low = split_high_low(gain_rows[z : z + 1])
        out[z] = jnp.concatenate([rows[6 * z : 6 * z + 6], high, low]).astype(bf16)


def column_kernel(given, out):
    total = given[0].astype(f32)
    for z in range(1, 16):
        total += given[z].astype(f32)
    high, low = split_high_low(total[6:7] + total[7:8])
    block = jnp.concatenate([total[0:6], high, low]).astype(bf16)
    for i in range(32):
        out[i] = block


def final_kernel(given, perm, taps, proj, gain, rows):
    scale = 1.0 / 64
    for q in range(4):
        for k in range(3):
            for half in range(2):
                block = given[(q * 3 + k) * 2 + half].astype(f32)
                taps[k, 6 * q : 6 * q + 6, 384 * half : 384 * half + 384] = block[0:6] * scale
    for u in range(8):
        rows[6 * u : 6 * u + 6] = given[24 + u].astype(f32)[0:6]
    proj[...] = dot(rows[...].astype(bf16), perm[...], 1, 1) * scale
    total = given[0].astype(f32)
    for i in range(1, 32):
        total += given[i].astype(f32)
    gain[...] = ((total[6:7] + total[7:8])[:, 0:48] * scale).reshape(48)


def call(kernel, out, ins, outs, name, room, scratch=(), **more):
    return pl.pallas_call(
        kernel,
        out_shape=out,
        in_specs=ins,
        out_specs=outs,
        scratch_shapes=scratch,
        compiler_params=pltpu.CompilerParams(vmem_limit_bytes=room * MB),
        name=name,
        **more,
    )


def shape(dims, kind):
    return jax.ShapeDtypeStruct(dims, kind)


HALF = shape((16, 96, 384), bf16)
ROWS = shape((SEQS, BINS, CHANNELS), bf16)
LOCAL = pltpu.VMEM((SEQS, BINS, CHANNELS), bf16)
MATRIX = pltpu.VMEM((CHANNELS, CHANNELS), bf16)


def waits(count):
    return pltpu.SemaphoreType.DMA((count,))


def make_piece(part, taps, proj, perm):
    return call(
        piece_kernel, shape((16, 8, 384), bf16), [SMEM] + [VMEM] * 3, VMEM, "piece", 6, [pltpu.VMEM((32, 8, 384), f32)]
    )(part, taps, proj, perm)


def make_stack(given):
    return call(stack_kernel, HALF, [VMEM], VMEM, "stack", 6, [pltpu.VMEM((96, 384), f32)])(given)


def make_norm(tokens, gain, cot):
    edge = shape((SEQS, 3 * STEP, CHANNELS), bf16)
    return call(norm_kernel, [edge, edge], [FAR] * 3, [VMEM] * 2, "norm", 12, [LOCAL, pltpu.VMEM((CHANNELS,), f32), waits(5)])(
        tokens, gain, cot
    )


def make_ready(tokens, gain, cot, perm, up, down, before, after):
    return call(
        ready_kernel,
        [
            shape((SEQS, BINS + 4 * STEP, CHANNELS), bf16),
            shape((SEQS, EXT, CHANNELS), bf16),
            shape((SEQS, BINS, CHANNELS), f32),
        ],
        [FAR, VMEM, FAR, FAR] + [VMEM] * 4,
        [VMEM] * 3,
        "ready",
        20,
        [LOCAL, LOCAL, MATRIX, waits(3)],
    )(tokens, gain, cot, perm, up, down, before, after)


def make_main(core, mine, other, act, cot):
    return call(
        main_kernel,
        [
            HALF,
            HALF,
            shape((SEQS, EXT, HIDDEN), bf16),
            shape((SEQS, BINS, HIDDEN), bf16),
            shape((3, HIDDEN, CHANNELS), bf16),
            shape((CHANNELS, HIDDEN), bf16),
        ],
        [SMEM, HBM, HBM, VMEM, VMEM],
        [HBM] * 2 + [VMEM] * 4,
        "main",
        24,
        [pltpu.VMEM((32, 96, 384), bf16), waits(32), waits(2)],
    )(core, mine, other, act, cot)


def make_pair(a, b):
    return call(pair_kernel, HALF, [VMEM] * 2, VMEM, "pair", 8)(a, b)


def make_tail(taps, proj, sum_cot, hidden, slope, tokens, gain, cot, perm):
    return call(
        tail_kernel,
        [ROWS, ROWS, shape((16, 384), f32)],
        [VMEM] * 5 + [FAR, VMEM, FAR, FAR],
        [FAR, FAR, VMEM],
        "tail",
        24,
        [LOCAL, LOCAL, MATRIX, pltpu.VMEM((2, SEQS, BINS, CHANNELS), bf16), waits(3), waits(4)],
    )(taps, proj, sum_cot, hidden, slope, tokens, gain, cot, perm)


def make_plane(given, gain_rows):
    return call(
        plane_kernel, shape((16, 8, 384), bf16), [VMEM] * 2, VMEM, "plane", 6, [pltpu.VMEM((96, 384), f32)]
    )(given, gain_rows)


def make_column(given):
    return call(column_kernel, shape((32, 8, 384), bf16), [VMEM], VMEM, "column", 6)(given)


def make_final(given, perm):
    return call(
        final_kernel,
        [shape((3, 24, CHANNELS), f32), shape((48, 384), f32), shape((48,), f32)],
        [VMEM] * 2,
        [VMEM] * 3,
        "final",
        6,
        [pltpu.VMEM((48, 384), f32)],
    )(given, perm)


def on_device(tokens, norm_gain, dilated_weight, output_weight, cotangent):
    yx = ("y", "x")
    swap = [(0, 1), (1, 0)]
    core = lax.axis_index("c").reshape(1)
    part = core * 16 + lax.axis_index(yx)
    lane_perm = jnp.asarray(permutation(4, 16, 6), bf16)
    row_perm = jnp.asarray(permutation(8, 16, 6), bf16)

    tokens = pltpu.with_memory_space_constraint(tokens, pltpu.HBM)
    cotangent = pltpu.with_memory_space_constraint(cotangent, pltpu.HBM)
    up, down = make_norm(tokens, pltpu.with_memory_space_constraint(norm_gain, pltpu.HBM), cotangent)
    before = lax.ppermute(up, "z", [(i, i + 1) for i in range(15)])
    after = lax.ppermute(down, "z", [(i + 1, i) for i in range(15)])

    piece = make_piece(part, dilated_weight.transpose(0, 2, 1), output_weight.T, lane_perm)
    from_z = lax.all_to_all(piece, "z", 0, 0)
    from_z, before, after = lax.optimization_barrier((from_z, before, after))
    mine = lax.all_to_all(make_stack(from_z), yx, 0, 0)
    mine, before, after = lax.optimization_barrier((mine, before, after))
    other = lax.ppermute(mine, "c", swap)
    act, cot_perm, slope = make_ready(tokens, norm_gain, cotangent, row_perm, up, down, before, after)

    keep, send, sum_cot, hidden, every_tap, every_proj = make_main(core, mine, other, act, cot_perm)
    received = lax.ppermute(send, "c", swap)
    residual_output, token_cotangent, gain_rows = make_tail(
        every_tap, every_proj, sum_cot, hidden, slope, tokens, norm_gain, cotangent, row_perm
    )
    received, residual_output, token_cotangent, gain_rows = lax.optimization_barrier(
        (received, residual_output, token_cotangent, gain_rows)
    )
    plane = lax.all_to_all(make_pair(keep, received), yx, 0, 0)
    column = lax.all_to_all(make_plane(plane, gain_rows), "z", 0, 0)
    spread = lax.all_to_all(make_column(column), ("c", "y", "x"), 0, 0)
    taps, proj, gain = make_final(spread, lane_perm)
    return residual_output, token_cotangent, taps.transpose(0, 2, 1), proj.T, gain


def solution(mesh):
    fine = Mesh(mesh.devices.reshape(4, 4, 2, 16), ("y", "x", "c", "z"))
    dp = ("y", "x", "c")
    rows = P(dp, "z", None)
    in_specs = (rows, P(), P(None, None, "z"), P(None, "z"), rows)
    out_specs = (rows, rows, P(None, None, "z"), P(None, "z"), P("z"))
    return jax.shard_map(on_device, mesh=fine, in_specs=in_specs, out_specs=out_specs, check_vma=False)
```

time: 154 us -> 137 us (0.89)
  blocking collectives: 82.4 us -> 103 us
  local copies, waits for them, and re-layouts: 17.5 us -> 0.03 us
  waiting for transfers between devices: 12.9 us -> 0.01 us
  starting transfers between devices: 18.3 us -> 13.4 us
  Pallas kernels: 20.9 us -> 19 us
    all_to_all x0 -> x1, blocking collectives: none -> 20.4 us  [on_device(): plane = lax.all_to_all(make_pair(keep, received), yx, 0, 0)]
    unnamed x56 -> x10, local copies, waits for them, and re-layouts: 16.3 us -> 0.03 us
    all_to_all x1 -> x0, waiting for transfers between devices: 8.01 us -> none  [on_device(): plane = lax.all_to_all(make_pair(keep, received), yx, 0, 0)]
    all_to_all x1 -> x0, starting transfers between devices: 4.51 us -> none  [on_device(): plane = lax.all_to_all(make_pair(keep, received), yx, 0, 0)]
    ppermute x1, waiting for transfers between devices: 2.45 us -> 0.01 us  [on_device(): other = lax.ppermute(mine, 'c', swap)]
    ppermute x1, waiting for transfers between devices: 2.45 us -> 0.01 us  [on_device(): received = lax.ppermute(send, 'c', swap)]
    pallas_call x6 -> x7, Pallas kernels: 18.4 us -> 17.7 us  [the longest x1 6.15 us: make_main(): call(main_kernel, [HALF, HALF, shape((SEQS, EXT, HIDDEN), bf16), shape((S...]
  transfers between devices with their start and end apart: 5 -> 4, of which waited for: 3 -> 0; matrix products, arithmetic and copies ran while one was open for 0% -> 0% of each run, Pallas kernels for 4% -> 7%
where the time goes in v4:
time: 137 us; the launch traced here: 136 us
  blocking collectives  103 us (75%)
  Pallas kernels  19 us (14%)
  starting transfers between devices  13.4 us (10%)
    all_to_all x1, blocking collectives, on_device(): from_z = lax.all_to_all(piece, 'z', 0, 0)  28.2 us
    all_to_all x1, blocking collectives, on_device(): mine = lax.all_to_all(make_stack(from_z), yx, 0, 0)  22.4 us
    all_to_all x1, blocking collectives, on_device(): plane = lax.all_to_all(make_pair(keep, received), yx, 0, 0)  20.4 us
    all_to_all x1, blocking collectives, on_device(): column = lax.all_to_all(make_plane(plane, gain_rows), 'z', 0, 0)  17.1 us
    all_to_all x1, blocking collectives, on_device(): spread = lax.all_to_all(make_column(column), ('c', 'y', 'x'), 0, 0)  14.8 us
    pallas_call x1, Pallas kernels, make_main(): call(main_kernel, [HALF, HALF, shape((SEQS, EXT, HIDDEN), bf16), shape((S...  6.15 us
    ppermute x1, starting transfers between devices, on_device(): other = lax.ppermute(mine, 'c', swap)  5.82 us
    pallas_call x1, Pallas kernels, make_tail(): call(tail_kernel, [ROWS, ROWS, shape((16, 384), f32)], [VMEM] * 5 + [FAR,...  5.6 us
  transfers between devices with their start and end apart: 4, of which 0 were waited for; matrix products, arithmetic and copies ran while one was open for 0% of the time, Pallas kernels for 7%

profile of v4, /device:TPU:1, one launch (start us, length us, event | category | flops | bytes accessed | tf_op | source)
XLA Modules:
  0.0 136.2 jit_solution(15080543169762932488)
XLA Ops:
  0.6 0.0 copy-start.1
  0.6 0.0 copy-start.4
  0.7 0.0 copy-start.2
  0.7 1.9 %norm.1 = (bf16[2,192,768]{2,1,0:T(8,128)(2,1)S(1)}, bf16[2,192,768]{2,1,0:T(8,128)(2,1)S(1)}) custom-call(bf16[2,256,768]{2,1,0:T(8,128)(2,1)} %tokens.5, f32[768]{0:T(1024)} %gain.3, bf16[2,256,768]{2,1,0:T(8,128)(2,1)} %cot.5), custom_call_target="tpu_custom_call" | custom-call | tf_op jit(solution)/shard_map/norm/pallas_call | solution.py:306
  2.6 4.4 %collective-permute-start = (bf16[2,192,768]{2,1,0:T(8,128)(2,1)S(1)}, bf16[2,192,768]{2,1,0:T(8,128)(2,1)S(1)}, u32[]{:S(2)}, u32[]{:S(2)}) collective-permute-start(bf16[2,192,768]{2,1,0:T(8,128)(2,1)S(1)} %get-tuple-element.32.up), channel_id=1, source_target_pairs={{0,1},{1,2},{2,3},{3,4},{4,5},{5,6},{6,7},{7,8},{8,9},{9,10},{10,1... | collective-permute-start | bytes 1769480 | tf_op jit(solution)/shard_map/ppermute | solution.py:395
  7.0 1.3 collective-permute-start.1
  8.3 0.0 copy-done.1
  8.3 0.0 copy-done.4
  8.3 0.0 copy-done.2
  8.4 0.2 piece.1
  8.5 28.2 %all_to_all.25.given = bf16[16,8,384]{2,1,0:T(8,128)(2,1)S(1)} all-to-all(bf16[16,8,384]{2,1,0:T(8,128)(2,1)S(1)} %piece.1), channel_id=1, replica_groups=mesh['y'=4,'x'=4,'c'=2,'z'=16] {'z'}, dimensions={0} | all-to-all | bytes 196608 | tf_op jit(solution)/shard_map/all_to_all | solution.py:399
  36.8 0.0 collective-permute-done.before
  36.8 0.0 collective-permute-done.1.after
  36.8 0.1 stack.1
  36.9 0.0 copy-start
  36.9 0.0 copy-start.3
  36.9 22.4 %all_to_all.26.mine = bf16[16,96,384]{2,1,0:T(8,128)(2,1)S(1)} all-to-all(bf16[16,96,384]{2,1,0:T(8,128)(2,1)S(1)} %stack.1), channel_id=1, replica_groups=mesh['y'=4,'x'=4,'c'=2,'z'=16] {'y','x'}, dimensions={0} | all-to-all | bytes 2359296 | tf_op jit(solution)/shard_map/all_to_all | solution.py:401
  59.3 5.8 %collective-permute-start.2 = (bf16[16,96,384]{2,1,0:T(8,128)(2,1)S(1)}, bf16[16,96,384]{2,1,0:T(8,128)(2,1)S(1)}, u32[]{:S(2)}, u32[]{:S(2)}) collective-permute-start(bf16[16,96,384]{2,1,0:T(8,128)(2,1)S(1)} %all_to_all.26.mine), channel_id=1, source_target_pairs={{0,16},{16,0},{1,17},{17,1},{2,18},{18,2},{3,19},{19,3},{4,20},{20... | collective-permute-start | bytes 3538952 | tf_op jit(solution)/shard_map/ppermute | solution.py:403
  65.1 0.0 copy-done
  65.1 0.0 copy-done.3
  65.2 3.5 %ready.1 = (bf16[2,512,768]{2,1,0:T(8,128)(2,1)S(1)}, bf16[2,384,768]{2,1,0:T(8,128)(2,1)S(1)}, f32[2,256,768]{2,1,0:T(8,128)S(1)}) custom-call(bf16[2,256,768]{2,1,0:T(8,128)(2,1)} %tokens.5, f32[768]{0:T(1024)S(1)} %copy-done.3, bf16[2,256,768]{2,1,0:T(8,128)(2,1)} %cot.5, bf16[768,768]{1,0:T(8,128)(2,1)S(1)} %copy-done, ...), custom_call_target="tpu_custom_call" | custom-call | tf_op jit(solution)/shard_map/ready/pallas_call | solution.py:312
  68.7 0.0 collective-permute-done.2.other
  68.7 6.2 %main.1 = (bf16[16,96,384]{2,1,0:T(8,128)(2,1)S(1)}, bf16[16,96,384]{2,1,0:T(8,128)(2,1)S(1)}, bf16[2,384,384]{2,1,0:T(8,128)(2,1)S(1)}, bf16[2,256,384]{2,1,0:T...) custom-call(s32[1]{0:T(128)} %bitcast.core, bf16[16,96,384]{2,1,0:T(8,128)(2,1)S(1)} %all_to_all.26.mine, ...), custom_call_target="tpu_custom_call" | custom-call | tf_op jit(solution)/shard_map/main/pallas_call | solution.py:328
  74.9 1.9 %collective-permute-start.3 = (bf16[16,96,384]{2,1,0:T(8,128)(2,1)S(1)}, bf16[16,96,384]{2,1,0:T(8,128)(2,1)S(1)}, u32[]{:S(2)}, u32[]{:S(2)}) collective-permute-start(bf16[16,96,384]{2,1,0:T(8,128)(2,1)S(1)} %get-tuple-element.42), channel_id=1, source_target_pairs={{0,16},{16,0},{1,17},{17,1},{2,18},{18,2},{3,19},{19,3},{4,20},{20... | collective-permute-start | bytes 3538952 | tf_op jit(solution)/shard_map/ppermute | solution.py:407
  76.8 5.6 %tail.1 = (bf16[2,256,768]{2,1,0:T(8,128)(2,1)}, bf16[2,256,768]{2,1,0:T(8,128)(2,1)}, f32[16,384]{1,0:T(8,128)S(1)}) custom-call(bf16[3,384,768]{2,1,0:T(8,128)(2,1)S(1)} %get-tuple-element.43.taps, bf16[768,384]{1,0:T(8,128)(2,1)S(1)} %get-tuple-element.44.proj, bf16[2,384,384]{2,1,0:T(8,128)(2,1)S(1)} %get-tuple-element.45.sum_cot, ...), custom_call_target="tpu_custom_call" | custom-call | tf_op jit(solution)/shard_map/tail/pallas_call | solution.py:351
  82.4 0.0 collective-permute-done.3.b
  82.4 0.3 pair.1
  82.7 20.4 %all_to_all.27.given = bf16[16,96,384]{2,1,0:T(8,128)(2,1)S(1)} all-to-all(bf16[16,96,384]{2,1,0:T(8,128)(2,1)S(1)} %pair.1), channel_id=1, replica_groups=mesh['y'=4,'x'=4,'c'=2,'z'=16] {'y','x'}, dimensions={0} | all-to-all | bytes 2359296 | tf_op jit(solution)/shard_map/all_to_all | solution.py:414
  103.1 0.2 plane.1
  103.4 17.1 %all_to_all.28.given = bf16[16,8,384]{2,1,0:T(8,128)(2,1)S(1)} all-to-all(bf16[16,8,384]{2,1,0:T(8,128)(2,1)S(1)} %plane.1), channel_id=1, replica_groups=mesh['y'=4,'x'=4,'c'=2,'z'=16] {'z'}, dimensions={0} | all-to-all | bytes 196608 | tf_op jit(solution)/shard_map/all_to_all | solution.py:415
  120.5 14.8 %all_to_all.29.given = bf16[32,8,384]{2,1,0:T(8,128)(2,1)S(1)} all-to-all(bf16[32,8,384]{2,1,0:T(8,128)(2,1)S(1)} %column.1), channel_id=1, replica_groups=mesh['y'=4,'x'=4,'c'=2,'z'=16] {'c','y','x'}, dimensions={0} | all-to-all | bytes 393216 | tf_op jit(solution)/shard_map/all_to_all | solution.py:416
  135.3 0.9 final.1
  (1 shorter events, 0.0 us)
Async XLA Ops:
  0.6 7.7 %copy-start.1 = (bf16[384,384]{1,0:T(8,128)(2,1)S(1)}, bf16[384,384]{1,0:T(8,128)(2,1)}, u32[]{:S(2)}) copy-start(bf16[384,384]{1,0:T(8,128)(2,1)} %constant.24.clone.perm) | copy-start | bytes 884740
  0.6 7.7 %copy-start.4 = (bf16[384,48]{0,1:T(8,128)(2,1)S(1)}, bf16[384,48]{0,1:T(8,128)(2,1)}, u32[]{:S(2)}) copy-start(bf16[384,48]{0,1:T(8,128)(2,1)} %param.10) | copy-start | bytes 110596
  0.7 7.7 %copy-start.2 = (bf16[3,768,24]{1,2,0:T(8,128)(2,1)S(1)}, bf16[3,768,24]{1,2,0:T(8,128)(2,1)}, u32[]{:S(2)}) copy-start(bf16[3,768,24]{1,2,0:T(8,128)(2,1)} %param.9) | copy-start | bytes 331780
  2.6 34.2 %collective-permute-start = (bf16[2,192,768]{2,1,0:T(8,128)(2,1)S(1)}, bf16[2,192,768]{2,1,0:T(8,128)(2,1)S(1)}, u32[]{:S(2)}, u32[]{:S(2)}) collective-permute-start(bf16[2,192,768]{2,1,0:T(8,128)(2,1)S(1)} %get-tuple-element.32.up), channel_id=1, source_target_pairs={{0,1},{1,2},{2,3},{3,4},{4,5},{5,6},{6,7},{7,8},{8,9},{9,10},{10,1... | collective-permute-start | bytes 1769480 | tf_op jit(solution)/shard_map/ppermute | solution.py:395
  7.0 29.8 %collective-permute-start.1 = (bf16[2,192,768]{2,1,0:T(8,128)(2,1)S(1)}, bf16[2,192,768]{2,1,0:T(8,128)(2,1)S(1)}, u32[]{:S(2)}, u32[]{:S(2)}) collective-permute-start(bf16[2,192,768]{2,1,0:T(8,128)(2,1)S(1)} %get-tuple-element.33.down), channel_id=1, source_target_pairs={{1,0},{2,1},{3,2},{4,3},{5,4},{6,5},{7,6},{8,7},{9,8},{10,9},{11,1... | collective-permute-start | bytes 1769480 | tf_op jit(solution)/shard_map/ppermute | solution.py:396
  36.9 28.2 %copy-start = (bf16[768,768]{1,0:T(8,128)(2,1)S(1)}, bf16[768,768]{1,0:T(8,128)(2,1)}, u32[]{:S(2)}) copy-start(bf16[768,768]{1,0:T(8,128)(2,1)} %constant.25.clone.perm) | copy-start | bytes 3538948
  36.9 28.2 %copy-start.3 = (f32[768]{0:T(1024)S(1)}, f32[768]{0:T(1024)}, u32[]{:S(2)}) copy-start(f32[768]{0:T(1024)} %gain.3) | copy-start | bytes 9220
  59.3 9.4 %collective-permute-start.2 = (bf16[16,96,384]{2,1,0:T(8,128)(2,1)S(1)}, bf16[16,96,384]{2,1,0:T(8,128)(2,1)S(1)}, u32[]{:S(2)}, u32[]{:S(2)}) collective-permute-start(bf16[16,96,384]{2,1,0:T(8,128)(2,1)S(1)} %all_to_all.26.mine), channel_id=1, source_target_pairs={{0,16},{16,0},{1,17},{17,1},{2,18},{18,2},{3,19},{19,3},{4,20},{20... | collective-permute-start | bytes 3538952 | tf_op jit(solution)/shard_map/ppermute | solution.py:403
  74.9 7.5 %collective-permute-start.3 = (bf16[16,96,384]{2,1,0:T(8,128)(2,1)S(1)}, bf16[16,96,384]{2,1,0:T(8,128)(2,1)S(1)}, u32[]{:S(2)}, u32[]{:S(2)}) collective-permute-start(bf16[16,96,384]{2,1,0:T(8,128)(2,1)S(1)} %get-tuple-element.42), channel_id=1, source_target_pairs={{0,16},{16,0},{1,17},{17,1},{2,18},{18,2},{3,19},{19,3},{4,20},{20... | collective-permute-start | bytes 3538952 | tf_op jit(solution)/shard_map/ppermute | solution.py:407

commit v5 on v4

--- a/solution.py
+++ b/solution.py
@@ -17,11 +17,11 @@
 epsilon = 1e-06
 bf16 = jnp.bfloat16
 f32 = jnp.float32
-HBM = pl.BlockSpec(memory_space=pl.ANY)
 SMEM = pl.BlockSpec(memory_space=pltpu.SMEM)
 VMEM = pl.BlockSpec(memory_space=pltpu.VMEM)
 FAR = pl.BlockSpec(memory_space=pltpu.HBM)
 MB = 1024 * 1024
+TILE = 32
 
 
 def permutation(outer, inner, width):
@@ -94,11 +94,11 @@
     gain_row = gain[...].reshape(1, CHANNELS)
     for s in range(SEQS):
         loads[s].wait()
-        v = rows[s].astype(f32)
-        normed = v * inverse_rms_of(v) * gain_row
-        a = activate(normed, tanh_of(normed)).astype(bf16)
-        up[s, 0 : 2 * STEP] = a[BINS - 2 * STEP :]
-        down[s, 0 : 2 * STEP] = a[: 2 * STEP]
+        for r in range(0, BINS, TILE):
+            v = rows[s, r : r + TILE].astype(f32)
+            normed = v * inverse_rms_of(v) * gain_row
+            edge, at = (down, r) if r < 2 * STEP else (up, r - 2 * STEP)
+            edge[s, at : at + TILE] = activate(normed, tanh_of(normed)).astype(bf16)
     for c in loads[SEQS + 1 :]:
         c.wait()
 
@@ -106,61 +106,61 @@
 def ready_kernel(
     tokens, gain, cot, perm, up, down, before, after,
     act, cot_perm, slope,
-    rows, cots, matrix, sems,
+    rows, cots, sems,
 ):
-    loads = [(cot, cots), (perm, matrix), (tokens, rows)]
+    loads = [(cot.at[s], cots.at[s]) for s in range(SEQS)] + [(tokens.at[s], rows.at[s]) for s in range(SEQS)]
     loads = run(loads, sems)
     half = 2 * STEP
     act[:, 0:half] = before[:, 0:half]
     act[:, half : 2 * half] = down[:, 0:half]
     act[:, 2 * half : 3 * half] = up[:, 0:half]
     act[:, 3 * half :] = after[:, 0:half]
-    for c in loads:
-        c.wait()
-    order = matrix[...]
+    order = perm[...]
     gain_row = gain[...].reshape(1, CHANNELS)
     for s in range(SEQS):
-        cot_perm[s, STEP : STEP + BINS] = dot(cots[s], order, 1, 0).astype(bf16)
         edges = dot(jnp.concatenate([before[s, half:], after[s, half:]]), order, 1, 0).astype(bf16)
         cot_perm[s, 0:STEP] = edges[0:STEP]
         cot_perm[s, STEP + BINS :] = edges[STEP:]
-        v = rows[s].astype(f32)
-        normed = v * inverse_rms_of(v) * gain_row
-        slope[s] = derivative(normed, tanh_of(normed))
-
-
-def weight_copies(core, mine, other, taps, proj, sems, act):
-    for here in range(2):
-
-        @pl.when(core[0] == here)
-        def _(here=here):
-            for p in range(32):
-                source = (mine if p // 16 == here else other).at[p % 16]
-                if p < 24:
-                    q, k, half = p // 6, p % 6 // 2, p % 2
-                    target = taps.at[k, 96 * q : 96 * q + 96, 384 * half : 384 * half + 384]
-                else:
-                    target = proj.at[96 * (p - 24) : 96 * (p - 24) + 96]
-                copy = pltpu.make_async_copy(source, target, sems.at[p])
-                copy.start() if act else copy.wait()
+    for s in range(SEQS):
+        loads[s].wait()
+        cot_perm[s, STEP : STEP + BINS] = dot(cots[s], order, 1, 0).astype(bf16)
+        loads[SEQS + s].wait()
+        for r in range(0, BINS, TILE):
+            v = rows[s, r : r + TILE].astype(f32)
+            normed = v * inverse_rms_of(v) * gain_row
+            slope[s, r : r + TILE] = derivative(normed, tanh_of(normed))
+
+
+def place(lower, upper, taps, proj):
+    for p in range(32):
+        piece = (lower if p < 16 else upper)[p % 16]
+        if p < 24:
+            q, k, half = p // 6, p % 6 // 2, p % 2
+            taps[k, 96 * q : 96 * q + 96, 384 * half : 384 * half + 384] = piece
+        else:
+            proj[96 * (p - 24) : 96 * (p - 24) + 96] = piece
 
 
 def main_kernel(
     core, mine, other, act, cot,
     keep, send, sum_cot, hidden, taps, proj,
-    grad, wsems, sems,
+    grad,
 ):
     own = BINS
-    weight_copies(core, mine, other, taps, proj, wsems, True)
-    weight_copies(core, mine, other, taps, proj, wsems, False)
+    pl.when(core[0] == 0)(lambda: place(mine, other, taps, proj))
+    pl.when(core[0] == 1)(lambda: place(other, mine, taps, proj))
     for s in range(SEQS):
         total = dot(act[s, 0:EXT], taps[0], 1, 1)
         total += dot(act[s, STEP : STEP + EXT], taps[1], 1, 1)
         total += dot(act[s, 2 * STEP : 2 * STEP + EXT], taps[2], 1, 1)
-        hidden_cot = dot(cot[s], proj[...], 1, 0).astype(bf16).astype(f32)
-        t = tanh_of(total)
-        hidden[s] = activate(total, t)[STEP : STEP + own].astype(bf16)
-        sum_cot[s] = (hidden_cot * derivative(total, t)).astype(bf16)
+        hidden_cot = dot(cot[s], proj[...], 1, 0)
+        for r in range(0, EXT, TILE):
+            v = total[r : r + TILE]
+            t = tanh_of(v)
+            if STEP <= r < STEP + own:
+                hidden[s, r - STEP : r - STEP + TILE] = activate(v, t).astype(bf16)
+            rounded = hidden_cot[r : r + TILE].astype(bf16).astype(f32)
+            sum_cot[s, r : r + TILE] = (rounded * derivative(v, t)).astype(bf16)
     centre = jnp.concatenate([sum_cot[s, STEP : STEP + own] for s in range(SEQS)])
     for k in range(3):
         rows = jnp.concatenate([act[s, STEP * (k + 1) : STEP * (k + 1) + own] for s in range(SEQS)])
@@ -172,12 +172,16 @@
     g = dot(rows, jnp.concatenate([hidden[s] for s in range(SEQS)]), 0, 0).astype(bf16)
     for u in range(8):
         grad[24 + u] = g[96 * u : 96 * u + 96]
-    saves = [
-        (grad.at[pl.ds(16 * core[0], 16)], keep),
-        (grad.at[pl.ds(16 - 16 * core[0], 16)], send),
-    ]
-    for c in run(saves, sems):
-        c.wait()
+
+    @pl.when(core[0] == 0)
+    def _():
+        keep[...] = grad[0:16]
+        send[...] = grad[16:32]
+
+    @pl.when(core[0] == 1)
+    def _():
+        keep[...] = grad[16:32]
+        send[...] = grad[0:16]
 
 
 def pair_kernel(a, b, out):
@@ -187,35 +191,39 @@
 def tail_kernel(
     taps, proj, sum_cot, hidden, slope, tokens, gain, cot, perm,
     block_output, token_gradient, gain_rows,
-    rows, cots, matrix, result, sems, out_sems,
+    rows, cots, result, sems, out_sems,
 ):
-    loads = run([(tokens, rows), (cot, cots), (perm, matrix)], sems)
-    for c in loads:
-        c.wait()
-    natural = dot(matrix[...], proj[...], 1, 0).astype(bf16)
+    loads = [(tokens.at[s], rows.at[s]) for s in range(SEQS)] + [(cot.at[s], cots.at[s]) for s in range(SEQS)]
+    loads = run(loads, sems)
+    natural = dot(perm[...], proj[...], 1, 0).astype(bf16)
     gain_row = gain[...].reshape(1, CHANNELS)
     gain_sum = jnp.zeros((1, CHANNELS), f32)
     saves = []
     for s in range(SEQS):
-        v = rows[s].astype(f32)
-        result[0, s] = (v + dot(hidden[s], natural, 1, 1)).astype(bf16)
         total = dot(sum_cot[s, 2 * STEP : 2 * STEP + BINS], taps[0], 1, 0)
         total += dot(sum_cot[s, STEP : STEP + BINS], taps[1], 1, 0)
         total += dot(sum_cot[s, 0:BINS], taps[2], 1, 0)
-        inverse_rms = inverse_rms_of(v)
-        normed_cot = total.astype(bf16).astype(f32) * slope[s]
-        scaled_cot = gain_row * normed_cot
-        mean = jnp.mean(scaled_cot * v, axis=-1, keepdims=True)
-        result[1, s] = (
-            cots[s].astype(f32) + inverse_rms * scaled_cot - v * (inverse_rms * inverse_rms * inverse_rms) * mean
-        ).astype(bf16)
+        projected = dot(hidden[s], natural, 1, 1)
+        loads[s].wait()
+        loads[SEQS + s].wait()
+        for r in range(0, BINS, TILE):
+            at = slice(r, r + TILE)
+            v = rows[s, at].astype(f32)
+            result[0, s, at] = (v + projected[at]).astype(bf16)
+            normed_cot = total[at].astype(bf16).astype(f32) * slope[s, at]
+            inverse_rms = inverse_rms_of(v)
+            scaled_cot = gain_row * normed_cot
+            mean = jnp.mean(scaled_cot * v, axis=-1, keepdims=True)
+            result[1, s, at] = (
+                cots[s, at].astype(f32) + inverse_rms * scaled_cot - v * (inverse_rms * inverse_rms * inverse_rms) * mean
+            ).astype(bf16)
+            gain_sum += jnp.sum(normed_cot * v * inverse_rms, axis=0, keepdims=True)
         saves += [
             pltpu.make_async_copy(result.at[0, s], block_output.at[s], out_sems.at[2 * s]),
             pltpu.make_async_copy(result.at[1, s], token_gradient.at[s], out_sems.at[2 * s + 1]),
         ]
         saves[-2].start()
         saves[-1].start()
-        gain_sum += jnp.sum(normed_cot * v * inverse_rms, axis=0, keepdims=True)
     gain_rows[...] = jnp.zeros((16, 384), f32)
     for z in range(16):
         gain_rows[z : z + 1, 0:48] = gain_sum[:, 48 * z : 48 * z + 48]
@@ -284,7 +292,6 @@
 HALF = shape((16, 96, 384), bf16)
 ROWS = shape((SEQS, BINS, CHANNELS), bf16)
 LOCAL = pltpu.VMEM((SEQS, BINS, CHANNELS), bf16)
-MATRIX = pltpu.VMEM((CHANNELS, CHANNELS), bf16)
 
 
 def waits(count):
@@ -303,7 +310,7 @@
 
 def make_norm(tokens, gain, cot):
     edge = shape((SEQS, 3 * STEP, CHANNELS), bf16)
-    return call(norm_kernel, [edge, edge], [FAR] * 3, [VMEM] * 2, "norm", 12, [LOCAL, pltpu.VMEM((CHANNELS,), f32), waits(5)])(
+    return call(norm_kernel, [edge, edge], [FAR] * 3, [VMEM] * 2, "norm", 6, [LOCAL, pltpu.VMEM((CHANNELS,), f32), waits(5)])(
         tokens, gain, cot
     )
 
@@ -316,11 +323,11 @@
             shape((SEQS, EXT, CHANNELS), bf16),
             shape((SEQS, BINS, CHANNELS), f32),
         ],
-        [FAR, VMEM, FAR, FAR] + [VMEM] * 4,
+        [FAR, VMEM, FAR] + [VMEM] * 5,
         [VMEM] * 3,
         "ready",
-        20,
-        [LOCAL, LOCAL, MATRIX, waits(3)],
+        10,
+        [LOCAL, LOCAL, waits(4)],
     )(tokens, gain, cot, perm, up, down, before, after)
 
 
@@ -335,11 +342,11 @@
             shape((3, HIDDEN, CHANNELS), bf16),
             shape((CHANNELS, HIDDEN), bf16),
         ],
-        [SMEM, HBM, HBM, VMEM, VMEM],
-        [HBM] * 2 + [VMEM] * 4,
+        [SMEM] + [VMEM] * 4,
+        [VMEM] * 6,
         "main",
-        24,
-        [pltpu.VMEM((32, 96, 384), bf16), waits(32), waits(2)],
+        10,
+        [pltpu.VMEM((32, 96, 384), bf16)],
     )(core, mine, other, act, cot)
 
 
@@ -351,11 +358,11 @@
     return call(
         tail_kernel,
         [ROWS, ROWS, shape((16, 384), f32)],
-        [VMEM] * 5 + [FAR, VMEM, FAR, FAR],
+        [VMEM] * 5 + [FAR, VMEM, FAR, VMEM],
         [FAR, FAR, VMEM],
         "tail",
-        24,
-        [LOCAL, LOCAL, MATRIX, pltpu.VMEM((2, SEQS, BINS, CHANNELS), bf16), waits(3), waits(4)],
+        12,
+        [LOCAL, LOCAL, pltpu.VMEM((2, SEQS, BINS, CHANNELS), bf16), waits(4), waits(4)],
     )(taps, proj, sum_cot, hidden, slope, tokens, gain, cot, perm)
 
 

time: 137 us -> 134 us (0.978)
  Pallas kernels: 19 us -> 16.4 us
    pallas_call x1, Pallas kernels: 6.15 us -> 4.7 us  [make_main(): call(main_kernel, [HALF, HALF, shape((SEQS, EXT, HIDDEN), bf16), shape((S...]
  transfers between devices with their start and end apart: 4 -> 4, of which waited for: 0 -> 0; matrix products, arithmetic and copies ran while one was open for 0% -> 0% of each run, Pallas kernels for 7% -> 6%
where the time goes in v5:
time: 134 us
  blocking collectives  103 us (77%)
  Pallas kernels  16.4 us (12%)
  starting transfers between devices  13.6 us (10%)
    all_to_all x1, blocking collectives, on_device(): from_z = lax.all_to_all(piece, 'z', 0, 0)  28.2 us
    all_to_all x1, blocking collectives, on_device(): mine = lax.all_to_all(make_stack(from_z), yx, 0, 0)  22.4 us
    all_to_all x1, blocking collectives, on_device(): plane = lax.all_to_all(make_pair(keep, received), yx, 0, 0)  20.4 us
    all_to_all x1, blocking collectives, on_device(): column = lax.all_to_all(make_plane(plane, gain_rows), 'z', 0, 0)  17.1 us
    all_to_all x1, blocking collectives, on_device(): spread = lax.all_to_all(make_column(column), ('c', 'y', 'x'), 0, 0)  14.8 us
    ppermute x1, starting transfers between devices, on_device(): other = lax.ppermute(mine, 'c', swap)  5.82 us
    pallas_call x1, Pallas kernels, make_main(): call(main_kernel, [HALF, HALF, shape((SEQS, EXT, HIDDEN), bf16), shape((S...  4.7 us
    pallas_call x1, Pallas kernels, make_tail(): call(tail_kernel, [ROWS, ROWS, shape((16, 384), f32)], [VMEM] * 5 + [FAR,...  4.5 us
  transfers between devices with their start and end apart: 4, of which 0 were waited for; matrix products, arithmetic and copies ran while one was open for 0% of the time, Pallas kernels for 6%

profile of v5, /device:TPU:1, one launch (start us, length us, event | category | flops | bytes accessed | tf_op | source)
XLA Modules:
  0.0 133.8 jit_solution(1907872634604842431)
XLA Ops:
  0.6 0.0 copy-start.1
  0.6 0.0 copy-start.4
  0.7 0.0 copy-start.2
  0.7 1.9 %norm.1 = (bf16[2,192,768]{2,1,0:T(8,128)(2,1)S(1)}, bf16[2,192,768]{2,1,0:T(8,128)(2,1)S(1)}) custom-call(bf16[2,256,768]{2,1,0:T(8,128)(2,1)} %tokens.5, f32[768]{0:T(1024)} %gain.3, bf16[2,256,768]{2,1,0:T(8,128)(2,1)} %cot.5), custom_call_target="tpu_custom_call" | custom-call | tf_op jit(solution)/shard_map/norm/pallas_call | solution.py:313
  2.6 4.4 %collective-permute-start = (bf16[2,192,768]{2,1,0:T(8,128)(2,1)S(1)}, bf16[2,192,768]{2,1,0:T(8,128)(2,1)S(1)}, u32[]{:S(2)}, u32[]{:S(2)}) collective-permute-start(bf16[2,192,768]{2,1,0:T(8,128)(2,1)S(1)} %get-tuple-element.32.up), channel_id=1, source_target_pairs={{0,1},{1,2},{2,3},{3,4},{4,5},{5,6},{6,7},{7,8},{8,9},{9,10},{10,1... | collective-permute-start | bytes 1769480 | tf_op jit(solution)/shard_map/ppermute | solution.py:402
  7.0 1.3 collective-permute-start.1
  8.3 0.0 copy-done.1
  8.3 0.0 copy-done.4
  8.3 0.0 copy-done.2
  8.4 0.2 piece.1
  8.5 28.2 %all_to_all.25.given = bf16[16,8,384]{2,1,0:T(8,128)(2,1)S(1)} all-to-all(bf16[16,8,384]{2,1,0:T(8,128)(2,1)S(1)} %piece.1), channel_id=1, replica_groups=mesh['y'=4,'x'=4,'c'=2,'z'=16] {'z'}, dimensions={0} | all-to-all | bytes 196608 | tf_op jit(solution)/shard_map/all_to_all | solution.py:406
  36.8 0.0 collective-permute-done.before
  36.8 0.0 collective-permute-done.1.after
  36.8 0.1 stack.1
  36.9 0.0 copy-start
  36.9 0.0 copy-start.3
  36.9 22.4 %all_to_all.26.mine = bf16[16,96,384]{2,1,0:T(8,128)(2,1)S(1)} all-to-all(bf16[16,96,384]{2,1,0:T(8,128)(2,1)S(1)} %stack.1), channel_id=1, replica_groups=mesh['y'=4,'x'=4,'c'=2,'z'=16] {'y','x'}, dimensions={0} | all-to-all | bytes 2359296 | tf_op jit(solution)/shard_map/all_to_all | solution.py:408
  59.3 5.8 %collective-permute-start.2 = (bf16[16,96,384]{2,1,0:T(8,128)(2,1)S(1)}, bf16[16,96,384]{2,1,0:T(8,128)(2,1)S(1)}, u32[]{:S(2)}, u32[]{:S(2)}) collective-permute-start(bf16[16,96,384]{2,1,0:T(8,128)(2,1)S(1)} %all_to_all.26.mine), channel_id=1, source_target_pairs={{0,16},{16,0},{1,17},{17,1},{2,18},{18,2},{3,19},{19,3},{4,20},{20... | collective-permute-start | bytes 3538952 | tf_op jit(solution)/shard_map/ppermute | solution.py:410
  65.1 0.0 copy-done
  65.1 0.0 copy-done.3
  65.2 3.6 %ready.1 = (bf16[2,512,768]{2,1,0:T(8,128)(2,1)S(1)}, bf16[2,384,768]{2,1,0:T(8,128)(2,1)S(1)}, f32[2,256,768]{2,1,0:T(8,128)S(1)}) custom-call(bf16[2,256,768]{2,1,0:T(8,128)(2,1)} %tokens.5, f32[768]{0:T(1024)S(1)} %copy-done.3, bf16[2,256,768]{2,1,0:T(8,128)(2,1)} %cot.5, bf16[768,768]{1,0:T(8,128)(2,1)S(1)} %copy-done, ...), custom_call_target="tpu_custom_call" | custom-call | tf_op jit(solution)/shard_map/ready/pallas_call | solution.py:319
  68.7 0.0 collective-permute-done.2.other
  68.7 4.7 %main.1 = (bf16[16,96,384]{2,1,0:T(8,128)(2,1)S(1)}, bf16[16,96,384]{2,1,0:T(8,128)(2,1)S(1)}, bf16[2,384,384]{2,1,0:T(8,128)(2,1)S(1)}, bf16[2,256,384]{2,1,0:T...) custom-call(s32[1]{0:T(128)} %bitcast.core, bf16[16,96,384]{2,1,0:T(8,128)(2,1)S(1)} %all_to_all.26.mine, ...), custom_call_target="tpu_custom_call" | custom-call | tf_op jit(solution)/shard_map/main/pallas_call | solution.py:335
  73.4 2.1 %collective-permute-start.3 = (bf16[16,96,384]{2,1,0:T(8,128)(2,1)S(1)}, bf16[16,96,384]{2,1,0:T(8,128)(2,1)S(1)}, u32[]{:S(2)}, u32[]{:S(2)}) collective-permute-start(bf16[16,96,384]{2,1,0:T(8,128)(2,1)S(1)} %get-tuple-element.42), channel_id=1, source_target_pairs={{0,16},{16,0},{1,17},{17,1},{2,18},{18,2},{3,19},{19,3},{4,20},{20... | collective-permute-start | bytes 3538952 | tf_op jit(solution)/shard_map/ppermute | solution.py:414
  75.5 4.5 %tail.1 = (bf16[2,256,768]{2,1,0:T(8,128)(2,1)}, bf16[2,256,768]{2,1,0:T(8,128)(2,1)}, f32[16,384]{1,0:T(8,128)S(1)}) custom-call(bf16[3,384,768]{2,1,0:T(8,128)(2,1)S(1)} %get-tuple-element.43.taps, bf16[768,384]{1,0:T(8,128)(2,1)S(1)} %get-tuple-element.44.proj, bf16[2,384,384]{2,1,0:T(8,128)(2,1)S(1)} %get-tuple-element.45.sum_cot, ...), custom_call_target="tpu_custom_call" | custom-call | tf_op jit(solution)/shard_map/tail/pallas_call | solution.py:358
  80.1 0.0 collective-permute-done.3.b
  80.1 0.3 pair.1
  80.4 20.4 %all_to_all.27.given = bf16[16,96,384]{2,1,0:T(8,128)(2,1)S(1)} all-to-all(bf16[16,96,384]{2,1,0:T(8,128)(2,1)S(1)} %pair.1), channel_id=1, replica_groups=mesh['y'=4,'x'=4,'c'=2,'z'=16] {'y','x'}, dimensions={0} | all-to-all | bytes 2359296 | tf_op jit(solution)/shard_map/all_to_all | solution.py:421
  100.7 0.2 plane.1
  101.0 17.1 %all_to_all.28.given = bf16[16,8,384]{2,1,0:T(8,128)(2,1)S(1)} all-to-all(bf16[16,8,384]{2,1,0:T(8,128)(2,1)S(1)} %plane.1), channel_id=1, replica_groups=mesh['y'=4,'x'=4,'c'=2,'z'=16] {'z'}, dimensions={0} | all-to-all | bytes 196608 | tf_op jit(solution)/shard_map/all_to_all | solution.py:422
  118.1 14.8 %all_to_all.29.given = bf16[32,8,384]{2,1,0:T(8,128)(2,1)S(1)} all-to-all(bf16[32,8,384]{2,1,0:T(8,128)(2,1)S(1)} %column.1), channel_id=1, replica_groups=mesh['y'=4,'x'=4,'c'=2,'z'=16] {'c','y','x'}, dimensions={0} | all-to-all | bytes 393216 | tf_op jit(solution)/shard_map/all_to_all | solution.py:423
  133.0 0.9 final.1
  (1 shorter events, 0.0 us)
Async XLA Ops:
  0.6 7.7 %copy-start.1 = (bf16[384,384]{1,0:T(8,128)(2,1)S(1)}, bf16[384,384]{1,0:T(8,128)(2,1)}, u32[]{:S(2)}) copy-start(bf16[384,384]{1,0:T(8,128)(2,1)} %constant.24.clone.perm) | copy-start | bytes 884740
  0.6 7.7 %copy-start.4 = (bf16[384,48]{0,1:T(8,128)(2,1)S(1)}, bf16[384,48]{0,1:T(8,128)(2,1)}, u32[]{:S(2)}) copy-start(bf16[384,48]{0,1:T(8,128)(2,1)} %param.10) | copy-start | bytes 110596
  0.7 7.7 %copy-start.2 = (bf16[3,768,24]{1,2,0:T(8,128)(2,1)S(1)}, bf16[3,768,24]{1,2,0:T(8,128)(2,1)}, u32[]{:S(2)}) copy-start(bf16[3,768,24]{1,2,0:T(8,128)(2,1)} %param.9) | copy-start | bytes 331780
  2.6 34.2 %collective-permute-start = (bf16[2,192,768]{2,1,0:T(8,128)(2,1)S(1)}, bf16[2,192,768]{2,1,0:T(8,128)(2,1)S(1)}, u32[]{:S(2)}, u32[]{:S(2)}) collective-permute-start(bf16[2,192,768]{2,1,0:T(8,128)(2,1)S(1)} %get-tuple-element.32.up), channel_id=1, source_target_pairs={{0,1},{1,2},{2,3},{3,4},{4,5},{5,6},{6,7},{7,8},{8,9},{9,10},{10,1... | collective-permute-start | bytes 1769480 | tf_op jit(solution)/shard_map/ppermute | solution.py:402
  7.0 29.8 %collective-permute-start.1 = (bf16[2,192,768]{2,1,0:T(8,128)(2,1)S(1)}, bf16[2,192,768]{2,1,0:T(8,128)(2,1)S(1)}, u32[]{:S(2)}, u32[]{:S(2)}) collective-permute-start(bf16[2,192,768]{2,1,0:T(8,128)(2,1)S(1)} %get-tuple-element.33.down), channel_id=1, source_target_pairs={{1,0},{2,1},{3,2},{4,3},{5,4},{6,5},{7,6},{8,7},{9,8},{10,9},{11,1... | collective-permute-start | bytes 1769480 | tf_op jit(solution)/shard_map/ppermute | solution.py:403
  36.9 28.2 %copy-start = (bf16[768,768]{1,0:T(8,128)(2,1)S(1)}, bf16[768,768]{1,0:T(8,128)(2,1)}, u32[]{:S(2)}) copy-start(bf16[768,768]{1,0:T(8,128)(2,1)} %constant.25.clone.perm) | copy-start | bytes 3538948
  36.9 28.2 %copy-start.3 = (f32[768]{0:T(1024)S(1)}, f32[768]{0:T(1024)}, u32[]{:S(2)}) copy-start(f32[768]{0:T(1024)} %gain.3) | copy-start | bytes 9220
  59.3 9.4 %collective-permute-start.2 = (bf16[16,96,384]{2,1,0:T(8,128)(2,1)S(1)}, bf16[16,96,384]{2,1,0:T(8,128)(2,1)S(1)}, u32[]{:S(2)}, u32[]{:S(2)}) collective-permute-start(bf16[16,96,384]{2,1,0:T(8,128)(2,1)S(1)} %all_to_all.26.mine), channel_id=1, source_target_pairs={{0,16},{16,0},{1,17},{17,1},{2,18},{18,2},{3,19},{19,3},{4,20},{20... | collective-permute-start | bytes 3538952 | tf_op jit(solution)/shard_map/ppermute | solution.py:410
  73.4 6.6 %collective-permute-start.3 = (bf16[16,96,384]{2,1,0:T(8,128)(2,1)S(1)}, bf16[16,96,384]{2,1,0:T(8,128)(2,1)S(1)}, u32[]{:S(2)}, u32[]{:S(2)}) collective-permute-start(bf16[16,96,384]{2,1,0:T(8,128)(2,1)S(1)} %get-tuple-element.42), channel_id=1, source_target_pairs={{0,16},{16,0},{1,17},{17,1},{2,18},{18,2},{3,19},{19,3},{4,20},{20... | collective-permute-start | bytes 3538952 | tf_op jit(solution)/shard_map/ppermute | solution.py:414

commit v6 on v5

--- a/solution.py
+++ b/solution.py
@@ -103,32 +103,34 @@
         c.wait()
 
 
-def ready_kernel(
-    tokens, gain, cot, perm, up, down, before, after,
-    act, cot_perm, slope,
-    rows, cots, sems,
-):
+def own_kernel(tokens, gain, cot, perm, cot_perm, slope, rows, cots, sems):
     loads = [(cot.at[s], cots.at[s]) for s in range(SEQS)] + [(tokens.at[s], rows.at[s]) for s in range(SEQS)]
     loads = run(loads, sems)
+    order = perm[...]
+    gain_row = gain[...].reshape(1, CHANNELS)
+    for s in range(SEQS):
+        loads[s].wait()
+        cot_perm[s] = dot(cots[s], order, 1, 0).astype(bf16)
+        loads[SEQS + s].wait()
+        for r in range(0, BINS, TILE):
+            v = rows[s, r : r + TILE].astype(f32)
+            normed = v * inverse_rms_of(v) * gain_row
+            slope[s, r : r + TILE] = derivative(normed, tanh_of(normed))
+
+
+def ready_kernel(own, perm, up, down, before, after, act, cot_perm):
     half = 2 * STEP
     act[:, 0:half] = before[:, 0:half]
     act[:, half : 2 * half] = down[:, 0:half]
     act[:, 2 * half : 3 * half] = up[:, 0:half]
     act[:, 3 * half :] = after[:, 0:half]
-    order = perm[...]
-    gain_row = gain[...].reshape(1, CHANNELS)
+    edges = [t[s, half:] for s in range(SEQS) for t in (before, after)]
+    edges = dot(jnp.concatenate(edges), perm[...], 1, 0).astype(bf16)
     for s in range(SEQS):
-        edges = dot(jnp.concatenate([before[s, half:], after[s, half:]]), order, 1, 0).astype(bf16)
-        cot_perm[s, 0:STEP] = edges[0:STEP]
-        cot_perm[s, STEP + BINS :] = edges[STEP:]
-    for s in range(SEQS):
-        loads[s].wait()
-        cot_perm[s, STEP : STEP + BINS] = dot(cots[s], order, 1, 0).astype(bf16)
-        loads[SEQS + s].wait()
-        for r in range(0, BINS, TILE):
-            v = rows[s, r : r + TILE].astype(f32)
-            normed = v * inverse_rms_of(v) * gain_row
-            slope[s, r : r + TILE] = derivative(normed, tanh_of(normed))
+        at = 2 * s * STEP
+        cot_perm[s, 0:STEP] = edges[at : at + STEP]
+        cot_perm[s, STEP : STEP + BINS] = own[s]
+        cot_perm[s, STEP + BINS :] = edges[at + STEP : at + 2 * STEP]
 
 
 def place(lower, upper, taps, proj):
@@ -315,20 +317,30 @@
     )
 
 
-def make_ready(tokens, gain, cot, perm, up, down, before, after):
+def make_own(tokens, gain, cot, perm):
+    return call(
+        own_kernel,
+        [ROWS, shape((SEQS, BINS, CHANNELS), f32)],
+        [FAR, VMEM, FAR, VMEM],
+        [VMEM] * 2,
+        "own",
+        10,
+        [LOCAL, LOCAL, waits(4)],
+    )(tokens, gain, cot, perm)
+
+
+def make_ready(own, perm, up, down, before, after):
     return call(
         ready_kernel,
         [
             shape((SEQS, BINS + 4 * STEP, CHANNELS), bf16),
             shape((SEQS, EXT, CHANNELS), bf16),
-            shape((SEQS, BINS, CHANNELS), f32),
         ],
-        [FAR, VMEM, FAR] + [VMEM] * 5,
-        [VMEM] * 3,
+        [VMEM] * 6,
+        [VMEM] * 2,
         "ready",
-        10,
-        [LOCAL, LOCAL, waits(4)],
-    )(tokens, gain, cot, perm, up, down, before, after)
+        8,
+    )(own, perm, up, down, before, after)
 
 
 def make_main(core, mine, other, act, cot):
@@ -398,17 +410,17 @@
 
     tokens = pltpu.with_memory_space_constraint(tokens, pltpu.HBM)
     cotangent = pltpu.with_memory_space_constraint(cotangent, pltpu.HBM)
+    piece = make_piece(part, dilated_weight.transpose(0, 2, 1), output_weight.T, lane_perm)
     up, down = make_norm(tokens, pltpu.with_memory_space_constraint(norm_gain, pltpu.HBM), cotangent)
+    from_z = lax.all_to_all(piece, "z", 0, 0)
     before = lax.ppermute(up, "z", [(i, i + 1) for i in range(15)])
     after = lax.ppermute(down, "z", [(i + 1, i) for i in range(15)])
-
-    piece = make_piece(part, dilated_weight.transpose(0, 2, 1), output_weight.T, lane_perm)
-    from_z = lax.all_to_all(piece, "z", 0, 0)
-    from_z, before, after = lax.optimization_barrier((from_z, before, after))
+    own, slope = make_own(tokens, norm_gain, cotangent, row_perm)
+    from_z, before, after, own, slope = lax.optimization_barrier((from_z, before, after, own, slope))
     mine = lax.all_to_all(make_stack(from_z), yx, 0, 0)
     mine, before, after = lax.optimization_barrier((mine, before, after))
     other = lax.ppermute(mine, "c", swap)
-    act, cot_perm, slope = make_ready(tokens, norm_gain, cotangent, row_perm, up, down, before, after)
+    act, cot_perm = make_ready(own, row_perm, up, down, before, after)
 
     keep, send, sum_cot, hidden, every_tap, every_proj = make_main(core, mine, other, act, cot_perm)
     received = lax.ppermute(send, "c", swap)

time: 134 us -> 135 us (level)
  blocking collectives: 103 us -> 73.4 us
  starting transfers between devices: 13.6 us -> 30.5 us
  waiting for transfers between devices: 0.01 us -> 7.67 us
  Pallas kernels: 16.4 us -> 20.3 us
  local copies, waits for them, and re-layouts: 0.03 us -> 1.67 us
    all_to_all x1 -> x0, blocking collectives: 28.2 us -> none  [on_device(): from_z = lax.all_to_all(piece, 'z', 0, 0)]
    all_to_all x0 -> x1, starting transfers between devices: none -> 15.8 us  [on_device(): from_z = lax.all_to_all(piece, 'z', 0, 0)]
    all_to_all x0 -> x1, waiting for transfers between devices: none -> 7.46 us  [on_device(): from_z = lax.all_to_all(piece, 'z', 0, 0)]
    pallas_call x0 -> x1, Pallas kernels: none -> 3.53 us  [make_own(): call(own_kernel, [ROWS, shape((SEQS, BINS, CHANNELS), f32)], [FAR, VMEM,...]
    unnamed x10 -> x14, local copies, waits for them, and re-layouts: 0.03 us -> 1.67 us
  transfers between devices with their start and end apart: 4 -> 5, of which waited for: 0 -> 2; matrix products, arithmetic and copies ran while one was open for 0% -> 0% of each run, Pallas kernels for 6% -> 8%
where the time goes in v6:
time: 135 us; the launch traced here: 134 us
  blocking collectives  73.4 us (54%)
  starting transfers between devices  30.5 us (23%)
  Pallas kernels  20.3 us (15%)
  waiting for transfers between devices  7.67 us (6%)
  local copies, waits for them, and re-layouts  1.67 us (1%)
    all_to_all x1, blocking collectives, on_device(): mine = lax.all_to_all(make_stack(from_z), yx, 0, 0)  22.4 us
    all_to_all x1, blocking collectives, on_device(): plane = lax.all_to_all(make_pair(keep, received), yx, 0, 0)  21 us
    all_to_all x1, blocking collectives, on_device(): column = lax.all_to_all(make_plane(plane, gain_rows), 'z', 0, 0)  15.8 us
    all_to_all x1, starting transfers between devices, on_device(): from_z = lax.all_to_all(piece, 'z', 0, 0)  15.8 us
    all_to_all x1, blocking collectives, on_device(): spread = lax.all_to_all(make_column(column), ('c', 'y', 'x'), 0, 0)  14.2 us
    all_to_all x1, waiting for transfers between devices, on_device(): from_z = lax.all_to_all(piece, 'z', 0, 0)  7.46 us
    ppermute x1, starting transfers between devices, on_device(): other = lax.ppermute(mine, 'c', swap)  5.82 us
    ppermute x1, starting transfers between devices, on_device(): before = lax.ppermute(up, 'z', [(i, i + 1) for i in range(15)])  5.2 us
  transfers between devices with their start and end apart: 5, of which 2 were waited for; matrix products, arithmetic and copies ran while one was open for 0% of the time, Pallas kernels for 8%

profile of v6, /device:TPU:1, one launch (start us, length us, event | category | flops | bytes accessed | tf_op | source)
XLA Modules:
  0.0 134.5 jit_solution(16248993398421551624)
XLA Ops:
  0.6 0.0 copy-start.1
  0.6 0.0 copy-start
  0.7 0.0 copy-start.5
  0.7 0.0 copy-start.4
  0.7 3.0 %norm.1 = (bf16[2,192,768]{2,1,0:T(8,128)(2,1)}, bf16[2,192,768]{2,1,0:T(8,128)(2,1)}) custom-call(bf16[2,256,768]{2,1,0:T(8,128)(2,1)} %tokens.5, f32[768]{0:T(1024)} %gain.3, bf16[2,256,768]{2,1,0:T(8,128)(2,1)} %cot.5), custom_call_target="tpu_custom_call" | custom-call | tf_op jit(solution)/shard_map/norm/pallas_call | solution.py:315
  3.7 5.2 %collective-permute-start = (bf16[2,192,768]{2,1,0:T(8,128)(2,1)}, bf16[2,192,768]{2,1,0:T(8,128)(2,1)}, u32[]{:S(2)}, u32[]{:S(2)}) collective-permute-start(bf16[2,192,768]{2,1,0:T(8,128)(2,1)} %get-tuple-element.35.up), channel_id=1, source_target_pairs={{0,1},{1,2},{2,3},{3,4},{4,5},{5,6},{6,7},{7,8},{8,9},{9,10},{10,1... | collective-permute-start | bytes 1769480 | tf_op jit(solution)/shard_map/ppermute | solution.py:416
  8.9 1.3 collective-permute-start.1
  10.2 0.0 copy-done.1
  10.2 0.0 copy-done.4
  10.2 0.0 copy-start.6
  10.2 0.8 copy-done.6
  11.0 0.8 piece.1
  11.8 15.8 %all-to-all-start = ((bf16[16,8,384]{2,1,0:T(8,128)(2,1)}), bf16[16,8,384]{2,1,0:T(8,128)(2,1)S(1)}, u32[]{:S(2)}, u32[]{:S(2)}) async-start(bf16[16,8,384]{2,1,0:T(8,128)(2,1)} %piece.1), calls=%async_computation | async-start | bytes 196608 | tf_op jit(solution)/shard_map/all_to_all | solution.py:415
  27.6 0.0 copy-done
  27.6 0.0 copy-done.5
  27.6 3.5 %own.1 = (bf16[2,256,768]{2,1,0:T(8,128)(2,1)S(1)}, f32[2,256,768]{2,1,0:T(8,128)S(1)}) custom-call(bf16[2,256,768]{2,1,0:T(8,128)(2,1)} %tokens.5, f32[768]{0:T(1024)S(1)} %copy-done.5, bf16[2,256,768]{2,1,0:T(8,128)(2,1)} %cot.5, bf16[768,768]{1,0:T(8,128)(2,1)S(1)} %copy-done), custom_call_target="tpu_custom_call" | custom-call | tf_op jit(solution)/shard_map/own/pallas_call | solution.py:321
  31.2 0.0 copy-start.2
  31.2 0.9 copy-done.2
  32.0 7.5 %all-to-all-done.given = bf16[16,8,384]{2,1,0:T(8,128)(2,1)S(1)} async-done(((bf16[16,8,384]{2,1,0:T(8,128)(2,1)}), bf16[16,8,384]{2,1,0:T(8,128)(2,1)S(1)}, u32[]{:S(2)}, u32[]{:S(2)}) %all-to-all-start) | async-done | bytes 98336 | tf_op jit(solution)/shard_map/all_to_all | solution.py:415
  39.5 0.0 collective-permute-done.before
  39.5 0.0 collective-permute-done.1.after
  39.5 0.1 stack.1
  39.6 0.0 copy-start.3
  39.7 22.4 %all_to_all.25.mine = bf16[16,96,384]{2,1,0:T(8,128)(2,1)S(1)} all-to-all(bf16[16,96,384]{2,1,0:T(8,128)(2,1)S(1)} %stack.1), channel_id=1, replica_groups=mesh['y'=4,'x'=4,'c'=2,'z'=16] {'y','x'}, dimensions={0} | all-to-all | bytes 2359296 | tf_op jit(solution)/shard_map/all_to_all | solution.py:420
  62.0 5.8 %collective-permute-start.2 = (bf16[16,96,384]{2,1,0:T(8,128)(2,1)S(1)}, bf16[16,96,384]{2,1,0:T(8,128)(2,1)S(1)}, u32[]{:S(2)}, u32[]{:S(2)}) collective-permute-start(bf16[16,96,384]{2,1,0:T(8,128)(2,1)S(1)} %all_to_all.25.mine), channel_id=1, source_target_pairs={{0,16},{16,0},{1,17},{17,1},{2,18},{18,2},{3,19},{19,3},{4,20},{20... | collective-permute-start | bytes 3538952 | tf_op jit(solution)/shard_map/ppermute | solution.py:422
  67.8 0.0 copy-done.3
  67.9 2.2 %ready.1 = (bf16[2,512,768]{2,1,0:T(8,128)(2,1)S(1)}, bf16[2,384,768]{2,1,0:T(8,128)(2,1)S(1)}) custom-call(bf16[2,256,768]{2,1,0:T(8,128)(2,1)S(1)} %copy-done.3, bf16[768,768]{1,0:T(8,128)(2,1)S(1)} %copy-done, bf16[2,192,768]{2,1,0:T(8,128)(2,1)} %get-tuple-element.35.up, bf16[2,192,768]{2,1,0:T(8,128)(2,1)} %get-tuple-element.36.down, ...), custom_call_target="tpu_custom_call" | custom-call | tf_op jit(solution)/shard_map/ready/pallas_call | solution.py:333
  70.1 0.2 collective-permute-done.2.other
  70.3 4.7 %main.1 = (bf16[16,96,384]{2,1,0:T(8,128)(2,1)S(1)}, bf16[16,96,384]{2,1,0:T(8,128)(2,1)S(1)}, bf16[2,384,384]{2,1,0:T(8,128)(2,1)S(1)}, bf16[2,256,384]{2,1,0:T...) custom-call(s32[1]{0:T(128)} %bitcast.core, bf16[16,96,384]{2,1,0:T(8,128)(2,1)S(1)} %all_to_all.25.mine, ...), custom_call_target="tpu_custom_call" | custom-call | tf_op jit(solution)/shard_map/main/pallas_call | solution.py:347
  75.0 2.4 %collective-permute-start.3 = (bf16[16,96,384]{2,1,0:T(8,128)(2,1)S(1)}, bf16[16,96,384]{2,1,0:T(8,128)(2,1)S(1)}, u32[]{:S(2)}, u32[]{:S(2)}) collective-permute-start(bf16[16,96,384]{2,1,0:T(8,128)(2,1)S(1)} %get-tuple-element.48), channel_id=1, source_target_pairs={{0,16},{16,0},{1,17},{17,1},{2,18},{18,2},{3,19},{19,3},{4,20},{20... | collective-permute-start | bytes 3538952 | tf_op jit(solution)/shard_map/ppermute | solution.py:426
  77.4 4.5 %tail.1 = (bf16[2,256,768]{2,1,0:T(8,128)(2,1)}, bf16[2,256,768]{2,1,0:T(8,128)(2,1)}, f32[16,384]{1,0:T(8,128)S(1)}) custom-call(bf16[3,384,768]{2,1,0:T(8,128)(2,1)S(1)} %get-tuple-element.49.taps, bf16[768,384]{1,0:T(8,128)(2,1)S(1)} %get-tuple-element.50.proj, bf16[2,384,384]{2,1,0:T(8,128)(2,1)S(1)} %get-tuple-element.51.sum_cot, ...), custom_call_target="tpu_custom_call" | custom-call | tf_op jit(solution)/shard_map/tail/pallas_call | solution.py:370
  81.9 0.0 collective-permute-done.3.b
  81.9 0.3 pair.1
  82.2 21.0 %all_to_all.26.given = bf16[16,96,384]{2,1,0:T(8,128)(2,1)S(1)} all-to-all(bf16[16,96,384]{2,1,0:T(8,128)(2,1)S(1)} %pair.1), channel_id=1, replica_groups=mesh['y'=4,'x'=4,'c'=2,'z'=16] {'y','x'}, dimensions={0} | all-to-all | bytes 2359296 | tf_op jit(solution)/shard_map/all_to_all | solution.py:433
  103.2 0.2 plane.1
  103.5 15.8 %all_to_all.27.given = bf16[16,8,384]{2,1,0:T(8,128)(2,1)S(1)} all-to-all(bf16[16,8,384]{2,1,0:T(8,128)(2,1)S(1)} %plane.1), channel_id=1, replica_groups=mesh['y'=4,'x'=4,'c'=2,'z'=16] {'z'}, dimensions={0} | all-to-all | bytes 196608 | tf_op jit(solution)/shard_map/all_to_all | solution.py:434
  119.4 14.2 %all_to_all.28.given = bf16[32,8,384]{2,1,0:T(8,128)(2,1)S(1)} all-to-all(bf16[32,8,384]{2,1,0:T(8,128)(2,1)S(1)} %column.1), channel_id=1, replica_groups=mesh['y'=4,'x'=4,'c'=2,'z'=16] {'c','y','x'}, dimensions={0} | all-to-all | bytes 393216 | tf_op jit(solution)/shard_map/all_to_all | solution.py:435
  133.6 0.9 final.1
  (1 shorter events, 0.0 us)
Async XLA Ops:
  0.6 9.6 %copy-start.1 = (bf16[384,384]{1,0:T(8,128)(2,1)S(1)}, bf16[384,384]{1,0:T(8,128)(2,1)}, u32[]{:S(2)}) copy-start(bf16[384,384]{1,0:T(8,128)(2,1)} %constant.24.clone.perm) | copy-start | bytes 884740
  0.6 27.0 %copy-start = (bf16[768,768]{1,0:T(8,128)(2,1)S(1)}, bf16[768,768]{1,0:T(8,128)(2,1)}, u32[]{:S(2)}) copy-start(bf16[768,768]{1,0:T(8,128)(2,1)} %constant.25.clone.perm) | copy-start | bytes 3538948
  0.7 27.0 %copy-start.5 = (f32[768]{0:T(1024)S(1)}, f32[768]{0:T(1024)}, u32[]{:S(2)}) copy-start(f32[768]{0:T(1024)} %gain.3) | copy-start | bytes 9220
  0.7 9.6 %copy-start.4 = (bf16[3,768,24]{1,2,0:T(8,128)(2,1)S(1)}, bf16[3,768,24]{1,2,0:T(8,128)(2,1)}, u32[]{:S(2)}) copy-start(bf16[3,768,24]{1,2,0:T(8,128)(2,1)} %param.9) | copy-start | bytes 331780
  3.7 35.8 %collective-permute-start = (bf16[2,192,768]{2,1,0:T(8,128)(2,1)}, bf16[2,192,768]{2,1,0:T(8,128)(2,1)}, u32[]{:S(2)}, u32[]{:S(2)}) collective-permute-start(bf16[2,192,768]{2,1,0:T(8,128)(2,1)} %get-tuple-element.35.up), channel_id=1, source_target_pairs={{0,1},{1,2},{2,3},{3,4},{4,5},{5,6},{6,7},{7,8},{8,9},{9,10},{10,1... | collective-permute-start | bytes 1769480 | tf_op jit(solution)/shard_map/ppermute | solution.py:416
  8.9 30.6 %collective-permute-start.1 = (bf16[2,192,768]{2,1,0:T(8,128)(2,1)}, bf16[2,192,768]{2,1,0:T(8,128)(2,1)}, u32[]{:S(2)}, u32[]{:S(2)}) collective-permute-start(bf16[2,192,768]{2,1,0:T(8,128)(2,1)} %get-tuple-element.36.down), channel_id=1, source_target_pairs={{1,0},{2,1},{3,2},{4,3},{5,4},{6,5},{7,6},{8,7},{9,8},{10,9},{11,1... | collective-permute-start | bytes 1769480 | tf_op jit(solution)/shard_map/ppermute | solution.py:417
  10.2 0.8 copy-start.6
  11.8 27.7 %all-to-all-start = ((bf16[16,8,384]{2,1,0:T(8,128)(2,1)}), bf16[16,8,384]{2,1,0:T(8,128)(2,1)S(1)}, u32[]{:S(2)}, u32[]{:S(2)}) async-start(bf16[16,8,384]{2,1,0:T(8,128)(2,1)} %piece.1), calls=%async_computation | async-start | bytes 196608 | tf_op jit(solution)/shard_map/all_to_all | solution.py:415
  31.2 0.9 copy-start.2
  39.6 28.2 %copy-start.3 = (bf16[2,256,768]{2,1,0:T(8,128)(2,1)S(1)}, bf16[2,256,768]{2,1,0:T(8,128)(2,1)}, u32[]{:S(2)}) copy-start(bf16[2,256,768]{2,1,0:T(8,128)(2,1)} %copy-done.2) | copy-start | bytes 2359300
  62.0 8.3 %collective-permute-start.2 = (bf16[16,96,384]{2,1,0:T(8,128)(2,1)S(1)}, bf16[16,96,384]{2,1,0:T(8,128)(2,1)S(1)}, u32[]{:S(2)}, u32[]{:S(2)}) collective-permute-start(bf16[16,96,384]{2,1,0:T(8,128)(2,1)S(1)} %all_to_all.25.mine), channel_id=1, source_target_pairs={{0,16},{16,0},{1,17},{17,1},{2,18},{18,2},{3,19},{19,3},{4,20},{20... | collective-permute-start | bytes 3538952 | tf_op jit(solution)/shard_map/ppermute | solution.py:422
  75.0 6.9 %collective-permute-start.3 = (bf16[16,96,384]{2,1,0:T(8,128)(2,1)S(1)}, bf16[16,96,384]{2,1,0:T(8,128)(2,1)S(1)}, u32[]{:S(2)}, u32[]{:S(2)}) collective-permute-start(bf16[16,96,384]{2,1,0:T(8,128)(2,1)S(1)} %get-tuple-element.48), channel_id=1, source_target_pairs={{0,16},{16,0},{1,17},{17,1},{2,18},{18,2},{3,19},{19,3},{4,20},{20... | collective-permute-start | bytes 3538952 | tf_op jit(solution)/shard_map/ppermute | solution.py:426

commit v7 on v5

--- a/solution.py
+++ b/solution.py
@@ -83,33 +83,31 @@
 
 
 def norm_kernel(tokens, gain_in, cot, up, down, rows, gain, sems):
-    loads = [(tokens.at[s], rows.at[s]) for s in range(SEQS)]
+    parts = [(s, pl.ds(r, BINS // 2)) for s in range(SEQS) for r in (0, BINS // 2)]
+    loads = [(gain_in, gain)] + [(tokens.at[s, at], rows.at[s, at]) for s, at in parts]
     loads += [
-        (gain_in, gain),
         (cot.at[:, BINS - STEP :], up.at[:, 2 * STEP :]),
         (cot.at[:, 0:STEP], down.at[:, 2 * STEP :]),
     ]
     loads = run(loads, sems)
-    loads[SEQS].wait()
+    loads[0].wait()
     gain_row = gain[...].reshape(1, CHANNELS)
     for s in range(SEQS):
-        loads[s].wait()
         for r in range(0, BINS, TILE):
+            if r % (BINS // 2) == 0:
+                loads[1 + 2 * s + r // (BINS // 2)].wait()
             v = rows[s, r : r + TILE].astype(f32)
             normed = v * inverse_rms_of(v) * gain_row
             edge, at = (down, r) if r < 2 * STEP else (up, r - 2 * STEP)
             edge[s, at : at + TILE] = activate(normed, tanh_of(normed)).astype(bf16)
-    for c in loads[SEQS + 1 :]:
+    for c in loads[1 + 2 * SEQS :]:
         c.wait()
 
 
 def ready_kernel(
-    tokens, gain, cot, perm, up, down, before, after,
+    rows, gain, cots, perm, up, down, before, after,
     act, cot_perm, slope,
-    rows, cots, sems,
 ):
-    loads = [(cot.at[s], cots.at[s]) for s in range(SEQS)] + [(tokens.at[s], rows.at[s]) for s in range(SEQS)]
-    loads = run(loads, sems)
     half = 2 * STEP
     act[:, 0:half] = before[:, 0:half]
     act[:, half : 2 * half] = down[:, 0:half]
@@ -122,9 +120,7 @@
         cot_perm[s, 0:STEP] = edges[0:STEP]
         cot_perm[s, STEP + BINS :] = edges[STEP:]
     for s in range(SEQS):
-        loads[s].wait()
         cot_perm[s, STEP : STEP + BINS] = dot(cots[s], order, 1, 0).astype(bf16)
-        loads[SEQS + s].wait()
         for r in range(0, BINS, TILE):
             v = rows[s, r : r + TILE].astype(f32)
             normed = v * inverse_rms_of(v) * gain_row
@@ -189,12 +185,10 @@
 
 
 def tail_kernel(
-    taps, proj, sum_cot, hidden, slope, tokens, gain, cot, perm,
+    taps, proj, sum_cot, hidden, slope, rows, gain, cots, perm,
     block_output, token_gradient, gain_rows,
-    rows, cots, result, sems, out_sems,
+    result, out_sems,
 ):
-    loads = [(tokens.at[s], rows.at[s]) for s in range(SEQS)] + [(cot.at[s], cots.at[s]) for s in range(SEQS)]
-    loads = run(loads, sems)
     natural = dot(perm[...], proj[...], 1, 0).astype(bf16)
     gain_row = gain[...].reshape(1, CHANNELS)
     gain_sum = jnp.zeros((1, CHANNELS), f32)
@@ -204,8 +198,6 @@
         total += dot(sum_cot[s, STEP : STEP + BINS], taps[1], 1, 0)
         total += dot(sum_cot[s, 0:BINS], taps[2], 1, 0)
         projected = dot(hidden[s], natural, 1, 1)
-        loads[s].wait()
-        loads[SEQS + s].wait()
         for r in range(0, BINS, TILE):
             at = slice(r, r + TILE)
             v = rows[s, at].astype(f32)
@@ -310,7 +302,7 @@
 
 def make_norm(tokens, gain, cot):
     edge = shape((SEQS, 3 * STEP, CHANNELS), bf16)
-    return call(norm_kernel, [edge, edge], [FAR] * 3, [VMEM] * 2, "norm", 6, [LOCAL, pltpu.VMEM((CHANNELS,), f32), waits(5)])(
+    return call(norm_kernel, [edge, edge], [FAR] * 3, [VMEM] * 2, "norm", 6, [LOCAL, pltpu.VMEM((CHANNELS,), f32), waits(7)])(
         tokens, gain, cot
     )
 
@@ -323,11 +315,10 @@
             shape((SEQS, EXT, CHANNELS), bf16),
             shape((SEQS, BINS, CHANNELS), f32),
         ],
-        [FAR, VMEM, FAR] + [VMEM] * 5,
+        [VMEM] * 8,
         [VMEM] * 3,
         "ready",
-        10,
-        [LOCAL, LOCAL, waits(4)],
+        8,
     )(tokens, gain, cot, perm, up, down, before, after)
 
 
@@ -358,11 +349,11 @@
     return call(
         tail_kernel,
         [ROWS, ROWS, shape((16, 384), f32)],
-        [VMEM] * 5 + [FAR, VMEM, FAR, VMEM],
+        [VMEM] * 9,
         [FAR, FAR, VMEM],
         "tail",
         12,
-        [LOCAL, LOCAL, pltpu.VMEM((2, SEQS, BINS, CHANNELS), bf16), waits(4), waits(4)],
+        [pltpu.VMEM((2, SEQS, BINS, CHANNELS), bf16), waits(4)],
     )(taps, proj, sum_cot, hidden, slope, tokens, gain, cot, perm)
 
 
@@ -396,9 +387,8 @@
     lane_perm = jnp.asarray(permutation(4, 16, 6), bf16)
     row_perm = jnp.asarray(permutation(8, 16, 6), bf16)
 
-    tokens = pltpu.with_memory_space_constraint(tokens, pltpu.HBM)
-    cotangent = pltpu.with_memory_space_constraint(cotangent, pltpu.HBM)
-    up, down = make_norm(tokens, pltpu.with_memory_space_constraint(norm_gain, pltpu.HBM), cotangent)
+    far = [pltpu.with_memory_space_constraint(a, pltpu.HBM) for a in (tokens, norm_gain, cotangent)]
+    up, down = make_norm(*far)
     before = lax.ppermute(up, "z", [(i, i + 1) for i in range(15)])
     after = lax.ppermute(down, "z", [(i + 1, i) for i in range(15)])
 

time: 134 us -> 133 us (level)
  Pallas kernels: 16.4 us -> 14.6 us
    pallas_call x1, Pallas kernels: 3.55 us -> 2.18 us  [make_ready(): call(ready_kernel, [shape((SEQS, BINS + 4 * STEP, CHANNELS), bf16), shape...]
  transfers between devices with their start and end apart: 4 -> 4, of which waited for: 0 -> 1; matrix products, arithmetic and copies ran while one was open for 0% -> 0% of each run, Pallas kernels for 6% -> 5%
where the time goes in v7:
time: 133 us; the launch traced here: 132 us
  blocking collectives  103 us (77%)
  Pallas kernels  14.6 us (11%)
  starting transfers between devices  13.8 us (10%)
    all_to_all x1, blocking collectives, on_device(): from_z = lax.all_to_all(piece, 'z', 0, 0)  28.2 us
    all_to_all x1, blocking collectives, on_device(): mine = lax.all_to_all(make_stack(from_z), yx, 0, 0)  22.4 us
    all_to_all x1, blocking collectives, on_device(): plane = lax.all_to_all(make_pair(keep, received), yx, 0, 0)  21 us
    all_to_all x1, blocking collectives, on_device(): column = lax.all_to_all(make_plane(plane, gain_rows), 'z', 0, 0)  17.2 us
    all_to_all x1, blocking collectives, on_device(): spread = lax.all_to_all(make_column(column), ('c', 'y', 'x'), 0, 0)  14.2 us
    ppermute x1, starting transfers between devices, on_device(): other = lax.ppermute(mine, 'c', swap)  5.82 us
    pallas_call x1, Pallas kernels, make_main(): call(main_kernel, [HALF, HALF, shape((SEQS, EXT, HIDDEN), bf16), shape((S...  4.68 us
    ppermute x1, starting transfers between devices, on_device(): before = lax.ppermute(up, 'z', [(i, i + 1) for i in range(15)])  4.41 us
  transfers between devices with their start and end apart: 4, of which 1 were waited for; matrix products, arithmetic and copies ran while one was open for 0% of the time, Pallas kernels for 5%

profile of v7, /device:TPU:1, one launch (start us, length us, event | category | flops | bytes accessed | tf_op | source)
XLA Modules:
  0.0 132.5 jit_solution(12409170473412046759)
XLA Ops:
  0.6 0.0 copy-start.3
  0.6 0.0 copy-start.6
  0.7 0.0 copy-start.4
  0.7 2.1 %norm.1 = (bf16[2,192,768]{2,1,0:T(8,128)(2,1)S(1)}, bf16[2,192,768]{2,1,0:T(8,128)(2,1)S(1)}) custom-call(bf16[2,256,768]{2,1,0:T(8,128)(2,1)} %rows.3, f32[768]{0:T(1024)} %gain.3, bf16[2,256,768]{2,1,0:T(8,128)(2,1)} %cots.3), custom_call_target="tpu_custom_call" | custom-call | tf_op jit(solution)/shard_map/norm/pallas_call | solution.py:305
  2.8 4.4 %collective-permute-start = (bf16[2,192,768]{2,1,0:T(8,128)(2,1)S(1)}, bf16[2,192,768]{2,1,0:T(8,128)(2,1)S(1)}, u32[]{:S(2)}, u32[]{:S(2)}) collective-permute-start(bf16[2,192,768]{2,1,0:T(8,128)(2,1)S(1)} %get-tuple-element.32.up), channel_id=1, source_target_pairs={{0,1},{1,2},{2,3},{3,4},{4,5},{5,6},{6,7},{7,8},{8,9},{9,10},{10,1... | collective-permute-start | bytes 1769480 | tf_op jit(solution)/shard_map/ppermute | solution.py:392
  7.2 1.3 collective-permute-start.1
  8.5 0.0 copy-done.3
  8.5 0.0 copy-done.6
  8.5 0.0 copy-done.4
  8.5 0.2 piece.1
  8.7 28.2 %all_to_all.25.given = bf16[16,8,384]{2,1,0:T(8,128)(2,1)S(1)} all-to-all(bf16[16,8,384]{2,1,0:T(8,128)(2,1)S(1)} %piece.1), channel_id=1, replica_groups=mesh['y'=4,'x'=4,'c'=2,'z'=16] {'z'}, dimensions={0} | all-to-all | bytes 196608 | tf_op jit(solution)/shard_map/all_to_all | solution.py:396
  36.9 0.0 collective-permute-done.before
  36.9 0.0 collective-permute-done.1.after
  37.0 0.0 copy-start.2
  37.0 0.1 stack.1
  37.1 0.0 copy-start
  37.1 0.0 copy-start.1
  37.1 0.0 copy-start.5
  37.1 22.4 %all_to_all.26.mine = bf16[16,96,384]{2,1,0:T(8,128)(2,1)S(1)} all-to-all(bf16[16,96,384]{2,1,0:T(8,128)(2,1)S(1)} %stack.1), channel_id=1, replica_groups=mesh['y'=4,'x'=4,'c'=2,'z'=16] {'y','x'}, dimensions={0} | all-to-all | bytes 2359296 | tf_op jit(solution)/shard_map/all_to_all | solution.py:398
  59.5 5.8 %collective-permute-start.2 = (bf16[16,96,384]{2,1,0:T(8,128)(2,1)S(1)}, bf16[16,96,384]{2,1,0:T(8,128)(2,1)S(1)}, u32[]{:S(2)}, u32[]{:S(2)}) collective-permute-start(bf16[16,96,384]{2,1,0:T(8,128)(2,1)S(1)} %all_to_all.26.mine), channel_id=1, source_target_pairs={{0,16},{16,0},{1,17},{17,1},{2,18},{18,2},{3,19},{19,3},{4,20},{20... | collective-permute-start | bytes 3538952 | tf_op jit(solution)/shard_map/ppermute | solution.py:400
  65.3 0.0 copy-done.2
  65.3 0.0 copy-done
  65.3 0.0 copy-done.1
  65.3 0.0 copy-done.5
  65.4 2.2 %ready.1 = (bf16[2,512,768]{2,1,0:T(8,128)(2,1)S(1)}, bf16[2,384,768]{2,1,0:T(8,128)(2,1)S(1)}, f32[2,256,768]{2,1,0:T(8,128)S(1)}) custom-call(bf16[2,256,768]{2,1,0:T(8,128)(2,1)S(1)} %copy-done, f32[768]{0:T(1024)S(1)} %copy-done.5, bf16[2,256,768]{2,1,0:T(8,128)(2,1)S(1)} %copy-done.1, bf16[768,768]{1,0:T(8,128)(2,1)S(1)} %copy-done.2, ...), custom_call_target="tpu_custom_call" | custom-call | tf_op jit(solution)/shard_map/ready/pallas_call | solution.py:311
  67.5 0.2 collective-permute-done.2.other
  67.8 4.7 %main.1 = (bf16[16,96,384]{2,1,0:T(8,128)(2,1)S(1)}, bf16[16,96,384]{2,1,0:T(8,128)(2,1)S(1)}, bf16[2,384,384]{2,1,0:T(8,128)(2,1)S(1)}, bf16[2,256,384]{2,1,0:T...) custom-call(s32[1]{0:T(128)} %bitcast.core, bf16[16,96,384]{2,1,0:T(8,128)(2,1)S(1)} %all_to_all.26.mine, ...), custom_call_target="tpu_custom_call" | custom-call | tf_op jit(solution)/shard_map/main/pallas_call | solution.py:326
  72.5 2.3 %collective-permute-start.3 = (bf16[16,96,384]{2,1,0:T(8,128)(2,1)S(1)}, bf16[16,96,384]{2,1,0:T(8,128)(2,1)S(1)}, u32[]{:S(2)}, u32[]{:S(2)}) collective-permute-start(bf16[16,96,384]{2,1,0:T(8,128)(2,1)S(1)} %get-tuple-element.42), channel_id=1, source_target_pairs={{0,16},{16,0},{1,17},{17,1},{2,18},{18,2},{3,19},{19,3},{4,20},{20... | collective-permute-start | bytes 3538952 | tf_op jit(solution)/shard_map/ppermute | solution.py:404
  74.7 3.9 %tail.1 = (bf16[2,256,768]{2,1,0:T(8,128)(2,1)}, bf16[2,256,768]{2,1,0:T(8,128)(2,1)}, f32[16,384]{1,0:T(8,128)S(1)}) custom-call(bf16[3,384,768]{2,1,0:T(8,128)(2,1)S(1)} %get-tuple-element.43.taps, bf16[768,384]{1,0:T(8,128)(2,1)S(1)} %get-tuple-element.44.proj, bf16[2,384,384]{2,1,0:T(8,128)(2,1)S(1)} %get-tuple-element.45.sum_cot, ...), custom_call_target="tpu_custom_call" | custom-call | tf_op jit(solution)/shard_map/tail/pallas_call | solution.py:349
  78.6 0.0 collective-permute-done.3.b
  78.6 0.3 pair.1
  78.9 21.0 %all_to_all.27.given = bf16[16,96,384]{2,1,0:T(8,128)(2,1)S(1)} all-to-all(bf16[16,96,384]{2,1,0:T(8,128)(2,1)S(1)} %pair.1), channel_id=1, replica_groups=mesh['y'=4,'x'=4,'c'=2,'z'=16] {'y','x'}, dimensions={0} | all-to-all | bytes 2359296 | tf_op jit(solution)/shard_map/all_to_all | solution.py:411
  99.9 0.2 plane.1
  100.2 17.2 %all_to_all.28.given = bf16[16,8,384]{2,1,0:T(8,128)(2,1)S(1)} all-to-all(bf16[16,8,384]{2,1,0:T(8,128)(2,1)S(1)} %plane.1), channel_id=1, replica_groups=mesh['y'=4,'x'=4,'c'=2,'z'=16] {'z'}, dimensions={0} | all-to-all | bytes 196608 | tf_op jit(solution)/shard_map/all_to_all | solution.py:412
  117.4 14.2 %all_to_all.29.given = bf16[32,8,384]{2,1,0:T(8,128)(2,1)S(1)} all-to-all(bf16[32,8,384]{2,1,0:T(8,128)(2,1)S(1)} %column.1), channel_id=1, replica_groups=mesh['y'=4,'x'=4,'c'=2,'z'=16] {'c','y','x'}, dimensions={0} | all-to-all | bytes 393216 | tf_op jit(solution)/shard_map/all_to_all | solution.py:413
  131.6 0.9 final.1
  (1 shorter events, 0.0 us)
Async XLA Ops:
  0.6 7.9 %copy-start.3 = (bf16[384,384]{1,0:T(8,128)(2,1)S(1)}, bf16[384,384]{1,0:T(8,128)(2,1)}, u32[]{:S(2)}) copy-start(bf16[384,384]{1,0:T(8,128)(2,1)} %constant.24.clone.perm) | copy-start | bytes 884740
  0.6 7.8 %copy-start.6 = (bf16[384,48]{0,1:T(8,128)(2,1)S(1)}, bf16[384,48]{0,1:T(8,128)(2,1)}, u32[]{:S(2)}) copy-start(bf16[384,48]{0,1:T(8,128)(2,1)} %param.10) | copy-start | bytes 110596
  0.7 7.8 %copy-start.4 = (bf16[3,768,24]{1,2,0:T(8,128)(2,1)S(1)}, bf16[3,768,24]{1,2,0:T(8,128)(2,1)}, u32[]{:S(2)}) copy-start(bf16[3,768,24]{1,2,0:T(8,128)(2,1)} %param.9) | copy-start | bytes 331780
  2.8 34.2 %collective-permute-start = (bf16[2,192,768]{2,1,0:T(8,128)(2,1)S(1)}, bf16[2,192,768]{2,1,0:T(8,128)(2,1)S(1)}, u32[]{:S(2)}, u32[]{:S(2)}) collective-permute-start(bf16[2,192,768]{2,1,0:T(8,128)(2,1)S(1)} %get-tuple-element.32.up), channel_id=1, source_target_pairs={{0,1},{1,2},{2,3},{3,4},{4,5},{5,6},{6,7},{7,8},{8,9},{9,10},{10,1... | collective-permute-start | bytes 1769480 | tf_op jit(solution)/shard_map/ppermute | solution.py:392
  7.2 29.8 %collective-permute-start.1 = (bf16[2,192,768]{2,1,0:T(8,128)(2,1)S(1)}, bf16[2,192,768]{2,1,0:T(8,128)(2,1)S(1)}, u32[]{:S(2)}, u32[]{:S(2)}) collective-permute-start(bf16[2,192,768]{2,1,0:T(8,128)(2,1)S(1)} %get-tuple-element.33.down), channel_id=1, source_target_pairs={{1,0},{2,1},{3,2},{4,3},{5,4},{6,5},{7,6},{8,7},{9,8},{10,9},{11,1... | collective-permute-start | bytes 1769480 | tf_op jit(solution)/shard_map/ppermute | solution.py:393
  37.0 28.4 %copy-start.2 = (bf16[768,768]{1,0:T(8,128)(2,1)S(1)}, bf16[768,768]{1,0:T(8,128)(2,1)}, u32[]{:S(2)}) copy-start(bf16[768,768]{1,0:T(8,128)(2,1)} %constant.25.clone.perm) | copy-start | bytes 3538948
  37.1 28.2 %copy-start = (bf16[2,256,768]{2,1,0:T(8,128)(2,1)S(1)}, bf16[2,256,768]{2,1,0:T(8,128)(2,1)}, u32[]{:S(2)}) copy-start(bf16[2,256,768]{2,1,0:T(8,128)(2,1)} %rows.3) | copy-start | bytes 2359300
  37.1 28.2 %copy-start.1 = (bf16[2,256,768]{2,1,0:T(8,128)(2,1)S(1)}, bf16[2,256,768]{2,1,0:T(8,128)(2,1)}, u32[]{:S(2)}) copy-start(bf16[2,256,768]{2,1,0:T(8,128)(2,1)} %cots.3) | copy-start | bytes 2359300
  37.1 28.2 %copy-start.5 = (f32[768]{0:T(1024)S(1)}, f32[768]{0:T(1024)}, u32[]{:S(2)}) copy-start(f32[768]{0:T(1024)} %gain.3) | copy-start | bytes 9220
  59.5 8.3 %collective-permute-start.2 = (bf16[16,96,384]{2,1,0:T(8,128)(2,1)S(1)}, bf16[16,96,384]{2,1,0:T(8,128)(2,1)S(1)}, u32[]{:S(2)}, u32[]{:S(2)}) collective-permute-start(bf16[16,96,384]{2,1,0:T(8,128)(2,1)S(1)} %all_to_all.26.mine), channel_id=1, source_target_pairs={{0,16},{16,0},{1,17},{17,1},{2,18},{18,2},{3,19},{19,3},{4,20},{20... | collective-permute-start | bytes 3538952 | tf_op jit(solution)/shard_map/ppermute | solution.py:400
  72.5 6.2 %collective-permute-start.3 = (bf16[16,96,384]{2,1,0:T(8,128)(2,1)S(1)}, bf16[16,96,384]{2,1,0:T(8,128)(2,1)S(1)}, u32[]{:S(2)}, u32[]{:S(2)}) collective-permute-start(bf16[16,96,384]{2,1,0:T(8,128)(2,1)S(1)} %get-tuple-element.42), channel_id=1, source_target_pairs={{0,16},{16,0},{1,17},{17,1},{2,18},{18,2},{3,19},{19,3},{4,20},{20... | collective-permute-start | bytes 3538952 | tf_op jit(solution)/shard_map/ppermute | solution.py:404

commit v8 on v7

--- a/solution.py
+++ b/solution.py
@@ -83,8 +83,7 @@
 
 
 def norm_kernel(tokens, gain_in, cot, up, down, rows, gain, sems):
-    parts = [(s, pl.ds(r, BINS // 2)) for s in range(SEQS) for r in (0, BINS // 2)]
-    loads = [(gain_in, gain)] + [(tokens.at[s, at], rows.at[s, at]) for s, at in parts]
+    loads = [(gain_in, gain)] + [(tokens.at[s], rows.at[s]) for s in range(SEQS)]
     loads += [
         (cot.at[:, BINS - STEP :], up.at[:, 2 * STEP :]),
         (cot.at[:, 0:STEP], down.at[:, 2 * STEP :]),
@@ -93,14 +92,13 @@
     loads[0].wait()
     gain_row = gain[...].reshape(1, CHANNELS)
     for s in range(SEQS):
+        loads[1 + s].wait()
         for r in range(0, BINS, TILE):
-            if r % (BINS // 2) == 0:
-                loads[1 + 2 * s + r // (BINS // 2)].wait()
             v = rows[s, r : r + TILE].astype(f32)
             normed = v * inverse_rms_of(v) * gain_row
             edge, at = (down, r) if r < 2 * STEP else (up, r - 2 * STEP)
             edge[s, at : at + TILE] = activate(normed, tanh_of(normed)).astype(bf16)
-    for c in loads[1 + 2 * SEQS :]:
+    for c in loads[1 + SEQS :]:
         c.wait()
 
 
@@ -189,7 +187,6 @@
     block_output, token_gradient, gain_rows,
     result, out_sems,
 ):
-    natural = dot(perm[...], proj[...], 1, 0).astype(bf16)
     gain_row = gain[...].reshape(1, CHANNELS)
     gain_sum = jnp.zeros((1, CHANNELS), f32)
     saves = []
@@ -197,11 +194,9 @@
         total = dot(sum_cot[s, 2 * STEP : 2 * STEP + BINS], taps[0], 1, 0)
         total += dot(sum_cot[s, STEP : STEP + BINS], taps[1], 1, 0)
         total += dot(sum_cot[s, 0:BINS], taps[2], 1, 0)
-        projected = dot(hidden[s], natural, 1, 1)
         for r in range(0, BINS, TILE):
             at = slice(r, r + TILE)
             v = rows[s, at].astype(f32)
-            result[0, s, at] = (v + projected[at]).astype(bf16)
             normed_cot = total[at].astype(bf16).astype(f32) * slope[s, at]
             inverse_rms = inverse_rms_of(v)
             scaled_cot = gain_row * normed_cot
@@ -210,11 +205,12 @@
                 cots[s, at].astype(f32) + inverse_rms * scaled_cot - v * (inverse_rms * inverse_rms * inverse_rms) * mean
             ).astype(bf16)
             gain_sum += jnp.sum(normed_cot * v * inverse_rms, axis=0, keepdims=True)
-        saves += [
-            pltpu.make_async_copy(result.at[0, s], block_output.at[s], out_sems.at[2 * s]),
-            pltpu.make_async_copy(result.at[1, s], token_gradient.at[s], out_sems.at[2 * s + 1]),
-        ]
-        saves[-2].start()
+        saves.append(pltpu.make_async_copy(result.at[1, s], token_gradient.at[s], out_sems.at[2 * s + 1]))
+        saves[-1].start()
+    natural = dot(proj[...], perm[...], 0, 1).astype(bf16)
+    for s in range(SEQS):
+        result[0, s] = (rows[s].astype(f32) + dot(hidden[s], natural, 1, 0)).astype(bf16)
+        saves.append(pltpu.make_async_copy(result.at[0, s], block_output.at[s], out_sems.at[2 * s]))
         saves[-1].start()
     gain_rows[...] = jnp.zeros((16, 384), f32)
     for z in range(16):
@@ -302,7 +298,7 @@
 
 def make_norm(tokens, gain, cot):
     edge = shape((SEQS, 3 * STEP, CHANNELS), bf16)
-    return call(norm_kernel, [edge, edge], [FAR] * 3, [VMEM] * 2, "norm", 6, [LOCAL, pltpu.VMEM((CHANNELS,), f32), waits(7)])(
+    return call(norm_kernel, [edge, edge], [FAR] * 3, [VMEM] * 2, "norm", 6, [LOCAL, pltpu.VMEM((CHANNELS,), f32), waits(5)])(
         tokens, gain, cot
     )
 

time: 133 us -> 132 us (level)
  transfers between devices with their start and end apart: 4 -> 4, of which waited for: 1 -> 1; matrix products, arithmetic and copies ran while one was open for 0% -> 0% of each run, Pallas kernels for 5% -> 4%
where the time goes in v8:
time: 132 us
  blocking collectives  103 us (78%)
  Pallas kernels  14.1 us (11%)
  starting transfers between devices  13.8 us (10%)
    all_to_all x1, blocking collectives, on_device(): from_z = lax.all_to_all(piece, 'z', 0, 0)  28.2 us
    all_to_all x1, blocking collectives, on_device(): mine = lax.all_to_all(make_stack(from_z), yx, 0, 0)  22.4 us
    all_to_all x1, blocking collectives, on_device(): plane = lax.all_to_all(make_pair(keep, received), yx, 0, 0)  21 us
    all_to_all x1, blocking collectives, on_device(): column = lax.all_to_all(make_plane(plane, gain_rows), 'z', 0, 0)  17.2 us
    all_to_all x1, blocking collectives, on_device(): spread = lax.all_to_all(make_column(column), ('c', 'y', 'x'), 0, 0)  14.2 us
    ppermute x1, starting transfers between devices, on_device(): other = lax.ppermute(mine, 'c', swap)  5.82 us
    pallas_call x1, Pallas kernels, make_main(): call(main_kernel, [HALF, HALF, shape((SEQS, EXT, HIDDEN), bf16), shape((S...  4.68 us
    ppermute x1, starting transfers between devices, on_device(): before = lax.ppermute(up, 'z', [(i, i + 1) for i in range(15)])  4.41 us
  transfers between devices with their start and end apart: 4, of which 1 were waited for; matrix products, arithmetic and copies ran while one was open for 0% of the time, Pallas kernels for 4%

profile of v8, /device:TPU:1, one launch (start us, length us, event | category | flops | bytes accessed | tf_op | source)
XLA Modules:
  0.0 132.0 jit_solution(16369834487878162824)
XLA Ops:
  0.6 0.0 copy-start.3
  0.6 0.0 copy-start.6
  0.7 0.0 copy-start.4
  0.7 1.9 %norm.1 = (bf16[2,192,768]{2,1,0:T(8,128)(2,1)S(1)}, bf16[2,192,768]{2,1,0:T(8,128)(2,1)S(1)}) custom-call(bf16[2,256,768]{2,1,0:T(8,128)(2,1)} %rows.3, f32[768]{0:T(1024)} %gain.3, bf16[2,256,768]{2,1,0:T(8,128)(2,1)} %cots.3), custom_call_target="tpu_custom_call" | custom-call | tf_op jit(solution)/shard_map/norm/pallas_call | solution.py:301
  2.6 4.4 %collective-permute-start = (bf16[2,192,768]{2,1,0:T(8,128)(2,1)S(1)}, bf16[2,192,768]{2,1,0:T(8,128)(2,1)S(1)}, u32[]{:S(2)}, u32[]{:S(2)}) collective-permute-start(bf16[2,192,768]{2,1,0:T(8,128)(2,1)S(1)} %get-tuple-element.32.up), channel_id=1, source_target_pairs={{0,1},{1,2},{2,3},{3,4},{4,5},{5,6},{6,7},{7,8},{8,9},{9,10},{10,1... | collective-permute-start | bytes 1769480 | tf_op jit(solution)/shard_map/ppermute | solution.py:388
  7.0 1.3 collective-permute-start.1
  8.3 0.0 copy-done.3
  8.3 0.0 copy-done.6
  8.4 0.0 copy-done.4
  8.4 0.2 piece.1
  8.6 28.2 %all_to_all.25.given = bf16[16,8,384]{2,1,0:T(8,128)(2,1)S(1)} all-to-all(bf16[16,8,384]{2,1,0:T(8,128)(2,1)S(1)} %piece.1), channel_id=1, replica_groups=mesh['y'=4,'x'=4,'c'=2,'z'=16] {'z'}, dimensions={0} | all-to-all | bytes 196608 | tf_op jit(solution)/shard_map/all_to_all | solution.py:392
  36.8 0.0 collective-permute-done.before
  36.8 0.0 collective-permute-done.1.after
  36.8 0.0 copy-start.2
  36.8 0.1 stack.1
  36.9 0.0 copy-start
  37.0 0.0 copy-start.1
  37.0 0.0 copy-start.5
  37.0 22.4 %all_to_all.26.mine = bf16[16,96,384]{2,1,0:T(8,128)(2,1)S(1)} all-to-all(bf16[16,96,384]{2,1,0:T(8,128)(2,1)S(1)} %stack.1), channel_id=1, replica_groups=mesh['y'=4,'x'=4,'c'=2,'z'=16] {'y','x'}, dimensions={0} | all-to-all | bytes 2359296 | tf_op jit(solution)/shard_map/all_to_all | solution.py:394
  59.3 5.8 %collective-permute-start.2 = (bf16[16,96,384]{2,1,0:T(8,128)(2,1)S(1)}, bf16[16,96,384]{2,1,0:T(8,128)(2,1)S(1)}, u32[]{:S(2)}, u32[]{:S(2)}) collective-permute-start(bf16[16,96,384]{2,1,0:T(8,128)(2,1)S(1)} %all_to_all.26.mine), channel_id=1, source_target_pairs={{0,16},{16,0},{1,17},{17,1},{2,18},{18,2},{3,19},{19,3},{4,20},{20... | collective-permute-start | bytes 3538952 | tf_op jit(solution)/shard_map/ppermute | solution.py:396
  65.2 0.0 copy-done.2
  65.2 0.0 copy-done
  65.2 0.0 copy-done.1
  65.2 0.0 copy-done.5
  65.2 2.2 %ready.1 = (bf16[2,512,768]{2,1,0:T(8,128)(2,1)S(1)}, bf16[2,384,768]{2,1,0:T(8,128)(2,1)S(1)}, f32[2,256,768]{2,1,0:T(8,128)S(1)}) custom-call(bf16[2,256,768]{2,1,0:T(8,128)(2,1)S(1)} %copy-done, f32[768]{0:T(1024)S(1)} %copy-done.5, bf16[2,256,768]{2,1,0:T(8,128)(2,1)S(1)} %copy-done.1, bf16[768,768]{1,0:T(8,128)(2,1)S(1)} %copy-done.2, ...), custom_call_target="tpu_custom_call" | custom-call | tf_op jit(solution)/shard_map/ready/pallas_call | solution.py:307
  67.4 0.2 collective-permute-done.2.other
  67.6 4.7 %main.1 = (bf16[16,96,384]{2,1,0:T(8,128)(2,1)S(1)}, bf16[16,96,384]{2,1,0:T(8,128)(2,1)S(1)}, bf16[2,384,384]{2,1,0:T(8,128)(2,1)S(1)}, bf16[2,256,384]{2,1,0:T...) custom-call(s32[1]{0:T(128)} %bitcast.core, bf16[16,96,384]{2,1,0:T(8,128)(2,1)S(1)} %all_to_all.26.mine, ...), custom_call_target="tpu_custom_call" | custom-call | tf_op jit(solution)/shard_map/main/pallas_call | solution.py:322
  72.3 2.3 %collective-permute-start.3 = (bf16[16,96,384]{2,1,0:T(8,128)(2,1)S(1)}, bf16[16,96,384]{2,1,0:T(8,128)(2,1)S(1)}, u32[]{:S(2)}, u32[]{:S(2)}) collective-permute-start(bf16[16,96,384]{2,1,0:T(8,128)(2,1)S(1)} %get-tuple-element.42), channel_id=1, source_target_pairs={{0,16},{16,0},{1,17},{17,1},{2,18},{18,2},{3,19},{19,3},{4,20},{20... | collective-permute-start | bytes 3538952 | tf_op jit(solution)/shard_map/ppermute | solution.py:400
  74.6 3.5 %tail.1 = (bf16[2,256,768]{2,1,0:T(8,128)(2,1)}, bf16[2,256,768]{2,1,0:T(8,128)(2,1)}, f32[16,384]{1,0:T(8,128)S(1)}) custom-call(bf16[3,384,768]{2,1,0:T(8,128)(2,1)S(1)} %get-tuple-element.43.taps, bf16[768,384]{1,0:T(8,128)(2,1)S(1)} %get-tuple-element.44.proj, bf16[2,384,384]{2,1,0:T(8,128)(2,1)S(1)} %get-tuple-element.45.sum_cot, ...), custom_call_target="tpu_custom_call" | custom-call | tf_op jit(solution)/shard_map/tail/pallas_call | solution.py:345
  78.1 0.0 collective-permute-done.3.b
  78.1 0.3 pair.1
  78.4 21.0 %all_to_all.27.given = bf16[16,96,384]{2,1,0:T(8,128)(2,1)S(1)} all-to-all(bf16[16,96,384]{2,1,0:T(8,128)(2,1)S(1)} %pair.1), channel_id=1, replica_groups=mesh['y'=4,'x'=4,'c'=2,'z'=16] {'y','x'}, dimensions={0} | all-to-all | bytes 2359296 | tf_op jit(solution)/shard_map/all_to_all | solution.py:407
  99.4 0.2 plane.1
  99.7 17.2 %all_to_all.28.given = bf16[16,8,384]{2,1,0:T(8,128)(2,1)S(1)} all-to-all(bf16[16,8,384]{2,1,0:T(8,128)(2,1)S(1)} %plane.1), channel_id=1, replica_groups=mesh['y'=4,'x'=4,'c'=2,'z'=16] {'z'}, dimensions={0} | all-to-all | bytes 196608 | tf_op jit(solution)/shard_map/all_to_all | solution.py:408
  116.9 14.2 %all_to_all.29.given = bf16[32,8,384]{2,1,0:T(8,128)(2,1)S(1)} all-to-all(bf16[32,8,384]{2,1,0:T(8,128)(2,1)S(1)} %column.1), channel_id=1, replica_groups=mesh['y'=4,'x'=4,'c'=2,'z'=16] {'c','y','x'}, dimensions={0} | all-to-all | bytes 393216 | tf_op jit(solution)/shard_map/all_to_all | solution.py:409
  131.1 0.9 final.1
  (1 shorter events, 0.0 us)
Async XLA Ops:
  0.6 7.7 %copy-start.3 = (bf16[384,384]{1,0:T(8,128)(2,1)S(1)}, bf16[384,384]{1,0:T(8,128)(2,1)}, u32[]{:S(2)}) copy-start(bf16[384,384]{1,0:T(8,128)(2,1)} %constant.24.clone.perm) | copy-start | bytes 884740
  0.6 7.7 %copy-start.6 = (bf16[384,48]{0,1:T(8,128)(2,1)S(1)}, bf16[384,48]{0,1:T(8,128)(2,1)}, u32[]{:S(2)}) copy-start(bf16[384,48]{0,1:T(8,128)(2,1)} %param.10) | copy-start | bytes 110596
  0.7 7.7 %copy-start.4 = (bf16[3,768,24]{1,2,0:T(8,128)(2,1)S(1)}, bf16[3,768,24]{1,2,0:T(8,128)(2,1)}, u32[]{:S(2)}) copy-start(bf16[3,768,24]{1,2,0:T(8,128)(2,1)} %param.9) | copy-start | bytes 331780
  2.6 34.2 %collective-permute-start = (bf16[2,192,768]{2,1,0:T(8,128)(2,1)S(1)}, bf16[2,192,768]{2,1,0:T(8,128)(2,1)S(1)}, u32[]{:S(2)}, u32[]{:S(2)}) collective-permute-start(bf16[2,192,768]{2,1,0:T(8,128)(2,1)S(1)} %get-tuple-element.32.up), channel_id=1, source_target_pairs={{0,1},{1,2},{2,3},{3,4},{4,5},{5,6},{6,7},{7,8},{8,9},{9,10},{10,1... | collective-permute-start | bytes 1769480 | tf_op jit(solution)/shard_map/ppermute | solution.py:388
  7.0 29.8 %collective-permute-start.1 = (bf16[2,192,768]{2,1,0:T(8,128)(2,1)S(1)}, bf16[2,192,768]{2,1,0:T(8,128)(2,1)S(1)}, u32[]{:S(2)}, u32[]{:S(2)}) collective-permute-start(bf16[2,192,768]{2,1,0:T(8,128)(2,1)S(1)} %get-tuple-element.33.down), channel_id=1, source_target_pairs={{1,0},{2,1},{3,2},{4,3},{5,4},{6,5},{7,6},{8,7},{9,8},{10,9},{11,1... | collective-permute-start | bytes 1769480 | tf_op jit(solution)/shard_map/ppermute | solution.py:389
  36.8 28.4 %copy-start.2 = (bf16[768,768]{1,0:T(8,128)(2,1)S(1)}, bf16[768,768]{1,0:T(8,128)(2,1)}, u32[]{:S(2)}) copy-start(bf16[768,768]{1,0:T(8,128)(2,1)} %constant.25.clone.perm) | copy-start | bytes 3538948
  36.9 28.2 %copy-start = (bf16[2,256,768]{2,1,0:T(8,128)(2,1)S(1)}, bf16[2,256,768]{2,1,0:T(8,128)(2,1)}, u32[]{:S(2)}) copy-start(bf16[2,256,768]{2,1,0:T(8,128)(2,1)} %rows.3) | copy-start | bytes 2359300
  37.0 28.2 %copy-start.1 = (bf16[2,256,768]{2,1,0:T(8,128)(2,1)S(1)}, bf16[2,256,768]{2,1,0:T(8,128)(2,1)}, u32[]{:S(2)}) copy-start(bf16[2,256,768]{2,1,0:T(8,128)(2,1)} %cots.3) | copy-start | bytes 2359300
  37.0 28.2 %copy-start.5 = (f32[768]{0:T(1024)S(1)}, f32[768]{0:T(1024)}, u32[]{:S(2)}) copy-start(f32[768]{0:T(1024)} %gain.3) | copy-start | bytes 9220
  59.3 8.3 %collective-permute-start.2 = (bf16[16,96,384]{2,1,0:T(8,128)(2,1)S(1)}, bf16[16,96,384]{2,1,0:T(8,128)(2,1)S(1)}, u32[]{:S(2)}, u32[]{:S(2)}) collective-permute-start(bf16[16,96,384]{2,1,0:T(8,128)(2,1)S(1)} %all_to_all.26.mine), channel_id=1, source_target_pairs={{0,16},{16,0},{1,17},{17,1},{2,18},{18,2},{3,19},{19,3},{4,20},{20... | collective-permute-start | bytes 3538952 | tf_op jit(solution)/shard_map/ppermute | solution.py:396
  72.3 5.8 %collective-permute-start.3 = (bf16[16,96,384]{2,1,0:T(8,128)(2,1)S(1)}, bf16[16,96,384]{2,1,0:T(8,128)(2,1)S(1)}, u32[]{:S(2)}, u32[]{:S(2)}) collective-permute-start(bf16[16,96,384]{2,1,0:T(8,128)(2,1)S(1)} %get-tuple-element.42), channel_id=1, source_target_pairs={{0,16},{16,0},{1,17},{17,1},{2,18},{18,2},{3,19},{19,3},{4,20},{20... | collective-permute-start | bytes 3538952 | tf_op jit(solution)/shard_map/ppermute | solution.py:400
